TPU v7x, 256 devices: a whole 4x4x8 slice. The times are simulated.
256 devices in a mesh: comp: 2 (over x_lo), panel: 4 (over x_hi, core), col: 32 (over z, y).
Axes of the slice: x: 4 (x_hi: 2, x_lo: 2; x = x_hi * 2 + x_lo), y: 4, z: 8, core: 2. Of those that a mesh axis runs over, the one named last changes fastest.
Arguments:
- joint_tracer_field: float32 [2, 2, 4, 2048, 1024], P('comp', None, None, 'col', 'panel'), may hold values from -5 to 5
- courant_mixing_rates: float32 [2, 3, 4, 2048, 1024], P('comp', None, None, 'col', 'panel'), may hold values from -0.24 to 0.24, as said below
- oceanic_indicator: int32 [2, 2048, 1024], P('comp', 'col', 'panel'), may hold values 0 or 1
- glacial_indicator: int32 [2048, 1024], P('col', 'panel'), may hold values 0 or 1
- prior_oceanic_warmth: float32 [2048, 1024], P('col', 'panel'), may hold values from -4 to 4
- prior_glacial_cover: float32 [2048, 1024], P('col', 'panel'), may hold values from 0 to 0.8
- partner_devices: int32 [16384, 2], P(('panel', 'col')), may hold values from 0 to 127, all different within a row; in each aligned block of 128 rows (0 to 127, 128 to 255, ...) at most 4 rows name the same one
- receiving_tile_index: int32 [16384, 2], P(('panel', 'col')), may hold values from 0 to 127
- bank_tile_entry: int32 [16384, 2], P(('panel', 'col')), may hold values from 0 to 31
- conservative_overlay_factors: float32 [32, 128, 128], replicated, may hold values from 0.002 to 0.014
Outputs:
- new_state: float32 [2, 2, 4, 2048, 1024], P('comp', None, None, 'col', 'panel')
- surface: float32 [2, 2, 2048, 1024], P('comp', None, 'col', 'panel')
Inputs may be any that keep to these rules, and one draw needn't show every extreme that they name: `partner_devices`: each row names two different ocean devices, device p * 32 + q lying at index p of panel and q of col. Among the 128 rows of one device no ocean device is named more than 4 times, and in the rows of some devices one is named exactly 4 times. courant_mixing_rates[c, 0] and courant_mixing_rates[c, 1] lie in [-0.24, 0.24]; courant_mixing_rates[c, 2] lies in [0.01, 0.24].
All inputs are finite; a program needn't handle non-finite values. No bound on the sum of `oceanic_indicator` or of `glacial_indicator` on one device may be relied on, other than what follows from the above.
Results may differ from a plain program's by a relative error of at most 0.00013.
Values sent between devices are 32-bit elements; how exact they have to be, the bound alone decides.
A program may use at most 64 MiB of HBM per device.

v0:
```python
import jax
import jax.numpy as jnp
from jax import lax
from jax.sharding import PartitionSpec as P

TILE = 128
NSUB = 4
HIGHEST = lax.Precision.HIGHEST


def passed_along(value, axis, steps):
    count = lax.axis_size(axis)
    initial, last = (max(0, -steps), min(count, count - steps))
    return lax.ppermute(value, axis, [(source, source + steps) for source in range(initial, last)])


def from_behind(array, axis, by):
    count = lax.axis_size(axis)
    return lax.ppermute(array, axis, [(i, (i + by) % count) for i in range(count)])


def wide_halo(array, width):
    west = from_behind(array[..., -width:], "panel", 1)
    east = from_behind(array[..., :width], "panel", -1)
    array = jnp.concatenate([west, array, east], axis=-1)
    south = passed_along(array[..., -width:, :], "col", 1)
    north = passed_along(array[..., :width, :], "col", -1)
    return jnp.concatenate([south, array, north], axis=-2)


def vertical_mix(tracer, mixing):
    level_flux = mixing[:-1] * (tracer[:, 1:] - tracer[:, :-1])
    zero_level = jnp.zeros_like(tracer[:, :1])
    from_above = jnp.concatenate([level_flux, zero_level], axis=1)
    from_below = jnp.concatenate([zero_level, level_flux], axis=1)
    relaxation = jnp.concatenate(
        [jnp.zeros_like(tracer[:, :-1]), mixing[-1:] * tracer[:, -1:]], axis=1
    )
    return tracer + from_above - from_below - relaxation


def advect_mix(tracer, east_vel, north_vel, mixing):
    centre = tracer[..., 1:-1, 1:-1]
    vel_east = east_vel[:, 1:-1, 1:-1]
    vel_west = east_vel[:, 1:-1, :-2]
    vel_north = north_vel[:, 1:-1, 1:-1]
    vel_south = north_vel[:, :-2, 1:-1]
    flux_east = (
        jnp.maximum(vel_east, 0.0) * centre + jnp.minimum(vel_east, 0.0) * tracer[..., 1:-1, 2:]
    )
    flux_west = (
        jnp.maximum(vel_west, 0.0) * tracer[..., 1:-1, :-2] + jnp.minimum(vel_west, 0.0) * centre
    )
    flux_north = (
        jnp.maximum(vel_north, 0.0) * centre + jnp.minimum(vel_north, 0.0) * tracer[..., 2:, 1:-1]
    )
    flux_south = (
        jnp.maximum(vel_south, 0.0) * tracer[..., :-2, 1:-1] + jnp.minimum(vel_south, 0.0) * centre
    )
    advanced = centre - (flux_east - flux_west) - (flux_north - flux_south)
    return vertical_mix(advanced, mixing[:, 1:-1, 1:-1])


def to_tiles(field_grid):
    fcount, grid_rows, grid_cols = field_grid.shape
    blocks = field_grid.reshape(fcount, grid_rows, grid_cols // TILE, TILE)
    return blocks.transpose(1, 2, 0, 3).reshape(-1, fcount, TILE)


def from_tiles(tile_form, grid_rows, grid_cols):
    fcount = tile_form.shape[1]
    blocks = tile_form.reshape(grid_rows, grid_cols // TILE, fcount, TILE)
    return blocks.transpose(2, 0, 1, 3).reshape(fcount, grid_rows, grid_cols)


def bucket_places(partner_devices, owners, capacity):
    owner_list = partner_devices.reshape(-1)
    owner_hit = (owner_list[:, None] == jnp.arange(owners, dtype=jnp.int32)[None, :]).astype(
        jnp.int32
    )
    owner_rank = jnp.cumsum(owner_hit, axis=0) - owner_hit
    position = jnp.sum(owner_rank * owner_hit, axis=1)
    return owner_list * capacity + position


def advect(start, coeffs, grid_rows):
    fields = start.shape[0] * start.shape[1]
    both = jnp.concatenate([start.reshape((fields,) + start.shape[2:]), coeffs.reshape((-1,) + coeffs.shape[2:])])
    wide = wide_halo(both, NSUB)
    levels = coeffs.shape[1]
    tracer = wide[:fields].reshape(start.shape[:2] + wide.shape[1:])
    coeff_ext = wide[fields:].reshape((3, levels) + wide.shape[1:])
    rows_total = grid_rows * lax.axis_size("col")
    row_global = (
        lax.axis_index("col") * grid_rows
        + jnp.arange(grid_rows + 2 * NSUB, dtype=jnp.int32)
        - NSUB
    )
    row_open = ((row_global >= 0) & (row_global < rows_total - 1)).astype(jnp.float32)
    east_ext = coeff_ext[0]
    north_ext = coeff_ext[1] * row_open[None, :, None]
    mix_ext = coeff_ext[2]
    for step_index in range(NSUB):
        s = step_index
        e = east_ext.shape[1] - s
        w = east_ext.shape[2] - s
        tracer = advect_mix(
            tracer,
            east_ext[:, s:e, s:w],
            north_ext[:, s:e, s:w],
            mix_ext[:, s:e, s:w],
        )
    return tracer


def on_device(
    joint_tracer_field,
    courant_mixing_rates,
    oceanic_indicator,
    glacial_indicator,
    prior_oceanic_warmth,
    prior_glacial_cover,
    partner_devices,
    receiving_tile_index,
    bank_tile_entry,
    conservative_overlay_factors,
):
    owners = lax.axis_size("panel") * lax.axis_size("col")
    tile_count = partner_devices.shape[0]
    capacity = max(2, 4 * tile_count // owners)
    slots = owners * capacity
    nbank = conservative_overlay_factors.shape[0]
    on_atmos = lax.axis_index("comp") == 0
    device_tracer_share = joint_tracer_field[0]
    coeffs = courant_mixing_rates[0]
    grid_rows = coeffs.shape[2]
    grid_cols = coeffs.shape[3]
    sea_here = oceanic_indicator[0].astype(jnp.float32)
    wind_east = coeffs[0, 0]
    wind_north = coeffs[1, 0]
    airflow_speed = jnp.sqrt(wind_east * wind_east + wind_north * wind_north + 0.01)
    unfrozen_share = sea_here * (1.0 - prior_glacial_cover)
    thermal_exchange_rate = (
        2.0 * airflow_speed * (prior_oceanic_warmth - device_tracer_share[0, 0]) * unfrozen_share
    )
    evaporation_rate = (
        2.0
        * airflow_speed
        * (jnp.exp(0.1 * prior_oceanic_warmth) - device_tracer_share[1, 0])
        * unfrozen_share
    )
    heated = device_tracer_share.at[0, 0].add(thermal_exchange_rate).at[1, 0].add(evaporation_rate)
    start = jnp.where(on_atmos, heated, device_tracer_share)
    surface_flux = jnp.stack([thermal_exchange_rate, evaporation_rate])
    flux_tiles = passed_along(to_tiles(surface_flux), "comp", 1)

    flux_rows = flux_tiles.reshape(tile_count * 2, TILE)
    by_bank = jnp.einsum(
        "bji,ri->brj", conservative_overlay_factors, flux_rows, precision=HIGHEST
    ).reshape(nbank * tile_count, 2 * TILE)
    tile_ids = jnp.arange(tile_count, dtype=jnp.int32)[:, None]
    pair_rows = bank_tile_entry * tile_count + tile_ids
    contrib = by_bank[pair_rows.reshape(-1)]

    bucket_place = bucket_places(partner_devices, owners, capacity)
    slot_list = receiving_tile_index.reshape(-1)
    place_match = bucket_place[None, :] == jnp.arange(slots, dtype=jnp.int32)[:, None]
    place_hit = place_match.astype(jnp.float32)
    buffer = jnp.dot(place_hit, contrib, precision=HIGHEST).reshape(owners, capacity, 2, TILE)
    labels = jnp.sum(jnp.where(place_match, slot_list[None, :], 0), axis=1).reshape(
        owners, capacity
    )
    received = lax.all_to_all(buffer, ("panel", "col"), 0, 0, tiled=True)
    recv_slots = lax.all_to_all(labels, ("panel", "col"), 0, 0, tiled=True)
    slot_hit = (
        recv_slots.reshape(-1)[None, :] == jnp.arange(tile_count, dtype=jnp.int32)[:, None]
    ).astype(jnp.float32)
    summed = jnp.dot(slot_hit, received.reshape(slots, 2 * TILE), precision=HIGHEST)
    forcing = from_tiles(summed.reshape(tile_count, 2, TILE), grid_rows, grid_cols)

    tracer = advect(start, coeffs, grid_rows)
    forced = (
        tracer.at[0, 0]
        .add(-(0.5 * sea_here * forcing[0]))
        .at[1, 0]
        .add(0.5 * sea_here * forcing[1])
    )
    new_here = jnp.where(on_atmos, tracer, forced)
    sea_temp = new_here[0, 0]
    ice_cover = (
        glacial_indicator.astype(jnp.float32) * sea_here * jnp.clip(0.5 - sea_temp, 0.0, 1.0)
    )
    ocean_surface = jnp.stack([sea_temp, ice_cover])
    ocean_tiles = to_tiles(ocean_surface).reshape(tile_count, 2 * TILE)
    reply = jnp.einsum("ts,tc->sc", slot_hit, ocean_tiles, precision=HIGHEST)
    returned = lax.all_to_all(
        reply.reshape(owners, capacity, 2 * TILE), ("panel", "col"), 0, 0, tiled=True
    ).reshape(slots, 2 * TILE)
    values = jnp.einsum("sp,sc->pc", place_hit, returned, precision=HIGHEST)

    by_bank_back = jnp.einsum(
        "rj,bji->bri",
        values.reshape(tile_count * 4, TILE),
        conservative_overlay_factors,
        precision=HIGHEST,
    ).reshape(nbank * tile_count, 4 * TILE)
    first = by_bank_back[pair_rows[:, 0]][:, : 2 * TILE]
    second = by_bank_back[pair_rows[:, 1]][:, 2 * TILE :]
    column_sums = jnp.sum(conservative_overlay_factors, axis=1)
    denominator = column_sums[bank_tile_entry[:, 0]] + column_sums[bank_tile_entry[:, 1]]
    remap_back = (first + second).reshape(tile_count, 2, TILE) / denominator[:, None, :]
    remapped = passed_along(from_tiles(remap_back, grid_rows, grid_cols), "comp", -1)
    surface_here = jnp.where(on_atmos, remapped, ocean_surface)
    return (new_here[None], surface_here[None])


def solution(mesh):
    return jax.shard_map(
        on_device,
        mesh=mesh,
        in_specs=(
            P("comp", None, None, "col", "panel"),
            P("comp", None, None, "col", "panel"),
            P("comp", "col", "panel"),
            P("col", "panel"),
            P("col", "panel"),
            P("col", "panel"),
            P(("panel", "col"), None),
            P(("panel", "col"), None),
            P(("panel", "col"), None),
            P(),
        ),
        out_specs=(P("comp", None, None, "col", "panel"), P("comp", None, "col", "panel")),
        check_vma=False,
    )
```

profile of v0, /device:TPU:1, one launch (start us, length us, event | category | flops | bytes accessed | tf_op | source)
XLA Modules:
  0.0 204.0 jit_solution(16313261195618302890)
XLA Ops:
  8.2 2.0 copy.81
  10.2 4.1 %collective-permute-start = (f32[20,64,4]{1,2,0:T(4,128)}, f32[20,64,4]{1,2,0:T(4,128)}, u32[]{:S(2)}, u32[]{:S(2)}) collective-permute-start(f32[20,64,4]{1,2,0:T(4,128)} %copy.81), channel_id=1, source_target_pairs={{0,32},{32,64},{64,96},{96,0},{1,33},{33,65},{65,97},{97,1},{2,34}... | collective-permute-start | bytes 61448 | tf_op jit(solution)/shard_map/ppermute | solution.py:19
  14.3 1.9 copy.82
  18.6 2.7 %collective-permute-start.4 = (f32[128,2,128]{2,1,0:T(2,128)}, f32[128,2,128]{2,1,0:T(2,128)}, u32[]{:S(2)}, u32[]{:S(2)}) collective-permute-start(f32[128,2,128]{2,1,0:T(2,128)} %bitcast.26), channel_id=1, source_target_pairs={{0,128},{1,129},{2,130},{3,131},{4,132},{5,133},{6,134},{7,135},{8... | collective-permute-start | bytes 393224 | tf_op jit(solution)/shard_map/ppermute | solution.py:14
  25.6 16.5 %all-to-all-start = ((s32[128,1,4]{2,1,0:T(1,128)}), s32[128,1,4]{2,1,0:T(1,128)S(1)}, u32[]{:S(2)}, u32[]{:S(2)}) async-start(s32[128,1,4]{2,1,0:T(1,128)} %bitcast.22), calls=%async_computation | async-start | bytes 131072 | tf_op jit(solution)/shard_map/all_to_all | solution.py:174
  47.2 7.1 %all-to-all-done = s32[128,1,4]{2,1,0:T(1,128)S(1)} async-done(((s32[128,1,4]{2,1,0:T(1,128)}), s32[128,1,4]{2,1,0:T(1,128)S(1)}, u32[]{:S(2)}, u32[]{:S(2)}) %all-to-all-start) | async-done | bytes 2080 | tf_op jit(solution)/shard_map/all_to_all | solution.py:174
  54.9 1.4 reduce.11
  57.3 1.9 copy.83
  59.2 1.9 copy.84
  61.2 1.3 pad_maximum_fusion.7
  62.5 2.1 %collective-permute-start.2 = (f32[20,4,264]{2,1,0:T(4,128)S(1)}, f32[20,4,264]{2,1,0:T(4,128)S(1)}, u32[]{:S(2)}, u32[]{:S(2)}) collective-permute-start(f32[20,4,264]{2,1,0:T(4,128)S(1)} %get-tuple-element.56), channel_id=1, source_target_pairs={{0,1},{1,2},{2,3},{3,4},{4,5},{5,6},{6,7},{7,8},{8,9},{9,10},{10,1... | collective-permute-start | bytes 253448 | tf_op jit(solution)/shard_map/ppermute | solution.py:14
  64.7 1.5 collective-permute-start.3
  67.1 3.8 %collective-permute-done.3 = f32[20,4,264]{2,1,0:T(4,128)S(1)} collective-permute-done((f32[20,4,264]{2,1,0:T(4,128)S(1)}, f32[20,4,264]{2,1,0:T(4,128)S(1)}, u32[]{:S(2)}, u32[]{:S(2)}) %collective-permute-start.3) | collective-permute-done | bytes 84512 | tf_op jit(solution)/shard_map/ppermute | solution.py:14
  81.1 1.3 slice_maximum_fusion.13
  82.4 6.2 %convolution_bitcast_fusion.1 = f32[32,256,128]{2,1,0:T(8,128)} fusion(f32[256,128,1]{1,0,2:T(8,128)} %bitcast.28, f32[32,128,128]{2,1,0:T(8,128)S(1)} %copy-done), kind=kOutput, calls=%fused_computation.7 | convolution fusion | flops 1610612736 | bytes 6422528 | tf_op jit(solution)/shard_map/bji,ri->brj/dot_general | solution.py:158
  88.5 5.2 %reshape.439 = f32[4096,256]{1,0:T(8,128)} reshape(f32[32,256,128]{2,1,0:T(8,128)} %convolution_bitcast_fusion.1) | data formatting | bytes 8388608 | tf_op jit(solution)/shard_map/reshape | solution.py:160
  93.7 4.0 %gather_fusion = f32[256,256]{1,0:T(8,128)} fusion(f32[4096,256]{1,0:T(8,128)} %reshape.439, s32[1024]{0:T(1024)} %pad_clamp_fusion.4), kind=kCustom, calls=%fused_computation | custom fusion | bytes 525312 | tf_op jit(solution)/shard_map/gather | solution.py:163
  97.7 2.2 %fusion.37 = f32[512,256]{1,0:T(8,128)} fusion(f32[256,256]{1,0:T(8,128)} %gather_fusion, s32[256]{0:T(256)S(1)} %multiply_add_fusion.1), kind=kOutput, calls=%fused_computation.74 | convolution fusion | flops 402784256 | bytes 787456 | tf_op jit(solution)/shard_map/dot_general | solution.py:169
  99.9 2.1 %reshape.441 = f32[128,4,2,128]{3,2,1,0:T(2,128)} reshape(f32[512,256]{1,0:T(8,128)} %fusion.37) | data formatting | bytes 1048576 | tf_op jit(solution)/shard_map/reshape | solution.py:169
  102.0 11.3 %all-to-all-start.1 = ((f32[128,4,2,128]{3,2,1,0:T(2,128)}), f32[128,4,2,128]{3,2,1,0:T(2,128)}, u32[]{:S(2)}, u32[]{:S(2)}) async-start(f32[128,4,2,128]{3,2,1,0:T(2,128)} %reshape.441), calls=%async_computation.1 | async-start | bytes 1048576 | tf_op jit(solution)/shard_map/all_to_all | solution.py:173
  113.4 2.2 %fusion.30 = f32[2,4,64,256]{3,2,1,0:T(8,128)S(1)} fusion(f32[2,4,66,258]{3,2,1,0:T(8,128)S(1)} %pad_subtract_fusion, f32[4,64,256]{2,1,0:T(8,128)} %get-tuple-element.78, f32[4,64,256]{2,1,0:T(8,128)} %get-tuple-element.79, f32[4,64,256]{2,1,0:T(8,128)} %get-tuple-element.77, f32[4,64,256]{2,1,0:T(8,128)} %get-tuple-element.76, ...), kind=kLoop, calls=%fused_computation.62 | loop fusion | flops 2097152 | bytes 5242880 | tf_op jit(solution)/shard_map/sub | solution.py:60
  117.2 15.8 %all-to-all-done.1 = f32[128,4,2,128]{3,2,1,0:T(2,128)} async-done(((f32[128,4,2,128]{3,2,1,0:T(2,128)}), f32[128,4,2,128]{3,2,1,0:T(2,128)}, u32[]{:S(2)}, u32[]{:S(2)}) %all-to-all-start.1) | async-done | bytes 524320 | tf_op jit(solution)/shard_map/all_to_all | solution.py:173
  133.1 1.9 copy.109
  134.9 2.1 %copy.94 = f32[512,256]{0,1:T(8,128)} copy(f32[512,256]{1,0:T(8,128)} %bitcast.174) | data formatting | bytes 1048576 | tf_op jit(solution)/shard_map/reshape | solution.py:178
  137.0 1.5 convolution_bitcast_fusion.2
  142.4 6.6 %all-to-all-start.2 = ((f32[128,4,256]{2,1,0:T(4,128)}), f32[128,4,256]{2,1,0:T(4,128)S(1)}, u32[]{:S(2)}, u32[]{:S(2)}) async-start(f32[128,4,256]{2,1,0:T(4,128)} %copy.102), calls=%async_computation.2 | async-start | bytes 1048576 | tf_op jit(solution)/shard_map/all_to_all | solution.py:196
  150.6 18.5 %all-to-all-done.2 = f32[128,4,256]{2,1,0:T(4,128)S(1)} async-done(((f32[128,4,256]{2,1,0:T(4,128)}), f32[128,4,256]{2,1,0:T(4,128)S(1)}, u32[]{:S(2)}, u32[]{:S(2)}) %all-to-all-start.2) | async-done | bytes 524320 | tf_op jit(solution)/shard_map/all_to_all | solution.py:196
  169.9 8.9 %convolution_bitcast_fusion = f32[32,512,128]{2,1,0:T(8,128)} fusion(f32[512,128,1]{1,0,2:T(8,128)S(1)} %reshape.494, f32[32,128,128]{2,1,0:T(8,128)S(1)} %copy-done), kind=kOutput, calls=%fused_computation.5 | convolution fusion | flops 3221225472 | bytes 10747904 | tf_op jit(solution)/shard_map/rj,bji->bri/dot_general | solution.py:201
  178.8 9.3 %reshape.445 = f32[4096,512]{1,0:T(8,128)} reshape(f32[32,512,128]{2,1,0:T(8,128)} %convolution_bitcast_fusion) | data formatting | bytes 16777216 | tf_op jit(solution)/shard_map/reshape | solution.py:206
  188.2 4.3 %gather_fusion.1 = f32[128,512]{1,0:T(8,128)S(1)} fusion(f32[4096,512]{1,0:T(8,128)} %reshape.445, s32[1024]{0:T(1024)S(1)} %pad_clamp_fusion.3), kind=kCustom, calls=%fused_computation.1 | custom fusion | bytes 524800 | tf_op jit(solution)/shard_map/gather | solution.py:207
  192.4 4.3 %gather_fusion.2 = f32[128,512]{1,0:T(8,128)S(1)} fusion(f32[4096,512]{1,0:T(8,128)} %reshape.445, s32[1024]{0:T(1024)S(1)} %pad_clamp_fusion.2), kind=kCustom, calls=%fused_computation.2 | custom fusion | bytes 524800 | tf_op jit(solution)/shard_map/gather | solution.py:208
  198.4 5.0 %collective-permute-done.5 = f32[2,64,256]{2,1,0:T(8,128)S(1)} collective-permute-done((f32[2,64,256]{2,1,0:T(8,128)S(1)}, f32[2,64,256]{2,1,0:T(8,128)S(1)}, u32[]{:S(2)}, u32[]{:S(2)}) %collective-permute-start.5) | collective-permute-done | bytes 131104 | tf_op jit(solution)/shard_map/ppermute | solution.py:14
  (153 shorter events, 41.7 us)
Async XLA Ops:
  0.6 81.8 %copy-start = (f32[32,128,128]{2,1,0:T(8,128)S(1)}, f32[32,128,128]{2,1,0:T(8,128)}, u32[]{:S(2)}) copy-start(f32[32,128,128]{2,1,0:T(8,128)} %param.27) | copy-start | bytes 6291460
  0.6 6.3 %copy-start.1 = (f32[1,3,4,64,256]{4,3,2,1,0:T(8,128)S(1)}, f32[1,3,4,64,256]{4,3,2,1,0:T(8,128)}, u32[]{:S(2)}) copy-start(f32[1,3,4,64,256]{4,3,2,1,0:T(8,128)} %param.19) | copy-start | bytes 2359300
  4.8 0.8 copy-start.6
  6.9 14.4 %copy-start.20 = (s32[128,2]{0,1:T(2,128)S(1)}, s32[128,2]{0,1:T(2,128)}, u32[]{:S(2)}) copy-start(s32[128,2]{0,1:T(2,128)} %param.24) | copy-start | bytes 3076
  8.2 35.4 %copy-start.18 = (s32[128,2]{0,1:T(2,128)S(1)}, s32[128,2]{0,1:T(2,128)}, u32[]{:S(2)}) copy-start(s32[128,2]{0,1:T(2,128)} %param.26) | copy-start | bytes 3076
  10.2 47.1 %collective-permute-start = (f32[20,64,4]{1,2,0:T(4,128)}, f32[20,64,4]{1,2,0:T(4,128)}, u32[]{:S(2)}, u32[]{:S(2)}) collective-permute-start(f32[20,64,4]{1,2,0:T(4,128)} %copy.81), channel_id=1, source_target_pairs={{0,32},{32,64},{64,96},{96,0},{1,33},{33,65},{65,97},{97,1},{2,34}... | collective-permute-start | bytes 61448 | tf_op jit(solution)/shard_map/ppermute | solution.py:19
  16.2 43.0 %collective-permute-start.1 = (f32[20,64,4]{1,2,0:T(4,128)}, f32[20,64,4]{1,2,0:T(4,128)}, u32[]{:S(2)}, u32[]{:S(2)}) collective-permute-start(f32[20,64,4]{1,2,0:T(4,128)} %copy.82), channel_id=1, source_target_pairs={{0,96},{32,0},{64,32},{96,64},{1,97},{33,1},{65,33},{97,65},{2,98}... | collective-permute-start | bytes 61448 | tf_op jit(solution)/shard_map/ppermute | solution.py:19
  18.6 63.8 %collective-permute-start.4 = (f32[128,2,128]{2,1,0:T(2,128)}, f32[128,2,128]{2,1,0:T(2,128)}, u32[]{:S(2)}, u32[]{:S(2)}) collective-permute-start(f32[128,2,128]{2,1,0:T(2,128)} %bitcast.26), channel_id=1, source_target_pairs={{0,128},{1,129},{2,130},{3,131},{4,132},{5,133},{6,134},{7,135},{8... | collective-permute-start | bytes 393224 | tf_op jit(solution)/shard_map/ppermute | solution.py:14
  25.6 28.7 %all-to-all-start = ((s32[128,1,4]{2,1,0:T(1,128)}), s32[128,1,4]{2,1,0:T(1,128)S(1)}, u32[]{:S(2)}, u32[]{:S(2)}) async-start(s32[128,1,4]{2,1,0:T(1,128)} %bitcast.22), calls=%async_computation | async-start | bytes 131072 | tf_op jit(solution)/shard_map/all_to_all | solution.py:174
  61.1 5.0 %copy-start.2 = (f32[20,64,4]{2,1,0:T(8,128)S(1)}, f32[20,64,4]{2,1,0:T(8,128)}, u32[]{:S(2)}) copy-start(f32[20,64,4]{2,1,0:T(8,128)} %copy.83) | copy-start | bytes 61444
  61.2 9.8 %copy-start.3 = (f32[20,64,4]{2,1,0:T(8,128)S(1)}, f32[20,64,4]{2,1,0:T(8,128)}, u32[]{:S(2)}) copy-start(f32[20,64,4]{2,1,0:T(8,128)} %copy.84) | copy-start | bytes 61444
  62.5 4.6 %collective-permute-start.2 = (f32[20,4,264]{2,1,0:T(4,128)S(1)}, f32[20,4,264]{2,1,0:T(4,128)S(1)}, u32[]{:S(2)}, u32[]{:S(2)}) collective-permute-start(f32[20,4,264]{2,1,0:T(4,128)S(1)} %get-tuple-element.56), channel_id=1, source_target_pairs={{0,1},{1,2},{2,3},{3,4},{4,5},{5,6},{6,7},{7,8},{8,9},{9,10},{10,1... | collective-permute-start | bytes 253448 | tf_op jit(solution)/shard_map/ppermute | solution.py:14
  64.7 6.3 %collective-permute-start.3 = (f32[20,4,264]{2,1,0:T(4,128)S(1)}, f32[20,4,264]{2,1,0:T(4,128)S(1)}, u32[]{:S(2)}, u32[]{:S(2)}) collective-permute-start(f32[20,4,264]{2,1,0:T(4,128)S(1)} %get-tuple-element.57), channel_id=1, source_target_pairs={{1,0},{2,1},{3,2},{4,3},{5,4},{6,5},{7,6},{8,7},{9,8},{10,9},{11,1... | collective-permute-start | bytes 253448 | tf_op jit(solution)/shard_map/ppermute | solution.py:14
  67.0 4.8 %copy-start.22 = (f32[72]{0:T(128)S(1)}, f32[72]{0:T(128)}, u32[]{:S(2)}) copy-start(f32[72]{0:T(128)} %and_convert_fusion) | copy-start | bytes 868
  93.7 19.6 %copy-start.7 = (f32[4,64,256]{2,1,0:T(8,128)S(1)}, f32[4,64,256]{2,1,0:T(8,128)}, u32[]{:S(2)}) copy-start(f32[4,64,256]{2,1,0:T(8,128)} %get-tuple-element.72) | copy-start | bytes 786436
  102.0 31.1 %all-to-all-start.1 = ((f32[128,4,2,128]{3,2,1,0:T(2,128)}), f32[128,4,2,128]{3,2,1,0:T(2,128)}, u32[]{:S(2)}, u32[]{:S(2)}) async-start(f32[128,4,2,128]{3,2,1,0:T(2,128)} %reshape.441), calls=%async_computation.1 | async-start | bytes 1048576 | tf_op jit(solution)/shard_map/all_to_all | solution.py:173
  113.3 2.3 %copy-start.17 = (f32[3,64,256]{2,1,0:T(8,128)S(1)}, f32[3,64,256]{2,1,0:T(8,128)}, u32[]{:S(2)}) copy-start(f32[3,64,256]{2,1,0:T(8,128)} %slice.566) | copy-start | bytes 589828
  113.4 2.3 %copy-start.8 = (f32[4,64,256]{2,1,0:T(8,128)S(1)}, f32[4,64,256]{2,1,0:T(8,128)}, u32[]{:S(2)}) copy-start(f32[4,64,256]{2,1,0:T(8,128)} %get-tuple-element.73) | copy-start | bytes 786436
  113.4 2.3 %copy-start.9 = (f32[4,64,256]{2,1,0:T(8,128)S(1)}, f32[4,64,256]{2,1,0:T(8,128)}, u32[]{:S(2)}) copy-start(f32[4,64,256]{2,1,0:T(8,128)} %get-tuple-element.52) | copy-start | bytes 786436
  113.4 2.3 %copy-start.10 = (f32[4,64,256]{2,1,0:T(8,128)S(1)}, f32[4,64,256]{2,1,0:T(8,128)}, u32[]{:S(2)}) copy-start(f32[4,64,256]{2,1,0:T(8,128)} %get-tuple-element.76) | copy-start | bytes 786436
  113.4 2.3 %copy-start.11 = (f32[4,64,256]{2,1,0:T(8,128)S(1)}, f32[4,64,256]{2,1,0:T(8,128)}, u32[]{:S(2)}) copy-start(f32[4,64,256]{2,1,0:T(8,128)} %get-tuple-element.77) | copy-start | bytes 786436
  113.4 2.3 %copy-start.12 = (f32[4,64,256]{2,1,0:T(8,128)S(1)}, f32[4,64,256]{2,1,0:T(8,128)}, u32[]{:S(2)}) copy-start(f32[4,64,256]{2,1,0:T(8,128)} %get-tuple-element.78) | copy-start | bytes 786436
  113.4 2.3 %copy-start.13 = (f32[4,64,256]{2,1,0:T(8,128)S(1)}, f32[4,64,256]{2,1,0:T(8,128)}, u32[]{:S(2)}) copy-start(f32[4,64,256]{2,1,0:T(8,128)} %get-tuple-element.79) | copy-start | bytes 786436
  113.4 2.3 %copy-start.14 = (f32[4,64,256]{2,1,0:T(8,128)S(1)}, f32[4,64,256]{2,1,0:T(8,128)}, u32[]{:S(2)}) copy-start(f32[4,64,256]{2,1,0:T(8,128)} %get-tuple-element.112) | copy-start | bytes 786436
  116.4 0.8 copy-start.4
  117.2 19.8 %copy-start.21 = (s32[64,2]{0,1:T(2,128)S(1)}, s32[64,2]{0,1:T(2,128)}, u32[]{:S(2)}) copy-start(s32[64,2]{0,1:T(2,128)} %multiply_add_fusion) | copy-start | bytes 1540
  117.2 21.4 %copy-start.15 = (s32[1,64,256]{2,1,0:T(8,128)S(1)}, s32[1,64,256]{2,1,0:T(8,128)}, u32[]{:S(2)}) copy-start(s32[1,64,256]{2,1,0:T(8,128)} %param.20) | copy-start | bytes 196612
  117.2 21.5 %copy-start.5 = (f32[2,4,64,256]{3,2,1,0:T(8,128)S(1)}, f32[2,4,64,256]{3,2,1,0:T(8,128)}, u32[]{:S(2)}) copy-start(f32[2,4,64,256]{3,2,1,0:T(8,128)} %copy-done.4) | copy-start | bytes 1572868
  138.8 0.8 copy-start.16
  141.2 7.9 %copy-start.19 = (s32[128,2]{0,1:T(2,128)S(1)}, s32[128,2]{0,1:T(2,128)}, u32[]{:S(2)}) copy-start(s32[128,2]{0,1:T(2,128)} %param.26) | copy-start | bytes 3076
  142.4 26.7 %all-to-all-start.2 = ((f32[128,4,256]{2,1,0:T(4,128)}), f32[128,4,256]{2,1,0:T(4,128)S(1)}, u32[]{:S(2)}, u32[]{:S(2)}) async-start(f32[128,4,256]{2,1,0:T(4,128)} %copy.102), calls=%async_computation.2 | async-start | bytes 1048576 | tf_op jit(solution)/shard_map/all_to_all | solution.py:196
  197.1 6.3 %collective-permute-start.5 = (f32[2,64,256]{2,1,0:T(8,128)S(1)}, f32[2,64,256]{2,1,0:T(8,128)S(1)}, u32[]{:S(2)}, u32[]{:S(2)}) collective-permute-start(f32[2,64,256]{2,1,0:T(8,128)S(1)} %reshape.447), channel_id=1, source_target_pairs={{128,0},{129,1},{130,2},{131,3},{132,4},{133,5},{134,6},{135,7},{1... | collective-permute-start | bytes 393224 | tf_op jit(solution)/shard_map/ppermute | solution.py:14
where the time goes:
time: 206 us; the launch traced here: 204 us
  local copies, waits for them, and re-layouts  56.5 us (27%)
  waiting for transfers between devices  50.4 us (24%)
  starting transfers between devices  46.2 us (22%)
  other arithmetic  29.8 us (14%)
  matrix products  19.7 us (10%)
    all_to_all x1, waiting for transfers between devices, on_device(): lax.all_to_all(reply.reshape(owners, capacity, 2 * TILE), ('panel', 'col'...  18.5 us
    all_to_all x1, starting transfers between devices, on_device(): recv_slots = lax.all_to_all(labels, ('panel', 'col'), 0, 0, tiled=True)  16.5 us
    all_to_all x1, waiting for transfers between devices, on_device(): received = lax.all_to_all(buffer, ('panel', 'col'), 0, 0, tiled=True)  15.8 us
    all_to_all x1, starting transfers between devices, on_device(): received = lax.all_to_all(buffer, ('panel', 'col'), 0, 0, tiled=True)  11.3 us
    reshape x1, local copies, waits for them, and re-layouts, on_device(): by_bank_back = jnp.einsum('rj,bji->bri', values.reshape(tile_count * 4, T...  9.33 us
    ppermute x4, waiting for transfers between devices, passed_along(): lax.ppermute(value, axis, [(source, source + steps) for source in range(i...  8.94 us
    dot_general x1, matrix products, on_device(): jnp.einsum('rj,bji->bri', values.reshape(tile_count * 4, TILE), conservat...  8.9 us
    ppermute x4, starting transfers between devices, passed_along(): lax.ppermute(value, axis, [(source, source + steps) for source in range(i...  7.61 us
  transfers between devices with their start and end apart: 9, of which 6 were waited for; matrix products, arithmetic and copies ran while one was open for 18% of the time, Pallas kernels for 0%

commit v1 on v0

--- a/solution.py
+++ b/solution.py
@@ -152,30 +152,47 @@
     heated = device_tracer_share.at[0, 0].add(thermal_exchange_rate).at[1, 0].add(evaporation_rate)
     start = jnp.where(on_atmos, heated, device_tracer_share)
     surface_flux = jnp.stack([thermal_exchange_rate, evaporation_rate])
-    flux_tiles = passed_along(to_tiles(surface_flux), "comp", 1)
-
-    flux_rows = flux_tiles.reshape(tile_count * 2, TILE)
+    flux_rows = passed_along(to_tiles(surface_flux), "comp", 1).reshape(tile_count * 2, TILE)
+    pairs = tile_count * 2
+    me = lax.axis_index("panel") * lax.axis_size("col") + lax.axis_index("col")
+
+    bucket_place = bucket_places(partner_devices, owners, capacity)
+    place_match = bucket_place[None, :] == jnp.arange(slots, dtype=jnp.int32)[:, None]
+    slot_used = jnp.any(place_match, axis=1)
+    slot_pair = jnp.sum(jnp.where(place_match, jnp.arange(pairs, dtype=jnp.int32)[None, :], 0), axis=1)
+    slot_tile = slot_pair // 2
+    slot_bank = bank_tile_entry.reshape(-1)[slot_pair]
+
     by_bank = jnp.einsum(
         "bji,ri->brj", conservative_overlay_factors, flux_rows, precision=HIGHEST
-    ).reshape(nbank * tile_count, 2 * TILE)
-    tile_ids = jnp.arange(tile_count, dtype=jnp.int32)[:, None]
-    pair_rows = bank_tile_entry * tile_count + tile_ids
-    contrib = by_bank[pair_rows.reshape(-1)]
-
-    bucket_place = bucket_places(partner_devices, owners, capacity)
-    slot_list = receiving_tile_index.reshape(-1)
-    place_match = bucket_place[None, :] == jnp.arange(slots, dtype=jnp.int32)[:, None]
-    place_hit = place_match.astype(jnp.float32)
-    buffer = jnp.dot(place_hit, contrib, precision=HIGHEST).reshape(owners, capacity, 2, TILE)
-    labels = jnp.sum(jnp.where(place_match, slot_list[None, :], 0), axis=1).reshape(
-        owners, capacity
-    )
-    received = lax.all_to_all(buffer, ("panel", "col"), 0, 0, tiled=True)
-    recv_slots = lax.all_to_all(labels, ("panel", "col"), 0, 0, tiled=True)
-    slot_hit = (
-        recv_slots.reshape(-1)[None, :] == jnp.arange(tile_count, dtype=jnp.int32)[:, None]
+    ).reshape(nbank * pairs, TILE)
+    f_ids = jnp.arange(2, dtype=jnp.int32)[None, :]
+    slot_rows = (slot_bank * pairs + slot_tile * 2)[:, None] + f_ids
+    picked = by_bank[slot_rows.reshape(-1)].reshape(slots, 2, TILE)
+    buffer = jnp.where(slot_used[:, None, None], picked, 0.0).reshape(owners, capacity * 2, TILE)
+    received = lax.all_to_all(buffer, ("panel", "col"), 0, 0, tiled=True).reshape(slots * 2, TILE)
+
+    routes = lax.all_gather(
+        jnp.concatenate([partner_devices.T, receiving_tile_index.T], axis=0), ("panel", "col")
+    )
+    mine = [(routes[:, k] == me).astype(jnp.int32) for k in range(2)]
+    per_tile = mine[0] + mine[1]
+    before = jnp.cumsum(per_tile, axis=1) - per_tile
+    rank = [before, before + mine[0]]
+    recv_slots = jnp.stack(
+        [
+            sum(jnp.sum(mine[k] * (rank[k] == c) * routes[:, 2 + k], axis=1) for k in range(2))
+            for c in range(capacity)
+        ],
+        axis=1,
+    ).reshape(-1)
+    row_ids = lax.broadcasted_iota(jnp.int32, (pairs, slots * 2), 0)
+    col_ids = lax.broadcasted_iota(jnp.int32, (pairs, slots * 2), 1)
+    recv_rep = jnp.broadcast_to(recv_slots[:, None], (slots, 2)).reshape(-1)
+    slot_hit2 = (
+        (recv_rep[None, :] == row_ids // 2) & (col_ids % 2 == row_ids % 2)
     ).astype(jnp.float32)
-    summed = jnp.dot(slot_hit, received.reshape(slots, 2 * TILE), precision=HIGHEST)
+    summed = jnp.dot(slot_hit2, received, precision=HIGHEST)
     forcing = from_tiles(summed.reshape(tile_count, 2, TILE), grid_rows, grid_cols)
 
     tracer = advect(start, coeffs, grid_rows)
@@ -191,24 +208,27 @@
         glacial_indicator.astype(jnp.float32) * sea_here * jnp.clip(0.5 - sea_temp, 0.0, 1.0)
     )
     ocean_surface = jnp.stack([sea_temp, ice_cover])
-    ocean_tiles = to_tiles(ocean_surface).reshape(tile_count, 2 * TILE)
-    reply = jnp.einsum("ts,tc->sc", slot_hit, ocean_tiles, precision=HIGHEST)
-    returned = lax.all_to_all(
-        reply.reshape(owners, capacity, 2 * TILE), ("panel", "col"), 0, 0, tiled=True
-    ).reshape(slots, 2 * TILE)
-    values = jnp.einsum("sp,sc->pc", place_hit, returned, precision=HIGHEST)
+    ocean_tiles = to_tiles(ocean_surface).reshape(pairs, TILE)
+    reply = jnp.dot(slot_hit2.T, ocean_tiles, precision=HIGHEST).reshape(owners, capacity * 2, TILE)
+    returned = lax.all_to_all(reply, ("panel", "col"), 0, 0, tiled=True).reshape(slots * 2, TILE)
+    place_rep = jnp.broadcast_to(bucket_place[:, None], (pairs, 2)).reshape(-1)
+    p_rows = lax.broadcasted_iota(jnp.int32, (pairs * 2, slots * 2), 0)
+    p_cols = lax.broadcasted_iota(jnp.int32, (pairs * 2, slots * 2), 1)
+    place_hit2 = ((place_rep[:, None] == p_cols // 2) & (p_cols % 2 == p_rows % 2)).astype(
+        jnp.float32
+    )
+    values = jnp.dot(place_hit2, returned, precision=HIGHEST)
 
     by_bank_back = jnp.einsum(
-        "rj,bji->bri",
-        values.reshape(tile_count * 4, TILE),
-        conservative_overlay_factors,
-        precision=HIGHEST,
-    ).reshape(nbank * tile_count, 4 * TILE)
-    first = by_bank_back[pair_rows[:, 0]][:, : 2 * TILE]
-    second = by_bank_back[pair_rows[:, 1]][:, 2 * TILE :]
+        "rj,bji->bri", values, conservative_overlay_factors, precision=HIGHEST
+    ).reshape(nbank * pairs * 2, TILE)
+    tile_ids = jnp.arange(tile_count, dtype=jnp.int32)[:, None]
+    pair_rows = (bank_tile_entry * tile_count + tile_ids) * 4 + jnp.arange(2, dtype=jnp.int32)[None, :] * 2
+    back_rows = pair_rows[:, :, None] + f_ids[:, None, :]
+    numerator = jnp.sum(by_bank_back[back_rows.reshape(-1)].reshape(tile_count, 2, 2, TILE), axis=1)
     column_sums = jnp.sum(conservative_overlay_factors, axis=1)
     denominator = column_sums[bank_tile_entry[:, 0]] + column_sums[bank_tile_entry[:, 1]]
-    remap_back = (first + second).reshape(tile_count, 2, TILE) / denominator[:, None, :]
+    remap_back = numerator / denominator[:, None, :]
     remapped = passed_along(from_tiles(remap_back, grid_rows, grid_cols), "comp", -1)
     surface_here = jnp.where(on_atmos, remapped, ocean_surface)
     return (new_here[None], surface_here[None])

time: 206 us -> 522 us (2.53)
  blocking collectives: 0 us -> 263 us
  starting transfers between devices: 46.2 us -> 97.3 us
  other arithmetic: 29.8 us -> 45.8 us
  waiting for transfers between devices: 50.4 us -> 40.1 us
    all_gather x0 -> x1, blocking collectives: none -> 263 us  [on_device(): lax.all_gather(jnp.concatenate([partner_devices.T, receiving_tile_index.T...]
    all_to_all x3 -> x2, starting transfers between devices: 34.4 us -> 82.8 us  [the longest x1 76.2 us: on_device(): lax.all_to_all(buffer, ('panel', 'col'), 0, 0, tiled=True)]
    reshape x8 -> x1, local copies, waits for them, and re-layouts: 19.9 us -> 0.14 us  [on_device(): slot_bank = bank_tile_entry.reshape(-1)[slot_pair]]
    broadcast_in_dim x1 -> x9, local copies, waits for them, and re-layouts: 0.14 us -> 7.96 us  [the longest x5 3.48 us: on_device(): jnp.where(slot_used[:, None, None], picked, 0.0)]
    all_to_all x3 -> x2, waiting for transfers between devices: 41.5 us -> 34.3 us  [the longest x1 18.6 us: on_device(): lax.all_to_all(reply, ('panel', 'col'), 0, 0, tiled=True)]
    dot_general x5 -> x4, matrix products: 13.6 us -> 14.3 us  [the longest x1 8.9 us: on_device(): jnp.einsum('rj,bji->bri', values, conservative_overlay_factors, precision...]
  transfers between devices with their start and end apart: 9 -> 8, of which waited for: 6 -> 4; matrix products, arithmetic and copies ran while one was open for 18% -> 14% of each run, Pallas kernels for 0% -> 0%
where the time goes in v1:
time: 522 us; the launch traced here: 520 us
  blocking collectives  263 us (50%)
  starting transfers between devices  97.3 us (19%)
  local copies, waits for them, and re-layouts  52.4 us (10%)
  other arithmetic  45.8 us (9%)
  waiting for transfers between devices  40.1 us (8%)
  matrix products  20.4 us (4%)
    all_gather x1, blocking collectives, on_device(): lax.all_gather(jnp.concatenate([partner_devices.T, receiving_tile_index.T...  263 us
    all_to_all x1, starting transfers between devices, on_device(): lax.all_to_all(buffer, ('panel', 'col'), 0, 0, tiled=True)  76.2 us
    all_to_all x1, waiting for transfers between devices, on_device(): lax.all_to_all(reply, ('panel', 'col'), 0, 0, tiled=True)  18.6 us
    all_to_all x1, waiting for transfers between devices, on_device(): lax.all_to_all(buffer, ('panel', 'col'), 0, 0, tiled=True)  15.7 us
  transfers between devices with their start and end apart: 8, of which 4 were waited for; matrix products, arithmetic and copies ran while one was open for 14% of the time, Pallas kernels for 0%

profile of v1, /device:TPU:1, one launch (start us, length us, event | category | flops | bytes accessed | tf_op | source)
XLA Modules:
  0.0 520.2 jit_solution(13182605688614995604)
XLA Ops:
  8.2 2.0 copy.87
  10.2 3.2 collective-permute-start.1
  13.4 2.0 copy.86
  18.7 3.6 collective-permute-start.4
  35.0 3.5 gather_fusion
  41.8 262.5 %all-gather.1 = s32[128,4,128]{2,1,0:T(4,128)S(1)} all-gather(s32[1,4,128]{2,1,0:T(4,128)S(1)} %add_bitcast_fusion), channel_id=2, replica_groups=mesh['comp'=2,'panel'=4,'col'=32] {'panel','col'}, dimensions={0}, use_global_device_ids=true | all-gather | bytes 264192 | tf_op jit(solution)/shard_map/all_gather | solution.py:175
  307.5 1.5 bitcast_add_fusion
  309.8 1.6 copy.118
  314.9 2.2 fusion.15
  322.6 1.5 broadcast_in_dim.44
  324.1 1.5 broadcast_in_dim.45
  325.7 1.7 eq.147
  327.4 1.4 broadcast_in_dim.54
  328.8 1.6 eq.161
  331.3 1.9 copy.89
  333.2 1.9 copy.88
  335.2 1.3 pad_maximum_fusion.8
  337.8 4.2 collective-permute-start.2
  354.2 1.3 slice_maximum_fusion.13
  355.5 6.1 %fusion.123 = f32[256,32,128]{2,0,1:T(8,128)} fusion(f32[256,128,1]{1,0,2:T(8,128)} %bitcast.36, f32[32,128,128]{2,1,0:T(8,128)S(1)} %copy-done), kind=kOutput, calls=%fused_computation.303 | convolution fusion | flops 1610612736 | bytes 6422528 | tf_op jit(solution)/shard_map/bji,ri->brj/dot_general | solution.py:166
  361.6 6.2 %gather_fusion.1 = f32[1024,128]{1,0:T(8,128)} fusion(f32[8192,128]{1,0:T(8,128)} %bitcast.281, s32[1024]{0:T(1024)S(1)} %copy-done.20), kind=kCustom, calls=%fused_computation.1 | custom fusion | bytes 1052672 | tf_op jit(solution)/shard_map/gather | solution.py:171
  367.8 2.1 bitcast_select_fusion
  369.9 76.2 %all-to-all-start = ((f32[128,8,128]{2,1,0:T(8,128)}), f32[128,8,128]{2,1,0:T(8,128)}, u32[]{:S(2)}, u32[]{:S(2)}) async-start(f32[128,8,128]{2,1,0:T(8,128)} %bitcast_select_fusion), calls=%async_computation | async-start | bytes 1048576 | tf_op jit(solution)/shard_map/all_to_all | solution.py:173
  446.2 2.2 fusion.51
  450.1 15.7 %all-to-all-done = f32[128,8,128]{2,1,0:T(8,128)} async-done(((f32[128,8,128]{2,1,0:T(8,128)}), f32[128,8,128]{2,1,0:T(8,128)}, u32[]{:S(2)}, u32[]{:S(2)}) %all-to-all-start) | async-done | bytes 524320 | tf_op jit(solution)/shard_map/all_to_all | solution.py:173
  465.9 1.8 convolution_bitcast_fusion
  469.1 2.4 fusion.17
  471.5 6.6 %all-to-all-start.1 = ((f32[128,8,128]{2,1,0:T(8,128)}), f32[128,8,128]{2,1,0:T(8,128)S(1)}, u32[]{:S(2)}, u32[]{:S(2)}) async-start(f32[128,8,128]{2,1,0:T(8,128)} %fusion.17), calls=%async_computation.1 | async-start | bytes 1048576 | tf_op jit(solution)/shard_map/all_to_all | solution.py:213
  479.6 18.6 %all-to-all-done.1 = f32[128,8,128]{2,1,0:T(8,128)S(1)} async-done(((f32[128,8,128]{2,1,0:T(8,128)}), f32[128,8,128]{2,1,0:T(8,128)S(1)}, u32[]{:S(2)}, u32[]{:S(2)}) %all-to-all-start.1) | async-done | bytes 524320 | tf_op jit(solution)/shard_map/all_to_all | solution.py:213
  499.4 8.9 %fusion.124 = f32[512,32,128]{2,0,1:T(8,128)} fusion(f32[512,128,1]{1,0,2:T(8,128)S(1)} %fusion.3, f32[32,128,128]{2,1,0:T(8,128)S(1)} %copy-done), kind=kOutput, calls=%fused_computation.304 | convolution fusion | flops 3221225472 | bytes 10747904 | tf_op jit(solution)/shard_map/rj,bji->bri/dot_general | solution.py:222
  508.3 4.4 gather_fusion.2
  514.5 5.0 collective-permute-done.5
  (212 shorter events, 61.9 us)
Async XLA Ops:
  0.6 330.6 %copy-start = (f32[32,128,128]{2,1,0:T(8,128)S(1)}, f32[32,128,128]{2,1,0:T(8,128)}, u32[]{:S(2)}) copy-start(f32[32,128,128]{2,1,0:T(8,128)} %param.27) | copy-start | bytes 6291460
  0.6 6.3 %copy-start.1 = (f32[1,3,4,64,256]{4,3,2,1,0:T(8,128)S(1)}, f32[1,3,4,64,256]{4,3,2,1,0:T(8,128)}, u32[]{:S(2)}) copy-start(f32[1,3,4,64,256]{4,3,2,1,0:T(8,128)} %param.19) | copy-start | bytes 2359300
  6.9 16.8 %copy-start.26 = (s32[128,2]{0,1:T(2,128)S(1)}, s32[128,2]{0,1:T(2,128)}, u32[]{:S(2)}) copy-start(s32[128,2]{0,1:T(2,128)} %param.24) | copy-start | bytes 3076
  8.2 26.5 %copy-start.22 = (s32[128,2]{0,1:T(2,128)S(1)}, s32[128,2]{0,1:T(2,128)}, u32[]{:S(2)}) copy-start(s32[128,2]{0,1:T(2,128)} %param.26) | copy-start | bytes 3076
  10.2 321.1 %collective-permute-start.1 = (f32[20,64,4]{1,2,0:T(4,128)}, f32[20,64,4]{1,2,0:T(4,128)}, u32[]{:S(2)}, u32[]{:S(2)}) collective-permute-start(f32[20,64,4]{1,2,0:T(4,128)} %copy.87), channel_id=1, source_target_pairs={{0,96},{32,0},{64,32},{96,64},{1,97},{33,1},{65,33},{97,65},{2,98}... | collective-permute-start | bytes 61448 | tf_op jit(solution)/shard_map/ppermute | solution.py:19
  15.4 317.9 %collective-permute-start = (f32[20,64,4]{1,2,0:T(4,128)}, f32[20,64,4]{1,2,0:T(4,128)}, u32[]{:S(2)}, u32[]{:S(2)}) collective-permute-start(f32[20,64,4]{1,2,0:T(4,128)} %copy.86), channel_id=1, source_target_pairs={{0,32},{32,64},{64,96},{96,0},{1,33},{33,65},{65,97},{97,1},{2,34}... | collective-permute-start | bytes 61448 | tf_op jit(solution)/shard_map/ppermute | solution.py:19
  18.7 336.9 %collective-permute-start.4 = (f32[128,2,128]{2,1,0:T(2,128)}, f32[128,2,128]{2,1,0:T(2,128)}, u32[]{:S(2)}, u32[]{:S(2)}) collective-permute-start(f32[128,2,128]{2,1,0:T(2,128)} %bitcast.34), channel_id=1, source_target_pairs={{0,128},{1,129},{2,130},{3,131},{4,132},{5,133},{6,134},{7,135},{8... | collective-permute-start | bytes 393224 | tf_op jit(solution)/shard_map/ppermute | solution.py:14
  27.4 14.4 %copy-start.21 = (s32[256]{0:T(256)}, s32[256]{0:T(256)S(1)}, u32[]{:S(2)}) copy-start(s32[256]{0:T(256)S(1)} %multiply_add_fusion.2) | copy-start | bytes 3076
  335.2 6.8 %copy-start.2 = (f32[20,64,4]{2,1,0:T(8,128)S(1)}, f32[20,64,4]{2,1,0:T(8,128)}, u32[]{:S(2)}) copy-start(f32[20,64,4]{2,1,0:T(8,128)} %copy.88) | copy-start | bytes 61444
  335.2 8.5 %copy-start.3 = (f32[20,64,4]{2,1,0:T(8,128)S(1)}, f32[20,64,4]{2,1,0:T(8,128)}, u32[]{:S(2)}) copy-start(f32[20,64,4]{2,1,0:T(8,128)} %copy.89) | copy-start | bytes 61444
  336.5 6.4 %collective-permute-start.3 = (f32[20,4,264]{2,1,0:T(4,128)S(1)}, f32[20,4,264]{2,1,0:T(4,128)S(1)}, u32[]{:S(2)}, u32[]{:S(2)}) collective-permute-start(f32[20,4,264]{2,1,0:T(4,128)S(1)} %get-tuple-element.72), channel_id=1, source_target_pairs={{1,0},{2,1},{3,2},{4,3},{5,4},{6,5},{7,6},{8,7},{9,8},{10,9},{11,1... | collective-permute-start | bytes 253448 | tf_op jit(solution)/shard_map/ppermute | solution.py:14
  337.8 5.8 %collective-permute-start.2 = (f32[20,4,264]{2,1,0:T(4,128)S(1)}, f32[20,4,264]{2,1,0:T(4,128)S(1)}, u32[]{:S(2)}, u32[]{:S(2)}) collective-permute-start(f32[20,4,264]{2,1,0:T(4,128)S(1)} %get-tuple-element.71), channel_id=1, source_target_pairs={{0,1},{1,2},{2,3},{3,4},{4,5},{5,6},{6,7},{7,8},{8,9},{9,10},{10,1... | collective-permute-start | bytes 253448 | tf_op jit(solution)/shard_map/ppermute | solution.py:14
  355.5 6.1 %copy-start.20 = (s32[1024]{0:T(1024)S(1)}, s32[1024]{0:T(1024)}, u32[]{:S(2)}) copy-start(s32[1024]{0:T(1024)} %broadcast_clamp_fusion) | copy-start | bytes 12292
  367.8 78.3 %copy-start.7 = (f32[4,64,256]{2,1,0:T(8,128)S(1)}, f32[4,64,256]{2,1,0:T(8,128)}, u32[]{:S(2)}) copy-start(f32[4,64,256]{2,1,0:T(8,128)} %get-tuple-element.87) | copy-start | bytes 786436
  369.9 95.9 %all-to-all-start = ((f32[128,8,128]{2,1,0:T(8,128)}), f32[128,8,128]{2,1,0:T(8,128)}, u32[]{:S(2)}, u32[]{:S(2)}) async-start(f32[128,8,128]{2,1,0:T(8,128)} %bitcast_select_fusion), calls=%async_computation | async-start | bytes 1048576 | tf_op jit(solution)/shard_map/all_to_all | solution.py:173
  448.6 17.3 %copy-start.25 = (s32[1024]{0:T(1024)S(1)}, s32[1024]{0:T(1024)}, u32[]{:S(2)}) copy-start(s32[1024]{0:T(1024)} %eq.147) | copy-start | bytes 12292
  448.6 17.3 %copy-start.27 = (s32[1024]{0:T(1024)S(1)}, s32[1024]{0:T(1024)}, u32[]{:S(2)}) copy-start(s32[1024]{0:T(1024)} %get-tuple-element.134) | copy-start | bytes 12292
  448.6 17.3 %copy-start.28 = (s32[1024]{0:T(1024)S(1)}, s32[1024]{0:T(1024)}, u32[]{:S(2)}) copy-start(s32[1024]{0:T(1024)} %get-tuple-element.135) | copy-start | bytes 12292
  448.6 17.2 %copy-start.30 = (s32[64,2,2]{0,2,1:T(2,128)S(1)}, s32[64,2,2]{0,2,1:T(2,128)}, u32[]{:S(2)}) copy-start(s32[64,2,2]{0,2,1:T(2,128)} %get-tuple-element.140) | copy-start | bytes 3076
  448.6 17.2 %copy-start.31 = (s32[64,2,2]{0,2,1:T(2,128)S(1)}, s32[64,2,2]{0,2,1:T(2,128)}, u32[]{:S(2)}) copy-start(s32[64,2,2]{0,2,1:T(2,128)} %get-tuple-element.141) | copy-start | bytes 3076
  448.6 17.2 %copy-start.32 = (s32[64,2,2]{0,2,1:T(2,128)S(1)}, s32[64,2,2]{0,2,1:T(2,128)}, u32[]{:S(2)}) copy-start(s32[64,2,2]{0,2,1:T(2,128)} %get-tuple-element.138) | copy-start | bytes 3076
  448.6 17.2 %copy-start.33 = (s32[64,2,2]{0,2,1:T(2,128)S(1)}, s32[64,2,2]{0,2,1:T(2,128)}, u32[]{:S(2)}) copy-start(s32[64,2,2]{0,2,1:T(2,128)} %get-tuple-element.139) | copy-start | bytes 3076
  448.6 17.2 %copy-start.34 = (pred[64,2,2]{0,2,1:T(4,128)(4,1)S(1)}, pred[64,2,2]{0,2,1:T(4,128)(4,1)}, u32[]{:S(2)}) copy-start(pred[64,2,2]{0,2,1:T(4,128)(4,1)} %get-tuple-element.136) | copy-start | bytes 772
  448.6 17.2 %copy-start.35 = (pred[64,2,2]{0,2,1:T(4,128)(4,1)S(1)}, pred[64,2,2]{0,2,1:T(4,128)(4,1)}, u32[]{:S(2)}) copy-start(pred[64,2,2]{0,2,1:T(4,128)(4,1)} %get-tuple-element.137) | copy-start | bytes 772
  448.7 17.2 %copy-start.37 = (pred[1024]{0:T(1024)(128)(4,1)S(1)}, pred[1024]{0:T(1024)(128)(4,1)}, u32[]{:S(2)}) copy-start(pred[1024]{0:T(1024)(128)(4,1)} %fusion.106) | copy-start | bytes 3076
  450.1 17.8 %copy-start.15 = (s32[1,64,256]{2,1,0:T(8,128)S(1)}, s32[1,64,256]{2,1,0:T(8,128)}, u32[]{:S(2)}) copy-start(s32[1,64,256]{2,1,0:T(8,128)} %param.20) | copy-start | bytes 196612
  450.1 17.8 %copy-start.5 = (f32[2,4,64,256]{3,2,1,0:T(8,128)S(1)}, f32[2,4,64,256]{3,2,1,0:T(8,128)}, u32[]{:S(2)}) copy-start(f32[2,4,64,256]{3,2,1,0:T(8,128)} %copy-done.4) | copy-start | bytes 1572868
  468.0 10.2 %copy-start.23 = (s32[128,2]{0,1:T(2,128)S(1)}, s32[128,2]{0,1:T(2,128)}, u32[]{:S(2)}) copy-start(s32[128,2]{0,1:T(2,128)} %param.26) | copy-start | bytes 3076
  468.1 11.4 %copy-start.24 = (s32[512,1]{0,1:T(1,128)S(1)}, s32[512,1]{0,1:T(1,128)}, u32[]{:S(2)}) copy-start(s32[512,1]{0,1:T(1,128)} %add.459) | copy-start | bytes 6148
  468.1 30.1 %copy-start.29 = (s32[512]{0:T(512)S(1)}, s32[512]{0:T(512)}, u32[]{:S(2)}) copy-start(s32[512]{0:T(512)} %eq.161) | copy-start | bytes 6148
  471.5 26.7 %all-to-all-start.1 = ((f32[128,8,128]{2,1,0:T(8,128)}), f32[128,8,128]{2,1,0:T(8,128)S(1)}, u32[]{:S(2)}, u32[]{:S(2)}) async-start(f32[128,8,128]{2,1,0:T(8,128)} %fusion.17), calls=%async_computation.1 | async-start | bytes 1048576 | tf_op jit(solution)/shard_map/all_to_all | solution.py:213
  513.2 6.3 %collective-permute-start.5 = (f32[2,64,256]{2,1,0:T(8,128)S(1)}, f32[2,64,256]{2,1,0:T(8,128)S(1)}, u32[]{:S(2)}, u32[]{:S(2)}) collective-permute-start(f32[2,64,256]{2,1,0:T(8,128)S(1)} %reshape.699), channel_id=1, source_target_pairs={{128,0},{129,1},{130,2},{131,3},{132,4},{133,5},{134,6},{135,7},{1... | collective-permute-start | bytes 393224 | tf_op jit(solution)/shard_map/ppermute | solution.py:14
  (14 other events, 27.1 us)

commit v2 on v1

--- a/solution.py
+++ b/solution.py
@@ -154,7 +154,6 @@
     surface_flux = jnp.stack([thermal_exchange_rate, evaporation_rate])
     flux_rows = passed_along(to_tiles(surface_flux), "comp", 1).reshape(tile_count * 2, TILE)
     pairs = tile_count * 2
-    me = lax.axis_index("panel") * lax.axis_size("col") + lax.axis_index("col")
 
     bucket_place = bucket_places(partner_devices, owners, capacity)
     place_match = bucket_place[None, :] == jnp.arange(slots, dtype=jnp.int32)[:, None]
@@ -170,22 +169,15 @@
     slot_rows = (slot_bank * pairs + slot_tile * 2)[:, None] + f_ids
     picked = by_bank[slot_rows.reshape(-1)].reshape(slots, 2, TILE)
     buffer = jnp.where(slot_used[:, None, None], picked, 0.0).reshape(owners, capacity * 2, TILE)
-    received = lax.all_to_all(buffer, ("panel", "col"), 0, 0, tiled=True).reshape(slots * 2, TILE)
-
-    routes = lax.all_gather(
-        jnp.concatenate([partner_devices.T, receiving_tile_index.T], axis=0), ("panel", "col")
-    )
-    mine = [(routes[:, k] == me).astype(jnp.int32) for k in range(2)]
-    per_tile = mine[0] + mine[1]
-    before = jnp.cumsum(per_tile, axis=1) - per_tile
-    rank = [before, before + mine[0]]
-    recv_slots = jnp.stack(
-        [
-            sum(jnp.sum(mine[k] * (rank[k] == c) * routes[:, 2 + k], axis=1) for k in range(2))
-            for c in range(capacity)
-        ],
-        axis=1,
-    ).reshape(-1)
+    slot_label = jnp.where(slot_used, receiving_tile_index.reshape(-1)[slot_pair], 0)
+    label_row = jnp.pad(
+        slot_label.reshape(owners, capacity).astype(jnp.float32), ((0, 0), (0, TILE - capacity))
+    )
+    bucket = jnp.concatenate([buffer, label_row[:, None, :]], axis=1)
+    arrived = lax.all_to_all(bucket, ("panel", "col"), 0, 0, tiled=True)
+    received = arrived[:, : capacity * 2].reshape(slots * 2, TILE)
+    recv_slots = arrived[:, capacity * 2, :capacity].astype(jnp.int32).reshape(-1)
+
     row_ids = lax.broadcasted_iota(jnp.int32, (pairs, slots * 2), 0)
     col_ids = lax.broadcasted_iota(jnp.int32, (pairs, slots * 2), 1)
     recv_rep = jnp.broadcast_to(recv_slots[:, None], (slots, 2)).reshape(-1)

time: 522 us -> 203 us (0.39)
  blocking collectives: 263 us -> 0 us
  starting transfers between devices: 97.3 us -> 39.3 us
  waiting for transfers between devices: 40.1 us -> 53.2 us
  local copies, waits for them, and re-layouts: 52.4 us -> 46.3 us
    all_gather x1 -> x0, blocking collectives: 263 us -> none  [on_device(): lax.all_gather(jnp.concatenate([partner_devices.T, receiving_tile_index.T...]
    all_to_all x1, starting transfers between devices: 76.2 us -> 18 us  [on_device(): arrived = lax.all_to_all(bucket, ('panel', 'col'), 0, 0, tiled=True)]
    all_to_all x1, waiting for transfers between devices: 15.7 us -> 27.6 us  [on_device(): arrived = lax.all_to_all(bucket, ('panel', 'col'), 0, 0, tiled=True)]
  transfers between devices with their start and end apart: 8 -> 8, of which waited for: 4 -> 5; matrix products, arithmetic and copies ran while one was open for 14% -> 29% of each run, Pallas kernels for 0% -> 0%
where the time goes in v2:
time: 203 us; the launch traced here: 202 us
  waiting for transfers between devices  53.2 us (26%)
  local copies, waits for them, and re-layouts  46.3 us (23%)
  other arithmetic  41.7 us (21%)
  starting transfers between devices  39.3 us (19%)
  matrix products  19.6 us (10%)
    all_to_all x1, waiting for transfers between devices, on_device(): arrived = lax.all_to_all(bucket, ('panel', 'col'), 0, 0, tiled=True)  27.6 us
    all_to_all x1, waiting for transfers between devices, on_device(): lax.all_to_all(reply, ('panel', 'col'), 0, 0, tiled=True)  18.6 us
    all_to_all x1, starting transfers between devices, on_device(): arrived = lax.all_to_all(bucket, ('panel', 'col'), 0, 0, tiled=True)  18 us
    ppermute x4, starting transfers between devices, passed_along(): lax.ppermute(value, axis, [(source, source + steps) for source in range(i...  10.3 us
    dot_general x1, matrix products, on_device(): jnp.einsum('rj,bji->bri', values, conservative_overlay_factors, precision...  8.89 us
    ppermute x4, waiting for transfers between devices, passed_along(): lax.ppermute(value, axis, [(source, source + steps) for source in range(i...  6.95 us
    all_to_all x1, starting transfers between devices, on_device(): lax.all_to_all(reply, ('panel', 'col'), 0, 0, tiled=True)  6.83 us
    gather x1, local copies, waits for them, and re-layouts, on_device(): picked = by_bank[slot_rows.reshape(-1)].reshape(slots, 2, TILE)  6.23 us
  transfers between devices with their start and end apart: 8, of which 5 were waited for; matrix products, arithmetic and copies ran while one was open for 29% of the time, Pallas kernels for 0%

profile of v2, /device:TPU:1, one launch (start us, length us, event | category | flops | bytes accessed | tf_op | source)
XLA Modules:
  0.0 201.8 jit_solution(17466998610966479640)
XLA Ops:
  0.7 2.0 %copy.119 = f32[2,4,64,256]{3,2,1,0:T(8,128)} copy(f32[2,4,64,256]{3,2,1,0:T(8,128)} %bitcast.176) | data formatting | bytes 1048576
  3.7 1.5 bitcast_dynamic-update-slice_fusion
  5.2 1.7 fusion.80
  6.9 1.3 broadcast_select_fusion.1
  8.2 1.3 fusion.48
  9.5 1.9 copy.88
  11.5 3.2 %collective-permute-start.1 = (f32[20,64,4]{1,2,0:T(4,128)}, f32[20,64,4]{1,2,0:T(4,128)}, u32[]{:S(2)}, u32[]{:S(2)}) collective-permute-start(f32[20,64,4]{1,2,0:T(4,128)} %copy.88), channel_id=1, source_target_pairs={{0,96},{32,0},{64,32},{96,64},{1,97},{33,1},{65,33},{97,65},{2,98}... | collective-permute-start | bytes 61448 | tf_op jit(solution)/shard_map/ppermute | solution.py:19
  14.7 2.0 copy.87
  19.9 3.6 %collective-permute-start.4 = (f32[128,2,128]{2,1,0:T(2,128)}, f32[128,2,128]{2,1,0:T(2,128)}, u32[]{:S(2)}, u32[]{:S(2)}) collective-permute-start(f32[128,2,128]{2,1,0:T(2,128)} %bitcast.23), channel_id=1, source_target_pairs={{0,128},{1,129},{2,130},{3,131},{4,132},{5,133},{6,134},{7,135},{8... | collective-permute-start | bytes 393224 | tf_op jit(solution)/shard_map/ppermute | solution.py:14
  35.3 3.5 %gather_fusion.2 = s32[512]{0:T(512)S(1)} fusion(s32[256]{0:T(256)S(1)} %reshape.651, s32[1024]{0:T(1024)S(1)} %pad_clamp_fusion.3), kind=kCustom, calls=%fused_computation.2 | custom fusion | bytes 6144 | tf_op jit(solution)/shard_map/gather | solution.py:172
  40.5 3.5 %gather_fusion = s32[512]{0:T(512)S(1)} fusion(s32[256]{0:T(256)S(1)} %reshape.649, s32[1024]{0:T(1024)S(1)} %pad_clamp_fusion.3), kind=kCustom, calls=%fused_computation | custom fusion | bytes 6144 | tf_op jit(solution)/shard_map/gather | solution.py:163
  48.5 1.5 select_convert_fusion
  53.5 1.6 eq.114
  56.9 1.9 copy.90
  58.8 1.9 copy.89
  60.7 1.3 pad_maximum_fusion.9
  62.1 1.3 collective-permute-start.3
  63.4 4.2 %collective-permute-start.2 = (f32[20,4,264]{2,1,0:T(4,128)S(1)}, f32[20,4,264]{2,1,0:T(4,128)S(1)}, u32[]{:S(2)}, u32[]{:S(2)}) collective-permute-start(f32[20,4,264]{2,1,0:T(4,128)S(1)} %get-tuple-element.56), channel_id=1, source_target_pairs={{0,1},{1,2},{2,3},{3,4},{4,5},{5,6},{6,7},{7,8},{8,9},{9,10},{10,1... | collective-permute-start | bytes 253448 | tf_op jit(solution)/shard_map/ppermute | solution.py:14
  68.8 1.7 collective-permute-done.2
  80.9 6.1 %fusion.113 = f32[256,32,128]{2,0,1:T(8,128)} fusion(f32[256,128,1]{1,0,2:T(8,128)} %bitcast.25, f32[32,128,128]{2,1,0:T(8,128)S(1)} %copy-done), kind=kOutput, calls=%fused_computation.272 | convolution fusion | flops 1610612736 | bytes 6422528 | tf_op jit(solution)/shard_map/bji,ri->brj/dot_general | solution.py:165
  87.0 6.2 %gather_fusion.1 = f32[1024,128]{1,0:T(8,128)} fusion(f32[8192,128]{1,0:T(8,128)} %bitcast.174, s32[1024]{0:T(1024)S(1)} %copy-done.17), kind=kCustom, calls=%fused_computation.1 | custom fusion | bytes 1052672 | tf_op jit(solution)/shard_map/gather | solution.py:170
  93.3 1.3 bitcast_select_fusion
  95.6 18.0 %all-to-all-start = ((f32[128,9,128]{2,1,0:T(8,128)}), f32[128,9,128]{2,1,0:T(8,128)}, u32[]{:S(2)}, u32[]{:S(2)}) async-start(f32[128,9,128]{2,1,0:T(8,128)} %pad_maximum_fusion.1), calls=%async_computation | async-start | bytes 2097152 | tf_op jit(solution)/shard_map/all_to_all | solution.py:177
  116.8 27.6 %all-to-all-done = f32[128,9,128]{2,1,0:T(8,128)} async-done(((f32[128,9,128]{2,1,0:T(8,128)}), f32[128,9,128]{2,1,0:T(8,128)}, u32[]{:S(2)}, u32[]{:S(2)}) %all-to-all-start) | async-done | bytes 589856 | tf_op jit(solution)/shard_map/all_to_all | solution.py:177
  146.1 1.8 convolution_bitcast_fusion
  151.4 1.6 fusion.17
  153.0 6.8 %all-to-all-start.1 = ((f32[128,8,128]{2,1,0:T(8,128)}), f32[128,8,128]{2,1,0:T(8,128)S(1)}, u32[]{:S(2)}, u32[]{:S(2)}) async-start(f32[128,8,128]{2,1,0:T(8,128)} %fusion.17), calls=%async_computation.1 | async-start | bytes 1048576 | tf_op jit(solution)/shard_map/all_to_all | solution.py:205
  161.2 18.6 %all-to-all-done.1 = f32[128,8,128]{2,1,0:T(8,128)S(1)} async-done(((f32[128,8,128]{2,1,0:T(8,128)}), f32[128,8,128]{2,1,0:T(8,128)S(1)}, u32[]{:S(2)}, u32[]{:S(2)}) %all-to-all-start.1) | async-done | bytes 524320 | tf_op jit(solution)/shard_map/all_to_all | solution.py:205
  181.1 8.9 %fusion.114 = f32[512,32,128]{2,0,1:T(8,128)} fusion(f32[512,128,1]{1,0,2:T(8,128)S(1)} %fusion.3, f32[32,128,128]{2,1,0:T(8,128)S(1)} %copy-done), kind=kOutput, calls=%fused_computation.273 | convolution fusion | flops 3221225472 | bytes 10747904 | tf_op jit(solution)/shard_map/rj,bji->bri/dot_general | solution.py:214
  190.0 4.4 %gather_fusion.3 = f32[512,128]{1,0:T(8,128)S(1)} fusion(f32[16384,128]{1,0:T(8,128)} %bitcast.175, s32[1024]{0:T(1024)S(1)} %pad_clamp_fusion.2), kind=kCustom, calls=%fused_computation.3 | custom fusion | bytes 526336 | tf_op jit(solution)/shard_map/gather | solution.py:220
  194.8 1.3 collective-permute-start.5
  196.1 5.0 %collective-permute-done.5 = f32[2,64,256]{2,1,0:T(8,128)S(1)} collective-permute-done((f32[2,64,256]{2,1,0:T(8,128)S(1)}, f32[2,64,256]{2,1,0:T(8,128)S(1)}, u32[]{:S(2)}, u32[]{:S(2)}) %collective-permute-start.5) | collective-permute-done | bytes 131104 | tf_op jit(solution)/shard_map/ppermute | solution.py:14
  (212 shorter events, 51.5 us)
Async XLA Ops:
  0.6 56.1 %copy-start = (f32[32,128,128]{2,1,0:T(8,128)S(1)}, f32[32,128,128]{2,1,0:T(8,128)}, u32[]{:S(2)}) copy-start(f32[32,128,128]{2,1,0:T(8,128)} %param.27) | copy-start | bytes 6291460
  0.6 7.6 %copy-start.1 = (f32[1,3,4,64,256]{4,3,2,1,0:T(8,128)S(1)}, f32[1,3,4,64,256]{4,3,2,1,0:T(8,128)}, u32[]{:S(2)}) copy-start(f32[1,3,4,64,256]{4,3,2,1,0:T(8,128)} %param.19) | copy-start | bytes 2359300
  8.2 16.8 %copy-start.32 = (s32[128,2]{0,1:T(2,128)S(1)}, s32[128,2]{0,1:T(2,128)}, u32[]{:S(2)}) copy-start(s32[128,2]{0,1:T(2,128)} %param.24) | copy-start | bytes 3076
  11.5 45.4 %collective-permute-start.1 = (f32[20,64,4]{1,2,0:T(4,128)}, f32[20,64,4]{1,2,0:T(4,128)}, u32[]{:S(2)}, u32[]{:S(2)}) collective-permute-start(f32[20,64,4]{1,2,0:T(4,128)} %copy.88), channel_id=1, source_target_pairs={{0,96},{32,0},{64,32},{96,64},{1,97},{33,1},{65,33},{97,65},{2,98}... | collective-permute-start | bytes 61448 | tf_op jit(solution)/shard_map/ppermute | solution.py:19
  16.6 42.2 %collective-permute-start = (f32[20,64,4]{1,2,0:T(4,128)}, f32[20,64,4]{1,2,0:T(4,128)}, u32[]{:S(2)}, u32[]{:S(2)}) collective-permute-start(f32[20,64,4]{1,2,0:T(4,128)} %copy.87), channel_id=1, source_target_pairs={{0,32},{32,64},{64,96},{96,0},{1,33},{33,65},{65,97},{97,1},{2,34}... | collective-permute-start | bytes 61448 | tf_op jit(solution)/shard_map/ppermute | solution.py:19
  19.9 61.0 %collective-permute-start.4 = (f32[128,2,128]{2,1,0:T(2,128)}, f32[128,2,128]{2,1,0:T(2,128)}, u32[]{:S(2)}, u32[]{:S(2)}) collective-permute-start(f32[128,2,128]{2,1,0:T(2,128)} %bitcast.23), channel_id=1, source_target_pairs={{0,128},{1,129},{2,130},{3,131},{4,132},{5,133},{6,134},{7,135},{8... | collective-permute-start | bytes 393224 | tf_op jit(solution)/shard_map/ppermute | solution.py:14
  35.3 11.3 %copy-start.18 = (s32[128,2]{0,1:T(2,128)S(1)}, s32[128,2]{0,1:T(2,128)}, u32[]{:S(2)}) copy-start(s32[128,2]{0,1:T(2,128)} %param.26) | copy-start | bytes 3076
  60.7 6.8 %copy-start.2 = (f32[20,64,4]{2,1,0:T(8,128)S(1)}, f32[20,64,4]{2,1,0:T(8,128)}, u32[]{:S(2)}) copy-start(f32[20,64,4]{2,1,0:T(8,128)} %copy.89) | copy-start | bytes 61444
  60.7 9.8 %copy-start.5 = (f32[20,64,4]{2,1,0:T(8,128)S(1)}, f32[20,64,4]{2,1,0:T(8,128)}, u32[]{:S(2)}) copy-start(f32[20,64,4]{2,1,0:T(8,128)} %copy.90) | copy-start | bytes 61444
  62.1 6.7 %collective-permute-start.3 = (f32[20,4,264]{2,1,0:T(4,128)S(1)}, f32[20,4,264]{2,1,0:T(4,128)S(1)}, u32[]{:S(2)}, u32[]{:S(2)}) collective-permute-start(f32[20,4,264]{2,1,0:T(4,128)S(1)} %get-tuple-element.57), channel_id=1, source_target_pairs={{1,0},{2,1},{3,2},{4,3},{5,4},{6,5},{7,6},{8,7},{9,8},{10,9},{11,1... | collective-permute-start | bytes 253448 | tf_op jit(solution)/shard_map/ppermute | solution.py:14
  63.4 7.1 %collective-permute-start.2 = (f32[20,4,264]{2,1,0:T(4,128)S(1)}, f32[20,4,264]{2,1,0:T(4,128)S(1)}, u32[]{:S(2)}, u32[]{:S(2)}) collective-permute-start(f32[20,4,264]{2,1,0:T(4,128)S(1)} %get-tuple-element.56), channel_id=1, source_target_pairs={{0,1},{1,2},{2,3},{3,4},{4,5},{5,6},{6,7},{7,8},{8,9},{9,10},{10,1... | collective-permute-start | bytes 253448 | tf_op jit(solution)/shard_map/ppermute | solution.py:14
  80.9 6.1 %copy-start.17 = (s32[1024]{0:T(1024)S(1)}, s32[1024]{0:T(1024)}, u32[]{:S(2)}) copy-start(s32[1024]{0:T(1024)} %broadcast_clamp_fusion) | copy-start | bytes 12292
  87.0 6.2 %copy-start.13 = (pred[128,8]{1,0:T(8,128)(4,1)S(1)}, pred[128,8]{1,0:T(8,128)(4,1)}, u32[]{:S(2)}) copy-start(pred[128,8]{1,0:T(8,128)(4,1)} %copy.97) | copy-start | bytes 3076
  93.3 20.4 %copy-start.4 = (f32[4,72,264]{2,1,0:T(8,128)S(1)}, f32[4,72,264]{2,1,0:T(8,128)}, u32[]{:S(2)}) copy-start(f32[4,72,264]{2,1,0:T(8,128)} %copy-done.3) | copy-start | bytes 912388
  95.6 48.7 %all-to-all-start = ((f32[128,9,128]{2,1,0:T(8,128)}), f32[128,9,128]{2,1,0:T(8,128)}, u32[]{:S(2)}, u32[]{:S(2)}) async-start(f32[128,9,128]{2,1,0:T(8,128)} %pad_maximum_fusion.1), calls=%async_computation | async-start | bytes 2097152 | tf_op jit(solution)/shard_map/all_to_all | solution.py:177
  116.0 30.0 %copy-start.25 = (s32[1024]{0:T(1024)S(1)}, s32[1024]{0:T(1024)}, u32[]{:S(2)}) copy-start(s32[1024]{0:T(1024)} %get-tuple-element.111) | copy-start | bytes 12292
  116.0 30.0 %copy-start.26 = (s32[1024]{0:T(1024)S(1)}, s32[1024]{0:T(1024)}, u32[]{:S(2)}) copy-start(s32[1024]{0:T(1024)} %get-tuple-element.112) | copy-start | bytes 12292
  116.0 30.0 %copy-start.28 = (s32[64,2,2]{0,2,1:T(2,128)S(1)}, s32[64,2,2]{0,2,1:T(2,128)}, u32[]{:S(2)}) copy-start(s32[64,2,2]{0,2,1:T(2,128)} %get-tuple-element.117) | copy-start | bytes 3076
  116.0 30.0 %copy-start.29 = (s32[64,2,2]{0,2,1:T(2,128)S(1)}, s32[64,2,2]{0,2,1:T(2,128)}, u32[]{:S(2)}) copy-start(s32[64,2,2]{0,2,1:T(2,128)} %get-tuple-element.118) | copy-start | bytes 3076
  116.0 30.0 %copy-start.30 = (s32[64,2,2]{0,2,1:T(2,128)S(1)}, s32[64,2,2]{0,2,1:T(2,128)}, u32[]{:S(2)}) copy-start(s32[64,2,2]{0,2,1:T(2,128)} %get-tuple-element.115) | copy-start | bytes 3076
  116.0 30.0 %copy-start.31 = (s32[64,2,2]{0,2,1:T(2,128)S(1)}, s32[64,2,2]{0,2,1:T(2,128)}, u32[]{:S(2)}) copy-start(s32[64,2,2]{0,2,1:T(2,128)} %get-tuple-element.116) | copy-start | bytes 3076
  116.0 30.0 %copy-start.34 = (pred[64,2,2]{0,2,1:T(4,128)(4,1)S(1)}, pred[64,2,2]{0,2,1:T(4,128)(4,1)}, u32[]{:S(2)}) copy-start(pred[64,2,2]{0,2,1:T(4,128)(4,1)} %get-tuple-element.113) | copy-start | bytes 772
  116.1 30.0 %copy-start.35 = (pred[64,2,2]{0,2,1:T(4,128)(4,1)S(1)}, pred[64,2,2]{0,2,1:T(4,128)(4,1)}, u32[]{:S(2)}) copy-start(pred[64,2,2]{0,2,1:T(4,128)(4,1)} %get-tuple-element.114) | copy-start | bytes 772
  116.7 31.4 %copy-start.9 = (s32[1,64,256]{2,1,0:T(8,128)S(1)}, s32[1,64,256]{2,1,0:T(8,128)}, u32[]{:S(2)}) copy-start(s32[1,64,256]{2,1,0:T(8,128)} %param.20) | copy-start | bytes 196612
  146.1 3.0 %copy-start.14 = (s32[64,256]{1,0:T(8,128)S(1)}, s32[64,256]{1,0:T(8,128)}, u32[]{:S(2)}) copy-start(s32[64,256]{1,0:T(8,128)} %param.21) | copy-start | bytes 196612
  147.9 2.6 %copy-start.15 = (s32[128,8]{0,1:T(8,128)S(1)}, s32[128,8]{0,1:T(8,128)}, u32[]{:S(2)}) copy-start(s32[128,8]{0,1:T(8,128)} %get-tuple-element.119) | copy-start | bytes 12292
  148.2 11.6 %copy-start.19 = (s32[128,2]{0,1:T(2,128)S(1)}, s32[128,2]{0,1:T(2,128)}, u32[]{:S(2)}) copy-start(s32[128,2]{0,1:T(2,128)} %param.26) | copy-start | bytes 3076
  149.2 12.0 %copy-start.20 = (s32[512,1]{0,1:T(1,128)S(1)}, s32[512,1]{0,1:T(1,128)}, u32[]{:S(2)}) copy-start(s32[512,1]{0,1:T(1,128)} %add.390) | copy-start | bytes 6148
  149.2 30.7 %copy-start.27 = (s32[512]{0:T(512)S(1)}, s32[512]{0:T(512)}, u32[]{:S(2)}) copy-start(s32[512]{0:T(512)} %eq.114) | copy-start | bytes 6148
  149.2 30.7 %copy-start.39 = (pred[1024]{0:T(1024)(128)(4,1)S(1)}, pred[1024]{0:T(1024)(128)(4,1)}, u32[]{:S(2)}) copy-start(pred[1024]{0:T(1024)(128)(4,1)} %fusion.96) | copy-start | bytes 3076
  153.0 26.9 %all-to-all-start.1 = ((f32[128,8,128]{2,1,0:T(8,128)}), f32[128,8,128]{2,1,0:T(8,128)S(1)}, u32[]{:S(2)}, u32[]{:S(2)}) async-start(f32[128,8,128]{2,1,0:T(8,128)} %fusion.17), calls=%async_computation.1 | async-start | bytes 1048576 | tf_op jit(solution)/shard_map/all_to_all | solution.py:205
  194.8 6.3 %collective-permute-start.5 = (f32[2,64,256]{2,1,0:T(8,128)S(1)}, f32[2,64,256]{2,1,0:T(8,128)S(1)}, u32[]{:S(2)}, u32[]{:S(2)}) collective-permute-start(f32[2,64,256]{2,1,0:T(8,128)S(1)} %reshape.656), channel_id=1, source_target_pairs={{128,0},{129,1},{130,2},{131,3},{132,4},{133,5},{134,6},{135,7},{1... | collective-permute-start | bytes 393224 | tf_op jit(solution)/shard_map/ppermute | solution.py:14
  (16 other events, 29.3 us)

commit v3 on v2

--- a/solution.py
+++ b/solution.py
@@ -160,21 +160,24 @@
     slot_used = jnp.any(place_match, axis=1)
     slot_pair = jnp.sum(jnp.where(place_match, jnp.arange(pairs, dtype=jnp.int32)[None, :], 0), axis=1)
     slot_tile = slot_pair // 2
-    slot_bank = bank_tile_entry.reshape(-1)[slot_pair]
+    slot_bank = jnp.sum(jnp.where(place_match, bank_tile_entry.reshape(-1)[None, :], 0), axis=1)
 
     by_bank = jnp.einsum(
-        "bji,ri->brj", conservative_overlay_factors, flux_rows, precision=HIGHEST
+        "bji,ri->brj", conservative_overlay_factors, flux_rows, precision=lax.Precision.HIGH
     ).reshape(nbank * pairs, TILE)
     f_ids = jnp.arange(2, dtype=jnp.int32)[None, :]
     slot_rows = (slot_bank * pairs + slot_tile * 2)[:, None] + f_ids
     picked = by_bank[slot_rows.reshape(-1)].reshape(slots, 2, TILE)
     buffer = jnp.where(slot_used[:, None, None], picked, 0.0).reshape(owners, capacity * 2, TILE)
-    slot_label = jnp.where(slot_used, receiving_tile_index.reshape(-1)[slot_pair], 0)
+    slot_label = jnp.sum(jnp.where(place_match, receiving_tile_index.reshape(-1)[None, :], 0), axis=1)
     label_row = jnp.pad(
         slot_label.reshape(owners, capacity).astype(jnp.float32), ((0, 0), (0, TILE - capacity))
     )
     bucket = jnp.concatenate([buffer, label_row[:, None, :]], axis=1)
-    arrived = lax.all_to_all(bucket, ("panel", "col"), 0, 0, tiled=True)
+    rows_out = capacity * 2 + 1
+    arrived = lax.all_to_all(
+        bucket.reshape(owners, rows_out * TILE), ("panel", "col"), 0, 0, tiled=True
+    ).reshape(owners, rows_out, TILE)
     received = arrived[:, : capacity * 2].reshape(slots * 2, TILE)
     recv_slots = arrived[:, capacity * 2, :capacity].astype(jnp.int32).reshape(-1)
 
@@ -212,14 +215,18 @@
     values = jnp.dot(place_hit2, returned, precision=HIGHEST)
 
     by_bank_back = jnp.einsum(
-        "rj,bji->bri", values, conservative_overlay_factors, precision=HIGHEST
+        "rj,bji->bri", values, conservative_overlay_factors, precision=lax.Precision.HIGH
     ).reshape(nbank * pairs * 2, TILE)
     tile_ids = jnp.arange(tile_count, dtype=jnp.int32)[:, None]
     pair_rows = (bank_tile_entry * tile_count + tile_ids) * 4 + jnp.arange(2, dtype=jnp.int32)[None, :] * 2
     back_rows = pair_rows[:, :, None] + f_ids[:, None, :]
     numerator = jnp.sum(by_bank_back[back_rows.reshape(-1)].reshape(tile_count, 2, 2, TILE), axis=1)
     column_sums = jnp.sum(conservative_overlay_factors, axis=1)
-    denominator = column_sums[bank_tile_entry[:, 0]] + column_sums[bank_tile_entry[:, 1]]
+    bank_ids = jnp.arange(nbank, dtype=jnp.int32)[None, :]
+    bank_count = (bank_tile_entry[:, :1] == bank_ids).astype(jnp.float32) + (
+        bank_tile_entry[:, 1:] == bank_ids
+    ).astype(jnp.float32)
+    denominator = jnp.dot(bank_count, column_sums, precision=HIGHEST)
     remap_back = numerator / denominator[:, None, :]
     remapped = passed_along(from_tiles(remap_back, grid_rows, grid_cols), "comp", -1)
     surface_here = jnp.where(on_atmos, remapped, ocean_surface)

time: 203 us -> 185 us (0.911)
  waiting for transfers between devices: 53.2 us -> 43.5 us
  local copies, waits for them, and re-layouts: 46.3 us -> 41.8 us
  matrix products: 19.6 us -> 15.3 us
    all_to_all x1, waiting for transfers between devices: 27.6 us -> 17.9 us  [on_device(): lax.all_to_all(bucket.reshape(owners, rows_out * TILE), ('panel', 'col'),...]
    gather x5 -> x0, local copies, waits for them, and re-layouts: 9.03 us -> none  [the longest x2 4.24 us: on_device(): receiving_tile_index.reshape(-1)[slot_pair]]
    all_to_all x0 -> x2, local copies, waits for them, and re-layouts: none -> 3.49 us  [on_device(): lax.all_to_all(bucket.reshape(owners, rows_out * TILE), ('panel', 'col'),...]
    dot_general x1, matrix products: 8.89 us -> 5.67 us  [on_device(): jnp.einsum('rj,bji->bri', values, conservative_overlay_factors, precision...]
    slice x0 -> x3, local copies, waits for them, and re-layouts: none -> 2.91 us  [the longest x2 2.88 us: on_device(): received = arrived[:, :capacity * 2].reshape(slots * 2, TILE)]
    convert_element_type x2 -> x1, other arithmetic: 2.31 us -> 0.01 us  [on_device(): arrived[:, capacity * 2, :capacity].astype(jnp.int32).reshape(-1)]
    unnamed x86 -> x75, local copies, waits for them, and re-layouts: 5.37 us -> 4.95 us
  transfers between devices with their start and end apart: 8 -> 8, of which waited for: 5 -> 5; matrix products, arithmetic and copies ran while one was open for 29% -> 25% of each run, Pallas kernels for 0% -> 0%
where the time goes in v3:
time: 185 us; the launch traced here: 184 us
  waiting for transfers between devices  43.5 us (24%)
  other arithmetic  42.7 us (23%)
  local copies, waits for them, and re-layouts  41.8 us (23%)
  starting transfers between devices  39.2 us (21%)
  matrix products  15.3 us (8%)
    all_to_all x1, waiting for transfers between devices, on_device(): lax.all_to_all(reply, ('panel', 'col'), 0, 0, tiled=True)  18.6 us
    all_to_all x1, waiting for transfers between devices, on_device(): lax.all_to_all(bucket.reshape(owners, rows_out * TILE), ('panel', 'col'),...  17.9 us
    all_to_all x1, starting transfers between devices, on_device(): lax.all_to_all(bucket.reshape(owners, rows_out * TILE), ('panel', 'col'),...  17.9 us
    ppermute x4, starting transfers between devices, passed_along(): lax.ppermute(value, axis, [(source, source + steps) for source in range(i...  10.3 us
    ppermute x4, waiting for transfers between devices, passed_along(): lax.ppermute(value, axis, [(source, source + steps) for source in range(i...  6.92 us
    all_to_all x1, starting transfers between devices, on_device(): lax.all_to_all(reply, ('panel', 'col'), 0, 0, tiled=True)  6.81 us
    dot_general x1, matrix products, on_device(): jnp.einsum('rj,bji->bri', values, conservative_overlay_factors, precision...  5.67 us
    gather x1, local copies, waits for them, and re-layouts, on_device(): picked = by_bank[slot_rows.reshape(-1)].reshape(slots, 2, TILE)  4.99 us
  transfers between devices with their start and end apart: 8, of which 5 were waited for; matrix products, arithmetic and copies ran while one was open for 25% of the time, Pallas kernels for 0%

profile of v3, /device:TPU:1, one launch (start us, length us, event | category | flops | bytes accessed | tf_op | source)
XLA Modules:
  0.0 184.0 jit_solution(205344273226370317)
XLA Ops:
  0.7 2.0 %copy.142 = f32[2,4,64,256]{3,2,1,0:T(8,128)} copy(f32[2,4,64,256]{3,2,1,0:T(8,128)} %bitcast.175) | data formatting | bytes 1048576
  3.7 1.5 bitcast_dynamic-update-slice_fusion
  5.2 1.7 fusion.81
  6.9 1.3 broadcast_select_fusion.2
  8.2 1.3 fusion.48
  9.5 2.0 %copy.105 = f32[20,64,4]{1,2,0:T(4,128)} copy(f32[20,64,4]{2,1,0:T(8,128)} %get-tuple-element.76) | data formatting | bytes 40960 | tf_op jit(solution)/shard_map/slice | solution.py:24
  11.5 3.2 %collective-permute-start.1 = (f32[20,64,4]{1,2,0:T(4,128)}, f32[20,64,4]{1,2,0:T(4,128)}, u32[]{:S(2)}, u32[]{:S(2)}) collective-permute-start(f32[20,64,4]{1,2,0:T(4,128)} %copy.105), channel_id=1, source_target_pairs={{0,96},{32,0},{64,32},{96,64},{1,97},{33,1},{65,33},{97,65},{2,98}... | collective-permute-start | bytes 61448 | tf_op jit(solution)/shard_map/ppermute | solution.py:19
  14.7 2.0 %copy.104 = f32[20,64,4]{1,2,0:T(4,128)} copy(f32[20,64,4]{2,1,0:T(8,128)} %get-tuple-element.75) | data formatting | bytes 40960 | tf_op jit(solution)/shard_map/slice | solution.py:23
  19.9 3.5 %collective-permute-start.4 = (f32[128,2,128]{2,1,0:T(2,128)}, f32[128,2,128]{2,1,0:T(2,128)}, u32[]{:S(2)}, u32[]{:S(2)}) collective-permute-start(f32[128,2,128]{2,1,0:T(2,128)} %bitcast.23), channel_id=1, source_target_pairs={{0,128},{1,129},{2,130},{3,131},{4,132},{5,133},{6,134},{7,135},{8... | collective-permute-start | bytes 393224 | tf_op jit(solution)/shard_map/ppermute | solution.py:14
  40.8 1.3 multiply_add_fusion.1
  46.1 1.9 %copy.107 = f32[20,64,4]{2,1,0:T(8,128)} copy(f32[20,64,4]{1,2,0:T(4,128)} %collective-permute-done.1) | data formatting | bytes 40960 | tf_op jit(solution)/shard_map/ppermute | solution.py:19
  48.0 1.9 %copy.106 = f32[20,64,4]{2,1,0:T(8,128)} copy(f32[20,64,4]{1,2,0:T(4,128)} %collective-permute-done) | data formatting | bytes 40960 | tf_op jit(solution)/shard_map/ppermute | solution.py:19
  50.0 1.3 pad_maximum_fusion.9
  51.3 1.3 collective-permute-start.3
  52.6 4.2 %collective-permute-start.2 = (f32[20,4,264]{2,1,0:T(4,128)S(1)}, f32[20,4,264]{2,1,0:T(4,128)S(1)}, u32[]{:S(2)}, u32[]{:S(2)}) collective-permute-start(f32[20,4,264]{2,1,0:T(4,128)S(1)} %get-tuple-element.61), channel_id=1, source_target_pairs={{0,1},{1,2},{2,3},{3,4},{4,5},{5,6},{6,7},{7,8},{8,9},{9,10},{10,1... | collective-permute-start | bytes 253448 | tf_op jit(solution)/shard_map/ppermute | solution.py:14
  58.0 1.7 collective-permute-done.2
  69.8 4.7 %fusion.119 = f32[256,32,128]{2,0,1:T(8,128)} fusion(f32[256,128,1]{1,0,2:T(8,128)} %bitcast.25, f32[32,128,128]{2,1,0:T(8,128)S(1)} %copy-done), kind=kOutput, calls=%fused_computation.273 | convolution fusion | flops 805306368 | bytes 6422528 | tf_op jit(solution)/shard_map/bji,ri->brj/dot_general | solution.py:165
  74.5 5.0 %gather_fusion = f32[1024,128]{1,0:T(8,128)S(1)} fusion(f32[8192,128]{1,0:T(8,128)} %bitcast.173, s32[1024]{0:T(1024)S(1)} %broadcast_clamp_fusion), kind=kCustom, calls=%fused_computation | custom fusion | bytes 1052672 | tf_op jit(solution)/shard_map/gather | solution.py:170
  81.7 1.7 pad_maximum_fusion.2
  83.4 2.0 %copy.119 = f32[128,1,1152]{2,1,0:T(1,128)} copy(f32[128,1,1152]{0,2,1:T(8,128)} %bitcast.178) | data formatting | bytes 1179648 | tf_op jit(solution)/shard_map/all_to_all | solution.py:178
  85.4 17.9 %all-to-all-start = ((f32[128,1,1152]{2,1,0:T(1,128)}), f32[128,1,1152]{2,1,0:T(1,128)}, u32[]{:S(2)}, u32[]{:S(2)}) async-start(f32[128,1,1152]{2,1,0:T(1,128)} %copy.119), calls=%async_computation | async-start | bytes 1179648 | tf_op jit(solution)/shard_map/all_to_all | solution.py:178
  106.4 17.9 %all-to-all-done = f32[128,1,1152]{2,1,0:T(1,128)} async-done(((f32[128,1,1152]{2,1,0:T(1,128)}), f32[128,1,1152]{2,1,0:T(1,128)}, u32[]{:S(2)}, u32[]{:S(2)}) %all-to-all-start) | async-done | bytes 589856 | tf_op jit(solution)/shard_map/all_to_all | solution.py:178
  124.4 1.5 copy.120
  126.7 2.0 %copy.122 = f32[128,8,128]{2,1,0:T(8,128)} copy(f32[128,8,128]{0,2,1:T(8,128)} %slice.560) | data formatting | bytes 1048576 | tf_op jit(solution)/shard_map/slice | solution.py:181
  131.1 1.8 convolution_bitcast_fusion
  136.9 1.6 fusion.17
  138.4 6.8 %all-to-all-start.1 = ((f32[128,8,128]{2,1,0:T(8,128)}), f32[128,8,128]{2,1,0:T(8,128)S(1)}, u32[]{:S(2)}, u32[]{:S(2)}) async-start(f32[128,8,128]{2,1,0:T(8,128)} %fusion.17), calls=%async_computation.1 | async-start | bytes 1048576 | tf_op jit(solution)/shard_map/all_to_all | solution.py:208
  146.7 18.6 %all-to-all-done.1 = f32[128,8,128]{2,1,0:T(8,128)S(1)} async-done(((f32[128,8,128]{2,1,0:T(8,128)}), f32[128,8,128]{2,1,0:T(8,128)S(1)}, u32[]{:S(2)}, u32[]{:S(2)}) %all-to-all-start.1) | async-done | bytes 524320 | tf_op jit(solution)/shard_map/all_to_all | solution.py:208
  166.5 5.7 %fusion.120 = f32[512,32,128]{2,0,1:T(8,128)} fusion(f32[512,128,1]{1,0,2:T(8,128)S(1)} %fusion.3, f32[32,128,128]{2,1,0:T(8,128)S(1)} %copy-done), kind=kOutput, calls=%fused_computation.274 | convolution fusion | flops 1610612736 | bytes 10747904 | tf_op jit(solution)/shard_map/rj,bji->bri/dot_general | solution.py:217
  172.2 4.4 %gather_fusion.1 = f32[512,128]{1,0:T(8,128)S(1)} fusion(f32[16384,128]{1,0:T(8,128)} %bitcast.174, s32[1024]{0:T(1024)S(1)} %pad_clamp_fusion), kind=kCustom, calls=%fused_computation.1 | custom fusion | bytes 526336 | tf_op jit(solution)/shard_map/gather | solution.py:223
  177.0 1.3 collective-permute-start.5
  178.3 5.0 %collective-permute-done.5 = f32[2,64,256]{2,1,0:T(8,128)S(1)} collective-permute-done((f32[2,64,256]{2,1,0:T(8,128)S(1)}, f32[2,64,256]{2,1,0:T(8,128)S(1)}, u32[]{:S(2)}, u32[]{:S(2)}) %collective-permute-start.5) | collective-permute-done | bytes 131104 | tf_op jit(solution)/shard_map/ppermute | solution.py:14
  (203 shorter events, 52.3 us)
Async XLA Ops:
  0.6 69.2 %copy-start = (f32[32,128,128]{2,1,0:T(8,128)S(1)}, f32[32,128,128]{2,1,0:T(8,128)}, u32[]{:S(2)}) copy-start(f32[32,128,128]{2,1,0:T(8,128)} %param.27) | copy-start | bytes 6291460
  0.6 7.6 %copy-start.1 = (f32[1,3,4,64,256]{4,3,2,1,0:T(8,128)S(1)}, f32[1,3,4,64,256]{4,3,2,1,0:T(8,128)}, u32[]{:S(2)}) copy-start(f32[1,3,4,64,256]{4,3,2,1,0:T(8,128)} %param.19) | copy-start | bytes 2359300
  8.2 16.7 %copy-start.29 = (s32[128,2]{0,1:T(2,128)S(1)}, s32[128,2]{0,1:T(2,128)}, u32[]{:S(2)}) copy-start(s32[128,2]{0,1:T(2,128)} %param.24) | copy-start | bytes 3076
  11.5 34.6 %collective-permute-start.1 = (f32[20,64,4]{1,2,0:T(4,128)}, f32[20,64,4]{1,2,0:T(4,128)}, u32[]{:S(2)}, u32[]{:S(2)}) collective-permute-start(f32[20,64,4]{1,2,0:T(4,128)} %copy.105), channel_id=1, source_target_pairs={{0,96},{32,0},{64,32},{96,64},{1,97},{33,1},{65,33},{97,65},{2,98}... | collective-permute-start | bytes 61448 | tf_op jit(solution)/shard_map/ppermute | solution.py:19
  16.6 31.4 %collective-permute-start = (f32[20,64,4]{1,2,0:T(4,128)}, f32[20,64,4]{1,2,0:T(4,128)}, u32[]{:S(2)}, u32[]{:S(2)}) collective-permute-start(f32[20,64,4]{1,2,0:T(4,128)} %copy.104), channel_id=1, source_target_pairs={{0,32},{32,64},{64,96},{96,0},{1,33},{33,65},{65,97},{97,1},{2,34}... | collective-permute-start | bytes 61448 | tf_op jit(solution)/shard_map/ppermute | solution.py:19
  19.9 49.9 %collective-permute-start.4 = (f32[128,2,128]{2,1,0:T(2,128)}, f32[128,2,128]{2,1,0:T(2,128)}, u32[]{:S(2)}, u32[]{:S(2)}) collective-permute-start(f32[128,2,128]{2,1,0:T(2,128)} %bitcast.23), channel_id=1, source_target_pairs={{0,128},{1,129},{2,130},{3,131},{4,132},{5,133},{6,134},{7,135},{8... | collective-permute-start | bytes 393224 | tf_op jit(solution)/shard_map/ppermute | solution.py:14
  50.0 6.8 %copy-start.2 = (f32[20,64,4]{2,1,0:T(8,128)S(1)}, f32[20,64,4]{2,1,0:T(8,128)}, u32[]{:S(2)}) copy-start(f32[20,64,4]{2,1,0:T(8,128)} %copy.106) | copy-start | bytes 61444
  50.0 9.8 %copy-start.5 = (f32[20,64,4]{2,1,0:T(8,128)S(1)}, f32[20,64,4]{2,1,0:T(8,128)}, u32[]{:S(2)}) copy-start(f32[20,64,4]{2,1,0:T(8,128)} %copy.107) | copy-start | bytes 61444
  51.3 6.7 %collective-permute-start.3 = (f32[20,4,264]{2,1,0:T(4,128)S(1)}, f32[20,4,264]{2,1,0:T(4,128)S(1)}, u32[]{:S(2)}, u32[]{:S(2)}) collective-permute-start(f32[20,4,264]{2,1,0:T(4,128)S(1)} %get-tuple-element.62), channel_id=1, source_target_pairs={{1,0},{2,1},{3,2},{4,3},{5,4},{6,5},{7,6},{8,7},{9,8},{10,9},{11,1... | collective-permute-start | bytes 253448 | tf_op jit(solution)/shard_map/ppermute | solution.py:14
  52.6 7.1 %collective-permute-start.2 = (f32[20,4,264]{2,1,0:T(4,128)S(1)}, f32[20,4,264]{2,1,0:T(4,128)S(1)}, u32[]{:S(2)}, u32[]{:S(2)}) collective-permute-start(f32[20,4,264]{2,1,0:T(4,128)S(1)} %get-tuple-element.61), channel_id=1, source_target_pairs={{0,1},{1,2},{2,3},{3,4},{4,5},{5,6},{6,7},{7,8},{8,9},{9,10},{10,1... | collective-permute-start | bytes 253448 | tf_op jit(solution)/shard_map/ppermute | solution.py:14
  80.5 22.9 %copy-start.4 = (f32[4,72,264]{2,1,0:T(8,128)S(1)}, f32[4,72,264]{2,1,0:T(8,128)}, u32[]{:S(2)}) copy-start(f32[4,72,264]{2,1,0:T(8,128)} %copy-done.3) | copy-start | bytes 912388
  85.4 38.9 %all-to-all-start = ((f32[128,1,1152]{2,1,0:T(1,128)}), f32[128,1,1152]{2,1,0:T(1,128)}, u32[]{:S(2)}, u32[]{:S(2)}) async-start(f32[128,1,1152]{2,1,0:T(1,128)} %copy.119), calls=%async_computation | async-start | bytes 1179648 | tf_op jit(solution)/shard_map/all_to_all | solution.py:178
  106.3 22.6 %copy-start.6 = (f32[2,4,64,256]{3,2,1,0:T(8,128)}, f32[2,4,64,256]{3,2,1,0:T(8,128)S(1)}, u32[]{:S(2)}) copy-start(f32[2,4,64,256]{3,2,1,0:T(8,128)S(1)} %pad_subtract_fusion.3) | copy-start | bytes 1572868
  106.3 24.7 %copy-start.23 = (s32[1024]{0:T(1024)S(1)}, s32[1024]{0:T(1024)}, u32[]{:S(2)}) copy-start(s32[1024]{0:T(1024)} %get-tuple-element.116) | copy-start | bytes 12292
  106.3 24.6 %copy-start.24 = (s32[1024]{0:T(1024)S(1)}, s32[1024]{0:T(1024)}, u32[]{:S(2)}) copy-start(s32[1024]{0:T(1024)} %get-tuple-element.117) | copy-start | bytes 12292
  106.4 24.6 %copy-start.25 = (s32[64,2,2]{0,2,1:T(2,128)S(1)}, s32[64,2,2]{0,2,1:T(2,128)}, u32[]{:S(2)}) copy-start(s32[64,2,2]{0,2,1:T(2,128)} %get-tuple-element.122) | copy-start | bytes 3076
  106.4 24.6 %copy-start.26 = (s32[64,2,2]{0,2,1:T(2,128)S(1)}, s32[64,2,2]{0,2,1:T(2,128)}, u32[]{:S(2)}) copy-start(s32[64,2,2]{0,2,1:T(2,128)} %get-tuple-element.123) | copy-start | bytes 3076
  106.4 24.6 %copy-start.27 = (s32[64,2,2]{0,2,1:T(2,128)S(1)}, s32[64,2,2]{0,2,1:T(2,128)}, u32[]{:S(2)}) copy-start(s32[64,2,2]{0,2,1:T(2,128)} %get-tuple-element.120) | copy-start | bytes 3076
  106.4 24.6 %copy-start.28 = (s32[64,2,2]{0,2,1:T(2,128)S(1)}, s32[64,2,2]{0,2,1:T(2,128)}, u32[]{:S(2)}) copy-start(s32[64,2,2]{0,2,1:T(2,128)} %get-tuple-element.121) | copy-start | bytes 3076
  106.4 24.6 %copy-start.31 = (pred[64,2,2]{0,2,1:T(4,128)(4,1)S(1)}, pred[64,2,2]{0,2,1:T(4,128)(4,1)}, u32[]{:S(2)}) copy-start(pred[64,2,2]{0,2,1:T(4,128)(4,1)} %get-tuple-element.118) | copy-start | bytes 772
  129.8 3.4 %copy-start.8 = (f32[2,4,64,256]{3,2,1,0:T(8,128)S(1)}, f32[2,4,64,256]{3,2,1,0:T(8,128)}, u32[]{:S(2)}) copy-start(f32[2,4,64,256]{3,2,1,0:T(8,128)} %copy-done.6) | copy-start | bytes 1572868
  129.8 5.1 %copy-start.7 = (f32[2,4,64,256]{3,2,1,0:T(8,128)S(1)}, f32[2,4,64,256]{3,2,1,0:T(8,128)}, u32[]{:S(2)}) copy-start(f32[2,4,64,256]{3,2,1,0:T(8,128)} %copy-done.6) | copy-start | bytes 1572868
  131.1 4.7 %copy-start.12 = (s32[1,64,256]{2,1,0:T(8,128)S(1)}, s32[1,64,256]{2,1,0:T(8,128)}, u32[]{:S(2)}) copy-start(s32[1,64,256]{2,1,0:T(8,128)} %param.20) | copy-start | bytes 196612
  131.1 4.7 %copy-start.17 = (s32[64,256]{1,0:T(8,128)S(1)}, s32[64,256]{1,0:T(8,128)}, u32[]{:S(2)}) copy-start(s32[64,256]{1,0:T(8,128)} %param.21) | copy-start | bytes 196612
  132.9 3.1 %copy-start.19 = (s32[256]{0:T(256)S(1)}, s32[256]{0:T(256)}, u32[]{:S(2)}) copy-start(s32[256]{0:T(256)} %get-tuple-element.126) | copy-start | bytes 3076
  132.9 3.1 %copy-start.20 = (s32[256]{0:T(256)S(1)}, s32[256]{0:T(256)}, u32[]{:S(2)}) copy-start(s32[256]{0:T(256)} %get-tuple-element.127) | copy-start | bytes 3076
  132.9 3.1 %copy-start.21 = (s32[256]{0:T(256)S(1)}, s32[256]{0:T(256)}, u32[]{:S(2)}) copy-start(s32[256]{0:T(256)} %get-tuple-element.128) | copy-start | bytes 3076
  134.9 10.3 %copy-start.18 = (s32[128,2]{0,1:T(2,128)S(1)}, s32[128,2]{0,1:T(2,128)}, u32[]{:S(2)}) copy-start(s32[128,2]{0,1:T(2,128)} %param.26) | copy-start | bytes 3076
  134.9 10.6 %copy-start.15 = (s32[128,2,2]{2,1,0:T(2,128)S(1)}, s32[128,2,2]{2,1,0:T(2,128)}, u32[]{:S(2)}) copy-start(s32[128,2,2]{2,1,0:T(2,128)} %iota_add_fusion.1) | copy-start | bytes 6148
  136.8 28.4 %copy-start.34 = (pred[1024]{0:T(1024)(128)(4,1)S(1)}, pred[1024]{0:T(1024)(128)(4,1)}, u32[]{:S(2)}) copy-start(pred[1024]{0:T(1024)(128)(4,1)} %fusion.104) | copy-start | bytes 3076
  138.4 26.9 %all-to-all-start.1 = ((f32[128,8,128]{2,1,0:T(8,128)}), f32[128,8,128]{2,1,0:T(8,128)S(1)}, u32[]{:S(2)}, u32[]{:S(2)}) async-start(f32[128,8,128]{2,1,0:T(8,128)} %fusion.17), calls=%async_computation.1 | async-start | bytes 1048576 | tf_op jit(solution)/shard_map/all_to_all | solution.py:208
  177.0 6.3 %collective-permute-start.5 = (f32[2,64,256]{2,1,0:T(8,128)S(1)}, f32[2,64,256]{2,1,0:T(8,128)S(1)}, u32[]{:S(2)}, u32[]{:S(2)}) collective-permute-start(f32[2,64,256]{2,1,0:T(8,128)S(1)} %reshape.651), channel_id=1, source_target_pairs={{128,0},{129,1},{130,2},{131,3},{132,4},{133,5},{134,6},{135,7},{1... | collective-permute-start | bytes 393224 | tf_op jit(solution)/shard_map/ppermute | solution.py:14
  (11 other events, 20.1 us)

commit v4 on v1

--- a/solution.py
+++ b/solution.py
@@ -154,17 +154,16 @@
     surface_flux = jnp.stack([thermal_exchange_rate, evaporation_rate])
     flux_rows = passed_along(to_tiles(surface_flux), "comp", 1).reshape(tile_count * 2, TILE)
     pairs = tile_count * 2
-    me = lax.axis_index("panel") * lax.axis_size("col") + lax.axis_index("col")
 
     bucket_place = bucket_places(partner_devices, owners, capacity)
     place_match = bucket_place[None, :] == jnp.arange(slots, dtype=jnp.int32)[:, None]
     slot_used = jnp.any(place_match, axis=1)
     slot_pair = jnp.sum(jnp.where(place_match, jnp.arange(pairs, dtype=jnp.int32)[None, :], 0), axis=1)
     slot_tile = slot_pair // 2
-    slot_bank = bank_tile_entry.reshape(-1)[slot_pair]
+    slot_bank = jnp.sum(jnp.where(place_match, bank_tile_entry.reshape(-1)[None, :], 0), axis=1)
 
     by_bank = jnp.einsum(
-        "bji,ri->brj", conservative_overlay_factors, flux_rows, precision=HIGHEST
+        "bji,ri->brj", conservative_overlay_factors, flux_rows, precision=lax.Precision.HIGH
     ).reshape(nbank * pairs, TILE)
     f_ids = jnp.arange(2, dtype=jnp.int32)[None, :]
     slot_rows = (slot_bank * pairs + slot_tile * 2)[:, None] + f_ids
@@ -172,9 +171,12 @@
     buffer = jnp.where(slot_used[:, None, None], picked, 0.0).reshape(owners, capacity * 2, TILE)
     received = lax.all_to_all(buffer, ("panel", "col"), 0, 0, tiled=True).reshape(slots * 2, TILE)
 
-    routes = lax.all_gather(
-        jnp.concatenate([partner_devices.T, receiving_tile_index.T], axis=0), ("panel", "col")
-    )
+    me = lax.axis_index("panel") * lax.axis_size("col") + lax.axis_index("col")
+    own_routes = jnp.concatenate([partner_devices.T, receiving_tile_index.T], axis=0)
+    owner_ids = jnp.arange(owners, dtype=jnp.int32)[:, None, None]
+    routes = lax.psum(
+        jnp.where(owner_ids == me, own_routes[None].astype(jnp.float32), 0.0), ("panel", "col")
+    ).astype(jnp.int32)
     mine = [(routes[:, k] == me).astype(jnp.int32) for k in range(2)]
     per_tile = mine[0] + mine[1]
     before = jnp.cumsum(per_tile, axis=1) - per_tile
@@ -220,14 +222,18 @@
     values = jnp.dot(place_hit2, returned, precision=HIGHEST)
 
     by_bank_back = jnp.einsum(
-        "rj,bji->bri", values, conservative_overlay_factors, precision=HIGHEST
+        "rj,bji->bri", values, conservative_overlay_factors, precision=lax.Precision.HIGH
     ).reshape(nbank * pairs * 2, TILE)
     tile_ids = jnp.arange(tile_count, dtype=jnp.int32)[:, None]
     pair_rows = (bank_tile_entry * tile_count + tile_ids) * 4 + jnp.arange(2, dtype=jnp.int32)[None, :] * 2
     back_rows = pair_rows[:, :, None] + f_ids[:, None, :]
     numerator = jnp.sum(by_bank_back[back_rows.reshape(-1)].reshape(tile_count, 2, 2, TILE), axis=1)
     column_sums = jnp.sum(conservative_overlay_factors, axis=1)
-    denominator = column_sums[bank_tile_entry[:, 0]] + column_sums[bank_tile_entry[:, 1]]
+    bank_ids = jnp.arange(nbank, dtype=jnp.int32)[None, :]
+    bank_count = (bank_tile_entry[:, :1] == bank_ids).astype(jnp.float32) + (
+        bank_tile_entry[:, 1:] == bank_ids
+    ).astype(jnp.float32)
+    denominator = jnp.dot(bank_count, column_sums, precision=HIGHEST)
     remap_back = numerator / denominator[:, None, :]
     remapped = passed_along(from_tiles(remap_back, grid_rows, grid_cols), "comp", -1)
     surface_here = jnp.where(on_atmos, remapped, ocean_surface)

time: 522 us -> 1240 us (2.38)
  waiting for transfers between devices: 40.1 us -> 1070 us
  blocking collectives: 263 us -> 0 us
  starting transfers between devices: 97.3 us -> 69 us
  local copies, waits for them, and re-layouts: 52.4 us -> 29.6 us
  between operations: 1.67 us -> 15 us
    psum x0 -> x1, waiting for transfers between devices: none -> 1050 us  [on_device(): lax.psum(jnp.where(owner_ids == me, own_routes[None].astype(jnp.float32),...]
    all_gather x1 -> x0, blocking collectives: 263 us -> none  [on_device(): lax.all_gather(jnp.concatenate([partner_devices.T, receiving_tile_index.T...]
    all_to_all x1, starting transfers between devices: 76.2 us -> 18.1 us  [on_device(): lax.all_to_all(buffer, ('panel', 'col'), 0, 0, tiled=True)]
    all_to_all x1, starting transfers between devices: 6.63 us -> 36.4 us  [on_device(): lax.all_to_all(reply, ('panel', 'col'), 0, 0, tiled=True)]
    all_to_all x1, waiting for transfers between devices: 15.7 us -> 0.01 us  [on_device(): lax.all_to_all(buffer, ('panel', 'col'), 0, 0, tiled=True)]
  transfers between devices with their start and end apart: 8 -> 9, of which waited for: 4 -> 5; matrix products, arithmetic and copies ran while one was open for 14% -> 4% of each run, Pallas kernels for 0% -> 0%
where the time goes in v4:
time: 1240 us
  waiting for transfers between devices  1070 us (86%)
  starting transfers between devices  69 us (6%)
  other arithmetic  38.4 us (3%)
  local copies, waits for them, and re-layouts  29.6 us (2%)
  matrix products  15.6 us (1%)
  between operations  15 us (1%)
    psum x1, waiting for transfers between devices, on_device(): lax.psum(jnp.where(owner_ids == me, own_routes[None].astype(jnp.float32),...  1050 us
    all_to_all x1, starting transfers between devices, on_device(): lax.all_to_all(reply, ('panel', 'col'), 0, 0, tiled=True)  36.4 us
  transfers between devices with their start and end apart: 9, of which 5 were waited for; matrix products, arithmetic and copies ran while one was open for 4% of the time, Pallas kernels for 0%

profile of v4, /device:TPU:1, one launch (start us, length us, event | category | flops | bytes accessed | tf_op | source)
XLA Modules:
  0.0 1241.6 jit_solution(11290199410697722666)
XLA Ops:
  7.2 2.1 copy.125
  10.3 1.5 bitcast_dynamic-update-slice_fusion
  11.8 1.7 fusion.81
  13.5 1.3 broadcast_select_fusion.1
  14.8 1.3 fusion.48
  16.1 2.0 copy.93
  18.1 3.2 collective-permute-start.1
  21.3 2.0 copy.92
  26.5 3.5 collective-permute-start.4
  41.1 1.2 reduce-window.9
  44.8 1.1 add.421
  48.8 1.9 copy.95
  50.7 1.9 copy.94
  52.6 1.3 pad_maximum_fusion.8
  54.0 1.3 collective-permute-start.3
  55.3 4.2 collective-permute-start.2
  59.7 1.5 collective-permute-done.3
  61.1 1.3 collective-permute-done.2
  74.5 5.1 fusion.135
  79.6 5.0 gather_fusion
  85.6 18.1 %all-to-all-start = ((f32[128,8,128]{2,1,0:T(8,128)}), f32[128,8,128]{2,1,0:T(8,128)}, u32[]{:S(2)}, u32[]{:S(2)}) async-start(f32[128,8,128]{2,1,0:T(8,128)} %bitcast_select_fusion), calls=%async_computation | async-start | bytes 1048576 | tf_op jit(solution)/shard_map/all_to_all | solution.py:172
  103.7 1047.6 %all-reduce.14.cloned.1.call-done = f32[128,4,128]{0,2,1:T(8,128)} async-done(((f32[128,4,128]{0,2,1:T(8,128)}), f32[128,4,128]{0,2,1:T(8,128)}) %all-reduce.14.cloned.1.call-update) | async-done | bytes 262160 | tf_op jit(solution)/shard_map/psum | solution.py:177
  1153.3 1.5 fusion.15
  1154.8 1.9 convolution_bitcast_fusion
  1158.1 1.5 fusion.17
  1159.6 36.4 %all-to-all-start.1 = ((f32[128,8,128]{2,1,0:T(8,128)}), f32[128,8,128]{2,1,0:T(8,128)S(1)}, u32[]{:S(2)}, u32[]{:S(2)}) async-start(f32[128,8,128]{2,1,0:T(8,128)} %fusion.17), calls=%async_computation.1 | async-start | bytes 1048576 | tf_op jit(solution)/shard_map/all_to_all | solution.py:215
  1197.5 18.6 %all-to-all-done.1 = f32[128,8,128]{2,1,0:T(8,128)S(1)} async-done(((f32[128,8,128]{2,1,0:T(8,128)}), f32[128,8,128]{2,1,0:T(8,128)S(1)}, u32[]{:S(2)}, u32[]{:S(2)}) %all-to-all-start.1) | async-done | bytes 524320 | tf_op jit(solution)/shard_map/all_to_all | solution.py:215
  1216.1 1.2 fusion.3
  1217.3 5.6 fusion.136
  1222.9 4.4 gather_fusion.1
  1227.8 1.3 collective-permute-start.5
  1229.1 5.0 collective-permute-done.5
  (194 shorter events, 39.2 us)
Async XLA Ops:
  7.2 67.3 %copy-start = (f32[32,128,128]{2,1,0:T(8,128)S(1)}, f32[32,128,128]{2,1,0:T(8,128)}, u32[]{:S(2)}) copy-start(f32[32,128,128]{2,1,0:T(8,128)} %param.27) | copy-start | bytes 6291460
  7.2 7.6 copy-start.1
  7.2 1144.2 %all-reduce.14.cloned.1.call-start = ((), (), s32[]{:S(2)}) async-start(), calls=%async_computation.2 | async-start | bytes 524288 | tf_op jit(solution)/shard_map/psum | solution.py:177
  14.8 15.3 %copy-start.22 = (s32[128,2]{0,1:T(2,128)S(1)}, s32[128,2]{0,1:T(2,128)}, u32[]{:S(2)}) copy-start(s32[128,2]{0,1:T(2,128)} %param.24) | copy-start | bytes 3076
  14.8 15.2 %copy-start.28 = (s32[128,2]{0,1:T(2,128)S(1)}, s32[128,2]{0,1:T(2,128)}, u32[]{:S(2)}) copy-start(s32[128,2]{0,1:T(2,128)} %param.25) | copy-start | bytes 3076
  18.1 25.2 %copy-start.15 = (s32[128,2]{0,1:T(2,128)S(1)}, s32[128,2]{0,1:T(2,128)}, u32[]{:S(2)}) copy-start(s32[128,2]{0,1:T(2,128)} %param.26) | copy-start | bytes 3076
  18.1 30.7 %collective-permute-start.1 = (f32[20,64,4]{1,2,0:T(4,128)}, f32[20,64,4]{1,2,0:T(4,128)}, u32[]{:S(2)}, u32[]{:S(2)}) collective-permute-start(f32[20,64,4]{1,2,0:T(4,128)} %copy.93), channel_id=1, source_target_pairs={{0,96},{32,0},{64,32},{96,64},{1,97},{33,1},{65,33},{97,65},{2,98}... | collective-permute-start | bytes 61448 | tf_op jit(solution)/shard_map/ppermute | solution.py:19
  23.2 27.5 %collective-permute-start = (f32[20,64,4]{1,2,0:T(4,128)}, f32[20,64,4]{1,2,0:T(4,128)}, u32[]{:S(2)}, u32[]{:S(2)}) collective-permute-start(f32[20,64,4]{1,2,0:T(4,128)} %copy.92), channel_id=1, source_target_pairs={{0,32},{32,64},{64,96},{96,0},{1,33},{33,65},{65,97},{97,1},{2,34}... | collective-permute-start | bytes 61448 | tf_op jit(solution)/shard_map/ppermute | solution.py:19
  26.5 47.9 %collective-permute-start.4 = (f32[128,2,128]{2,1,0:T(2,128)}, f32[128,2,128]{2,1,0:T(2,128)}, u32[]{:S(2)}, u32[]{:S(2)}) collective-permute-start(f32[128,2,128]{2,1,0:T(2,128)} %bitcast.33), channel_id=1, source_target_pairs={{0,128},{1,129},{2,130},{3,131},{4,132},{5,133},{6,134},{7,135},{8... | collective-permute-start | bytes 393224 | tf_op jit(solution)/shard_map/ppermute | solution.py:14
  52.6 6.8 copy-start.2
  52.6 9.8 copy-start.3
  54.0 7.1 collective-permute-start.3
  55.3 7.1 collective-permute-start.2
  74.5 5.1 copy-start.4
  84.6 1068.7 %copy-start.18 = (s32[256]{0:T(256)S(1)}, s32[256]{0:T(256)}, u32[]{:S(2)}) copy-start(s32[256]{0:T(256)} %get-tuple-element.138) | copy-start | bytes 3076
  84.6 1068.7 %copy-start.19 = (s32[256]{0:T(256)S(1)}, s32[256]{0:T(256)}, u32[]{:S(2)}) copy-start(s32[256]{0:T(256)} %get-tuple-element.139) | copy-start | bytes 3076
  84.6 1068.7 %copy-start.20 = (s32[256]{0:T(256)S(1)}, s32[256]{0:T(256)}, u32[]{:S(2)}) copy-start(s32[256]{0:T(256)} %get-tuple-element.140) | copy-start | bytes 3076
  84.6 1068.7 %copy-start.21 = (s32[256]{0:T(256)S(1)}, s32[256]{0:T(256)}, u32[]{:S(2)}) copy-start(s32[256]{0:T(256)} %get-tuple-element.141) | copy-start | bytes 3076
  84.6 1070.2 %copy-start.23 = (s32[1024]{0:T(1024)S(1)}, s32[1024]{0:T(1024)}, u32[]{:S(2)}) copy-start(s32[1024]{0:T(1024)} %get-tuple-element.128) | copy-start | bytes 12292
  84.6 1070.2 %copy-start.25 = (s32[1024]{0:T(1024)S(1)}, s32[1024]{0:T(1024)}, u32[]{:S(2)}) copy-start(s32[1024]{0:T(1024)} %get-tuple-element.129) | copy-start | bytes 12292
  84.6 1070.2 %copy-start.27 = (s32[64,2,2]{0,2,1:T(2,128)S(1)}, s32[64,2,2]{0,2,1:T(2,128)}, u32[]{:S(2)}) copy-start(s32[64,2,2]{0,2,1:T(2,128)} %get-tuple-element.134) | copy-start | bytes 3076
  85.6 1069.2 %all-to-all-start = ((f32[128,8,128]{2,1,0:T(8,128)}), f32[128,8,128]{2,1,0:T(8,128)}, u32[]{:S(2)}, u32[]{:S(2)}) async-start(f32[128,8,128]{2,1,0:T(8,128)} %bitcast_select_fusion), calls=%async_computation | async-start | bytes 1048576 | tf_op jit(solution)/shard_map/all_to_all | solution.py:172
  1152.6 4.3 copy-start.6
  1152.6 4.3 copy-start.9
  1153.0 4.0 copy-start.5
  1156.9 39.1 %copy-start.17 = (s32[256]{0:T(256)S(1)}, s32[256]{0:T(256)}, u32[]{:S(2)}) copy-start(s32[256]{0:T(256)} %copy-done.16) | copy-start | bytes 3076
  1157.0 39.2 %copy-start.12 = (s32[128,2,2]{2,1,0:T(2,128)S(1)}, s32[128,2,2]{2,1,0:T(2,128)}, u32[]{:S(2)}) copy-start(s32[128,2,2]{2,1,0:T(2,128)} %iota_add_fusion.1) | copy-start | bytes 6148
  1158.1 58.0 %copy-start.24 = (s32[1024]{0:T(1024)S(1)}, s32[1024]{0:T(1024)}, u32[]{:S(2)}) copy-start(s32[1024]{0:T(1024)} %get-tuple-element.128) | copy-start | bytes 12292
  1158.1 58.0 %copy-start.26 = (s32[1024]{0:T(1024)S(1)}, s32[1024]{0:T(1024)}, u32[]{:S(2)}) copy-start(s32[1024]{0:T(1024)} %get-tuple-element.129) | copy-start | bytes 12292
  1158.1 58.0 %copy-start.29 = (pred[1024]{0:T(1024)(128)(4,1)S(1)}, pred[1024]{0:T(1024)(128)(4,1)}, u32[]{:S(2)}) copy-start(pred[1024]{0:T(1024)(128)(4,1)} %fusion.121) | copy-start | bytes 3076
  1159.6 56.4 %all-to-all-start.1 = ((f32[128,8,128]{2,1,0:T(8,128)}), f32[128,8,128]{2,1,0:T(8,128)S(1)}, u32[]{:S(2)}, u32[]{:S(2)}) async-start(f32[128,8,128]{2,1,0:T(8,128)} %fusion.17), calls=%async_computation.1 | async-start | bytes 1048576 | tf_op jit(solution)/shard_map/all_to_all | solution.py:215
  1227.8 6.3 collective-permute-start.5
  (7 other events, 10.4 us)
Sparse Core Ops, SparseCore 0:
  31.1 1120.2 all-reduce.13

commit v5 on v3

--- a/solution.py
+++ b/solution.py
@@ -20,8 +20,8 @@
 
 
 def wide_halo(array, width):
-    west = from_behind(array[..., -width:], "panel", 1)
-    east = from_behind(array[..., :width], "panel", -1)
+    west = from_behind(array[..., -TILE:], "panel", 1)[..., -width:]
+    east = from_behind(array[..., :TILE], "panel", -1)[..., :width]
     array = jnp.concatenate([west, array, east], axis=-1)
     south = passed_along(array[..., -width:, :], "col", 1)
     north = passed_along(array[..., :width, :], "col", -1)

time: 185 us -> 167 us (0.903)
  waiting for transfers between devices: 43.5 us -> 26.2 us
  starting transfers between devices: 39.2 us -> 48.5 us
  local copies, waits for them, and re-layouts: 41.8 us -> 34.3 us
  other arithmetic: 42.7 us -> 40 us
    all_to_all x1, waiting for transfers between devices: 17.9 us -> 0.01 us  [on_device(): lax.all_to_all(bucket.reshape(owners, rows_out * TILE), ('panel', 'col'),...]
    all_to_all x1, starting transfers between devices: 6.81 us -> 18.8 us  [on_device(): lax.all_to_all(reply, ('panel', 'col'), 0, 0, tiled=True)]
    ppermute x2 -> x0, local copies, waits for them, and re-layouts: 3.85 us -> none  [from_behind(): lax.ppermute(array, axis, [(i, (i + by) % count) for i in range(count)])]
    all_to_all x1, starting transfers between devices: 17.9 us -> 15.2 us  [on_device(): lax.all_to_all(bucket.reshape(owners, rows_out * TILE), ('panel', 'col'),...]
    slice x2 -> x1, local copies, waits for them, and re-layouts: 3.91 us -> 1.32 us  [wide_halo(): west = from_behind(array[..., -TILE:], 'panel', 1)[..., -width:]]
    mul x7, other arithmetic: 0.45 us -> 2.72 us  [vertical_mix(): mixing[-1:] * tracer[:, -1:]]
    unnamed x75 -> x67, local copies, waits for them, and re-layouts: 4.95 us -> 5.01 us
  transfers between devices with their start and end apart: 8 -> 8, of which waited for: 5 -> 4; matrix products, arithmetic and copies ran while one was open for 25% -> 34% of each run, Pallas kernels for 0% -> 0%
where the time goes in v5:
time: 167 us; the launch traced here: 166 us
  starting transfers between devices  48.5 us (29%)
  other arithmetic  40 us (24%)
  local copies, waits for them, and re-layouts  34.3 us (21%)
  waiting for transfers between devices  26.2 us (16%)
  matrix products  15.3 us (9%)
  between operations  1.69 us (1%)
    all_to_all x1, starting transfers between devices, on_device(): lax.all_to_all(reply, ('panel', 'col'), 0, 0, tiled=True)  18.8 us
    all_to_all x1, waiting for transfers between devices, on_device(): lax.all_to_all(reply, ('panel', 'col'), 0, 0, tiled=True)  18.6 us
    all_to_all x1, starting transfers between devices, on_device(): lax.all_to_all(bucket.reshape(owners, rows_out * TILE), ('panel', 'col'),...  15.2 us
    ppermute x4, starting transfers between devices, passed_along(): lax.ppermute(value, axis, [(source, source + steps) for source in range(i...  10.3 us
    ppermute x4, waiting for transfers between devices, passed_along(): lax.ppermute(value, axis, [(source, source + steps) for source in range(i...  7.57 us
    gather x1, local copies, waits for them, and re-layouts, on_device(): picked = by_bank[slot_rows.reshape(-1)].reshape(slots, 2, TILE)  6.22 us
    dot_general x1, matrix products, on_device(): jnp.einsum('rj,bji->bri', values, conservative_overlay_factors, precision...  5.65 us
    unnamed x67, local copies, waits for them, and re-layouts  5.01 us
  transfers between devices with their start and end apart: 8, of which 4 were waited for; matrix products, arithmetic and copies ran while one was open for 34% of the time, Pallas kernels for 0%

profile of v5, /device:TPU:1, one launch (start us, length us, event | category | flops | bytes accessed | tf_op | source)
XLA Modules:
  0.0 166.0 jit_solution(7011838103280573741)
XLA Ops:
  0.7 2.0 %copy.132 = f32[2,4,64,256]{3,2,1,0:T(8,128)} copy(f32[2,4,64,256]{3,2,1,0:T(8,128)} %bitcast.176) | data formatting | bytes 1048576
  2.7 1.0 fusion.84
  3.7 1.5 bitcast_dynamic-update-slice_fusion
  5.2 1.7 %fusion.81 = (f32[2,4,64,256]{3,2,1,0:T(8,128)}, f32[64,256]{1,0:T(8,128)S(1)}) fusion(f32[2,4,64,256]{3,2,1,0:T(8,128)} %bitcast_dynamic-update-slice_fusion, f32[64,256]{1,0:T(8,128)} %param.23, s32[1,64,256]{2,1,0:T(8,128)} %param.20, f32[2,4,64,256]{3,2,1,0:T(8,128)} %bitcast.178, f32[64,256]{1,0:T(8,128)} %param.22, f32[3,4,64,256]{3,2,1,0:T(8,128)} %bitcast.157), kind=kLoop, calls=%fused_computation.182 | loop fusion | flops 212992 | bytes 589824 | tf_op jit(solution)/shard_map/scatter-add | solution.py:152
  6.9 1.3 broadcast_select_fusion.2
  8.2 1.2 fusion.48
  9.5 3.2 %collective-permute-start.1 = (f32[20,64,128]{2,1,0:T(8,128)}, f32[20,64,128]{2,1,0:T(8,128)}, u32[]{:S(2)}, u32[]{:S(2)}) collective-permute-start(f32[20,64,128]{2,1,0:T(8,128)} %get-tuple-element.76), channel_id=1, source_target_pairs={{0,96},{32,0},{64,32},{96,64},{1,97},{33,1},{65,33},{97,65},{2,98}... | collective-permute-start | bytes 1966088 | tf_op jit(solution)/shard_map/ppermute | solution.py:19
  16.0 3.6 %collective-permute-start.4 = (f32[128,2,128]{2,1,0:T(2,128)}, f32[128,2,128]{2,1,0:T(2,128)}, u32[]{:S(2)}, u32[]{:S(2)}) collective-permute-start(f32[128,2,128]{2,1,0:T(2,128)} %bitcast.23), channel_id=1, source_target_pairs={{0,128},{1,129},{2,130},{3,131},{4,132},{5,133},{6,134},{7,135},{8... | collective-permute-start | bytes 393224 | tf_op jit(solution)/shard_map/ppermute | solution.py:14
  33.7 1.1 add.347
  38.2 4.7 %fusion.119 = f32[256,32,128]{2,0,1:T(8,128)} fusion(f32[256,128,1]{1,0,2:T(8,128)} %bitcast.25, f32[32,128,128]{2,1,0:T(8,128)S(1)} %copy-done), kind=kOutput, calls=%fused_computation.273 | convolution fusion | flops 805306368 | bytes 6422528 | tf_op jit(solution)/shard_map/bji,ri->brj/dot_general | solution.py:165
  42.9 6.2 %gather_fusion = f32[1024,128]{1,0:T(8,128)} fusion(f32[8192,128]{1,0:T(8,128)} %bitcast.174, s32[1024]{0:T(1024)S(1)} %broadcast_clamp_fusion), kind=kCustom, calls=%fused_computation | custom fusion | bytes 1052672 | tf_op jit(solution)/shard_map/gather | solution.py:170
  49.1 2.1 %copy.106 = f32[128,8,128]{0,2,1:T(8,128)} copy(f32[128,8,128]{2,1,0:T(8,128)} %bitcast.182) | data formatting | bytes 1048576 | tf_op jit(solution)/shard_map/reshape | solution.py:170
  51.2 1.1 broadcast_select_fusion
  53.1 2.0 %copy.109 = f32[128,1,1152]{2,1,0:T(1,128)} copy(f32[128,1,1152]{0,2,1:T(8,128)} %bitcast.179) | data formatting | bytes 1179648 | tf_op jit(solution)/shard_map/all_to_all | solution.py:178
  55.2 15.2 %all-to-all-start = ((f32[128,1,1152]{2,1,0:T(1,128)}), f32[128,1,1152]{2,1,0:T(1,128)}, u32[]{:S(2)}, u32[]{:S(2)}) async-start(f32[128,1,1152]{2,1,0:T(1,128)} %copy.109), calls=%async_computation | async-start | bytes 1179648 | tf_op jit(solution)/shard_map/all_to_all | solution.py:178
  70.4 1.3 slice.512
  71.7 1.2 pad_maximum_fusion.9
  72.9 1.3 collective-permute-start.3
  74.2 4.2 %collective-permute-start.2 = (f32[20,4,264]{2,1,0:T(4,128)S(1)}, f32[20,4,264]{2,1,0:T(4,128)S(1)}, u32[]{:S(2)}, u32[]{:S(2)}) collective-permute-start(f32[20,4,264]{2,1,0:T(4,128)S(1)} %get-tuple-element.61), channel_id=1, source_target_pairs={{0,1},{1,2},{2,3},{3,4},{4,5},{5,6},{6,7},{7,8},{8,9},{9,10},{10,1... | collective-permute-start | bytes 253448 | tf_op jit(solution)/shard_map/ppermute | solution.py:14
  78.6 2.2 %collective-permute-done.3 = f32[20,4,264]{2,1,0:T(4,128)S(1)} collective-permute-done((f32[20,4,264]{2,1,0:T(4,128)S(1)}, f32[20,4,264]{2,1,0:T(4,128)S(1)}, u32[]{:S(2)}, u32[]{:S(2)}) %collective-permute-start.3) | collective-permute-done | bytes 84512 | tf_op jit(solution)/shard_map/ppermute | solution.py:14
  81.1 2.0 %pad_maximum_fusion = f32[20,72,264]{2,1,0:T(8,128)S(1)} fusion(f32[20,4,264]{2,1,0:T(4,128)S(1)} %collective-permute-done.3, f32[20,64,4]{2,1,0:T(8,128)} %bitcast.153, f32[12,64,256]{2,1,0:T(8,128)S(1)} %bitcast.163, f32[8,64,256]{2,1,0:T(8,128)S(1)} %bitcast.170, f32[20,64,4]{2,1,0:T(8,128)S(1)} %slice.512, f32[20,4,264]{2,1,0:T(4,128)S(1)} %collective-permute-done.2), kind=kLoop, calls=%fused_computation.2 | loop fusion | flops 1900800 | bytes 3041280 | tf_op jit(solution)/shard_map/concatenate | solution.py:28
  97.4 1.7 %copy.110 = f32[128,1,1152]{0,2,1:T(8,128)S(1)} copy(f32[128,1,1152]{2,1,0:T(1,128)} %all-to-all-done) | data formatting | bytes 1179648 | tf_op jit(solution)/shard_map/all_to_all | solution.py:178
  100.0 2.1 %copy.112 = f32[128,8,128]{2,1,0:T(8,128)} copy(f32[128,8,128]{0,2,1:T(8,128)} %slice.570) | data formatting | bytes 1048576 | tf_op jit(solution)/shard_map/slice | solution.py:181
  102.7 1.8 %convolution_bitcast_fusion = f32[2,64,2,128]{3,1,0,2:T(8,128)S(1)} fusion(f32[128,8,128]{2,1,0:T(8,128)} %copy.112, s32[64,2,2]{0,2,1:T(2,128)S(1)} %copy-done.20, s32[64,2,2]{0,2,1:T(2,128)S(1)} %copy-done.21, s32[1024]{0:T(1024)S(1)} %copy-done.18, s32[1024]{0:T(1024)S(1)} %copy-done.19, s32[64,2,2]{0,2,1:T(2,128)S(1)} %copy-done.23, ...), kind=kOutput, calls=%fused_computation.10 | convolution fusion | flops 404226048 | bytes 673280 | tf_op jit(solution)/shard_map/dot_general | solution.py:190
  106.8 1.6 fusion.17
  108.4 18.8 %all-to-all-start.1 = ((f32[128,8,128]{2,1,0:T(8,128)}), f32[128,8,128]{2,1,0:T(8,128)S(1)}, u32[]{:S(2)}, u32[]{:S(2)}) async-start(f32[128,8,128]{2,1,0:T(8,128)} %fusion.17), calls=%async_computation.1 | async-start | bytes 1048576 | tf_op jit(solution)/shard_map/all_to_all | solution.py:208
  128.7 18.6 %all-to-all-done.1 = f32[128,8,128]{2,1,0:T(8,128)S(1)} async-done(((f32[128,8,128]{2,1,0:T(8,128)}), f32[128,8,128]{2,1,0:T(8,128)S(1)}, u32[]{:S(2)}, u32[]{:S(2)}) %all-to-all-start.1) | async-done | bytes 524320 | tf_op jit(solution)/shard_map/all_to_all | solution.py:208
  147.3 1.2 fusion.3
  148.5 5.6 %fusion.120 = f32[512,32,128]{2,0,1:T(8,128)} fusion(f32[512,128,1]{1,0,2:T(8,128)S(1)} %fusion.3, f32[32,128,128]{2,1,0:T(8,128)S(1)} %copy-done), kind=kOutput, calls=%fused_computation.274 | convolution fusion | flops 1610612736 | bytes 10747904 | tf_op jit(solution)/shard_map/rj,bji->bri/dot_general | solution.py:217
  154.1 4.4 %gather_fusion.1 = f32[512,128]{1,0:T(8,128)S(1)} fusion(f32[16384,128]{1,0:T(8,128)} %bitcast.175, s32[1024]{0:T(1024)S(1)} %pad_clamp_fusion), kind=kCustom, calls=%fused_computation.1 | custom fusion | bytes 526336 | tf_op jit(solution)/shard_map/gather | solution.py:223
  159.0 1.3 collective-permute-start.5
  160.3 5.0 %collective-permute-done.5 = f32[2,64,256]{2,1,0:T(8,128)S(1)} collective-permute-done((f32[2,64,256]{2,1,0:T(8,128)S(1)}, f32[2,64,256]{2,1,0:T(8,128)S(1)}, u32[]{:S(2)}, u32[]{:S(2)}) %collective-permute-start.5) | collective-permute-done | bytes 131104 | tf_op jit(solution)/shard_map/ppermute | solution.py:14
  (192 shorter events, 42.0 us)
Async XLA Ops:
  0.6 37.6 %copy-start = (f32[32,128,128]{2,1,0:T(8,128)S(1)}, f32[32,128,128]{2,1,0:T(8,128)}, u32[]{:S(2)}) copy-start(f32[32,128,128]{2,1,0:T(8,128)} %param.27) | copy-start | bytes 6291460
  0.6 7.6 %copy-start.1 = (f32[1,3,4,64,256]{4,3,2,1,0:T(8,128)S(1)}, f32[1,3,4,64,256]{4,3,2,1,0:T(8,128)}, u32[]{:S(2)}) copy-start(f32[1,3,4,64,256]{4,3,2,1,0:T(8,128)} %param.19) | copy-start | bytes 2359300
  8.2 12.8 %copy-start.24 = (s32[128,2]{0,1:T(2,128)S(1)}, s32[128,2]{0,1:T(2,128)}, u32[]{:S(2)}) copy-start(s32[128,2]{0,1:T(2,128)} %param.24) | copy-start | bytes 3076
  8.2 22.0 %copy-start.13 = (s32[128,2]{0,1:T(2,128)S(1)}, s32[128,2]{0,1:T(2,128)}, u32[]{:S(2)}) copy-start(s32[128,2]{0,1:T(2,128)} %param.26) | copy-start | bytes 3076
  9.5 62.3 %collective-permute-start.1 = (f32[20,64,128]{2,1,0:T(8,128)}, f32[20,64,128]{2,1,0:T(8,128)}, u32[]{:S(2)}, u32[]{:S(2)}) collective-permute-start(f32[20,64,128]{2,1,0:T(8,128)} %get-tuple-element.76), channel_id=1, source_target_pairs={{0,96},{32,0},{64,32},{96,64},{1,97},{33,1},{65,33},{97,65},{2,98}... | collective-permute-start | bytes 1966088 | tf_op jit(solution)/shard_map/ppermute | solution.py:19
  12.7 57.7 %collective-permute-start = (f32[20,64,128]{2,1,0:T(8,128)}, f32[20,64,128]{2,1,0:T(8,128)}, u32[]{:S(2)}, u32[]{:S(2)}) collective-permute-start(f32[20,64,128]{2,1,0:T(8,128)} %get-tuple-element.75), channel_id=1, source_target_pairs={{0,32},{32,64},{64,96},{96,0},{1,33},{33,65},{65,97},{97,1},{2,34}... | collective-permute-start | bytes 1966088 | tf_op jit(solution)/shard_map/ppermute | solution.py:19
  16.0 22.2 %collective-permute-start.4 = (f32[128,2,128]{2,1,0:T(2,128)}, f32[128,2,128]{2,1,0:T(2,128)}, u32[]{:S(2)}, u32[]{:S(2)}) collective-permute-start(f32[128,2,128]{2,1,0:T(2,128)} %bitcast.23), channel_id=1, source_target_pairs={{0,128},{1,129},{2,130},{3,131},{4,132},{5,133},{6,134},{7,135},{8... | collective-permute-start | bytes 393224 | tf_op jit(solution)/shard_map/ppermute | solution.py:14
  55.2 42.2 %all-to-all-start = ((f32[128,1,1152]{2,1,0:T(1,128)}), f32[128,1,1152]{2,1,0:T(1,128)}, u32[]{:S(2)}, u32[]{:S(2)}) async-start(f32[128,1,1152]{2,1,0:T(1,128)} %copy.109), calls=%async_computation | async-start | bytes 1179648 | tf_op jit(solution)/shard_map/all_to_all | solution.py:178
  72.9 7.9 %collective-permute-start.3 = (f32[20,4,264]{2,1,0:T(4,128)S(1)}, f32[20,4,264]{2,1,0:T(4,128)S(1)}, u32[]{:S(2)}, u32[]{:S(2)}) collective-permute-start(f32[20,4,264]{2,1,0:T(4,128)S(1)} %get-tuple-element.62), channel_id=1, source_target_pairs={{1,0},{2,1},{3,2},{4,3},{5,4},{6,5},{7,6},{8,7},{9,8},{10,9},{11,1... | collective-permute-start | bytes 253448 | tf_op jit(solution)/shard_map/ppermute | solution.py:14
  74.2 6.9 %collective-permute-start.2 = (f32[20,4,264]{2,1,0:T(4,128)S(1)}, f32[20,4,264]{2,1,0:T(4,128)S(1)}, u32[]{:S(2)}, u32[]{:S(2)}) collective-permute-start(f32[20,4,264]{2,1,0:T(4,128)S(1)} %get-tuple-element.61), channel_id=1, source_target_pairs={{0,1},{1,2},{2,3},{3,4},{4,5},{5,6},{6,7},{7,8},{8,9},{9,10},{10,1... | collective-permute-start | bytes 253448 | tf_op jit(solution)/shard_map/ppermute | solution.py:14
  97.3 5.0 %copy-start.2 = (f32[2,4,64,256]{3,2,1,0:T(8,128)}, f32[2,4,64,256]{3,2,1,0:T(8,128)S(1)}, u32[]{:S(2)}) copy-start(f32[2,4,64,256]{3,2,1,0:T(8,128)S(1)} %pad_subtract_fusion.3) | copy-start | bytes 1572868
  97.3 5.3 %copy-start.18 = (s32[1024]{0:T(1024)S(1)}, s32[1024]{0:T(1024)}, u32[]{:S(2)}) copy-start(s32[1024]{0:T(1024)} %get-tuple-element.116) | copy-start | bytes 12292
  97.3 5.3 %copy-start.19 = (s32[1024]{0:T(1024)S(1)}, s32[1024]{0:T(1024)}, u32[]{:S(2)}) copy-start(s32[1024]{0:T(1024)} %get-tuple-element.117) | copy-start | bytes 12292
  97.3 5.3 %copy-start.20 = (s32[64,2,2]{0,2,1:T(2,128)S(1)}, s32[64,2,2]{0,2,1:T(2,128)}, u32[]{:S(2)}) copy-start(s32[64,2,2]{0,2,1:T(2,128)} %get-tuple-element.122) | copy-start | bytes 3076
  97.3 5.3 %copy-start.21 = (s32[64,2,2]{0,2,1:T(2,128)S(1)}, s32[64,2,2]{0,2,1:T(2,128)}, u32[]{:S(2)}) copy-start(s32[64,2,2]{0,2,1:T(2,128)} %get-tuple-element.123) | copy-start | bytes 3076
  97.3 5.3 %copy-start.22 = (s32[64,2,2]{0,2,1:T(2,128)S(1)}, s32[64,2,2]{0,2,1:T(2,128)}, u32[]{:S(2)}) copy-start(s32[64,2,2]{0,2,1:T(2,128)} %get-tuple-element.120) | copy-start | bytes 3076
  97.3 5.3 %copy-start.23 = (s32[64,2,2]{0,2,1:T(2,128)S(1)}, s32[64,2,2]{0,2,1:T(2,128)}, u32[]{:S(2)}) copy-start(s32[64,2,2]{0,2,1:T(2,128)} %get-tuple-element.121) | copy-start | bytes 3076
  97.4 5.3 %copy-start.26 = (pred[64,2,2]{0,2,1:T(4,128)(4,1)S(1)}, pred[64,2,2]{0,2,1:T(4,128)(4,1)}, u32[]{:S(2)}) copy-start(pred[64,2,2]{0,2,1:T(4,128)(4,1)} %get-tuple-element.118) | copy-start | bytes 772
  97.4 5.3 %copy-start.27 = (pred[64,2,2]{0,2,1:T(4,128)(4,1)S(1)}, pred[64,2,2]{0,2,1:T(4,128)(4,1)}, u32[]{:S(2)}) copy-start(pred[64,2,2]{0,2,1:T(4,128)(4,1)} %get-tuple-element.119) | copy-start | bytes 772
  97.4 5.3 %copy-start.30 = (pred[1024]{0:T(1024)(128)(4,1)S(1)}, pred[1024]{0:T(1024)(128)(4,1)}, u32[]{:S(2)}) copy-start(pred[1024]{0:T(1024)(128)(4,1)} %fusion.104) | copy-start | bytes 3076
  100.0 4.8 %copy-start.7 = (s32[1,64,256]{2,1,0:T(8,128)S(1)}, s32[1,64,256]{2,1,0:T(8,128)}, u32[]{:S(2)}) copy-start(s32[1,64,256]{2,1,0:T(8,128)} %param.20) | copy-start | bytes 196612
  102.4 2.4 %copy-start.4 = (f32[2,4,64,256]{3,2,1,0:T(8,128)S(1)}, f32[2,4,64,256]{3,2,1,0:T(8,128)}, u32[]{:S(2)}) copy-start(f32[2,4,64,256]{3,2,1,0:T(8,128)} %copy-done.2) | copy-start | bytes 1572868
  102.4 2.4 %copy-start.3 = (f32[2,4,64,256]{3,2,1,0:T(8,128)S(1)}, f32[2,4,64,256]{3,2,1,0:T(8,128)}, u32[]{:S(2)}) copy-start(f32[2,4,64,256]{3,2,1,0:T(8,128)} %copy-done.2) | copy-start | bytes 1572868
  102.7 3.1 %copy-start.12 = (s32[64,256]{1,0:T(8,128)S(1)}, s32[64,256]{1,0:T(8,128)}, u32[]{:S(2)}) copy-start(s32[64,256]{1,0:T(8,128)} %param.21) | copy-start | bytes 196612
  104.5 1.4 copy-start.14
  104.5 1.4 copy-start.15
  104.6 1.4 copy-start.16
  104.6 1.4 copy-start.17
  104.6 1.4 copy-start.25
  104.8 22.6 %copy-start.10 = (s32[128,2,2]{2,1,0:T(2,128)S(1)}, s32[128,2,2]{2,1,0:T(2,128)}, u32[]{:S(2)}) copy-start(s32[128,2,2]{2,1,0:T(2,128)} %iota_add_fusion.1) | copy-start | bytes 6148
  108.4 38.9 %all-to-all-start.1 = ((f32[128,8,128]{2,1,0:T(8,128)}), f32[128,8,128]{2,1,0:T(8,128)S(1)}, u32[]{:S(2)}, u32[]{:S(2)}) async-start(f32[128,8,128]{2,1,0:T(8,128)} %fusion.17), calls=%async_computation.1 | async-start | bytes 1048576 | tf_op jit(solution)/shard_map/all_to_all | solution.py:208
  159.0 6.3 %collective-permute-start.5 = (f32[2,64,256]{2,1,0:T(8,128)S(1)}, f32[2,64,256]{2,1,0:T(8,128)S(1)}, u32[]{:S(2)}, u32[]{:S(2)}) collective-permute-start(f32[2,64,256]{2,1,0:T(8,128)S(1)} %reshape.651), channel_id=1, source_target_pairs={{128,0},{129,1},{130,2},{131,3},{132,4},{133,5},{134,6},{135,7},{1... | collective-permute-start | bytes 393224 | tf_op jit(solution)/shard_map/ppermute | solution.py:14
  (7 other events, 7.5 us)

commit v6 on v5

--- a/solution.py
+++ b/solution.py
@@ -157,18 +157,21 @@
 
     bucket_place = bucket_places(partner_devices, owners, capacity)
     place_match = bucket_place[None, :] == jnp.arange(slots, dtype=jnp.int32)[:, None]
-    slot_used = jnp.any(place_match, axis=1)
-    slot_pair = jnp.sum(jnp.where(place_match, jnp.arange(pairs, dtype=jnp.int32)[None, :], 0), axis=1)
-    slot_tile = slot_pair // 2
-    slot_bank = jnp.sum(jnp.where(place_match, bank_tile_entry.reshape(-1)[None, :], 0), axis=1)
+    place_rep = jnp.broadcast_to(bucket_place[:, None], (pairs, 2)).reshape(-1)
+    p_rows = lax.broadcasted_iota(jnp.int32, (pairs * 2, slots * 2), 0)
+    p_cols = lax.broadcasted_iota(jnp.int32, (pairs * 2, slots * 2), 1)
+    place_hit2 = ((place_rep[:, None] == p_cols // 2) & (p_cols % 2 == p_rows % 2)).astype(
+        jnp.float32
+    )
 
     by_bank = jnp.einsum(
         "bji,ri->brj", conservative_overlay_factors, flux_rows, precision=lax.Precision.HIGH
     ).reshape(nbank * pairs, TILE)
     f_ids = jnp.arange(2, dtype=jnp.int32)[None, :]
-    slot_rows = (slot_bank * pairs + slot_tile * 2)[:, None] + f_ids
-    picked = by_bank[slot_rows.reshape(-1)].reshape(slots, 2, TILE)
-    buffer = jnp.where(slot_used[:, None, None], picked, 0.0).reshape(owners, capacity * 2, TILE)
+    tile_ids = jnp.arange(tile_count, dtype=jnp.int32)[:, None]
+    spread_rows = (bank_tile_entry * pairs + tile_ids * 2)[:, :, None] + f_ids[:, None, :]
+    contrib = by_bank[spread_rows.reshape(-1)]
+    buffer = jnp.dot(place_hit2.T, contrib, precision=HIGHEST).reshape(owners, capacity * 2, TILE)
     slot_label = jnp.sum(jnp.where(place_match, receiving_tile_index.reshape(-1)[None, :], 0), axis=1)
     label_row = jnp.pad(
         slot_label.reshape(owners, capacity).astype(jnp.float32), ((0, 0), (0, TILE - capacity))
@@ -206,18 +209,11 @@
     ocean_tiles = to_tiles(ocean_surface).reshape(pairs, TILE)
     reply = jnp.dot(slot_hit2.T, ocean_tiles, precision=HIGHEST).reshape(owners, capacity * 2, TILE)
     returned = lax.all_to_all(reply, ("panel", "col"), 0, 0, tiled=True).reshape(slots * 2, TILE)
-    place_rep = jnp.broadcast_to(bucket_place[:, None], (pairs, 2)).reshape(-1)
-    p_rows = lax.broadcasted_iota(jnp.int32, (pairs * 2, slots * 2), 0)
-    p_cols = lax.broadcasted_iota(jnp.int32, (pairs * 2, slots * 2), 1)
-    place_hit2 = ((place_rep[:, None] == p_cols // 2) & (p_cols % 2 == p_rows % 2)).astype(
-        jnp.float32
-    )
     values = jnp.dot(place_hit2, returned, precision=HIGHEST)
 
     by_bank_back = jnp.einsum(
         "rj,bji->bri", values, conservative_overlay_factors, precision=lax.Precision.HIGH
     ).reshape(nbank * pairs * 2, TILE)
-    tile_ids = jnp.arange(tile_count, dtype=jnp.int32)[:, None]
     pair_rows = (bank_tile_entry * tile_count + tile_ids) * 4 + jnp.arange(2, dtype=jnp.int32)[None, :] * 2
     back_rows = pair_rows[:, :, None] + f_ids[:, None, :]
     numerator = jnp.sum(by_bank_back[back_rows.reshape(-1)].reshape(tile_count, 2, 2, TILE), axis=1)

time: 167 us -> 173 us (1.036)
  matrix products: 15.3 us -> 19.1 us
    dot_general x0 -> x1, matrix products: none -> 3.88 us  [on_device(): jnp.dot(place_hit2.T, contrib, precision=HIGHEST)]
    gather x1, local copies, waits for them, and re-layouts: 6.22 us -> 3.84 us  [on_device(): contrib = by_bank[spread_rows.reshape(-1)]]
    broadcast_in_dim x2, local copies, waits for them, and re-layouts: 0.09 us -> 2.19 us  [on_device(): bucket = jnp.concatenate([buffer, label_row[:, None, :]], axis=1)]
    unnamed x67 -> x82, local copies, waits for them, and re-layouts: 5.01 us -> 4.69 us
  transfers between devices with their start and end apart: 8 -> 8, of which waited for: 4 -> 4; matrix products, arithmetic and copies ran while one was open for 34% -> 36% of each run, Pallas kernels for 0% -> 0%
where the time goes in v6:
time: 173 us; the launch traced here: 171 us
  starting transfers between devices  48.6 us (28%)
  other arithmetic  41.5 us (24%)
  local copies, waits for them, and re-layouts  34.2 us (20%)
  waiting for transfers between devices  26.1 us (15%)
  matrix products  19.1 us (11%)
    all_to_all x1, starting transfers between devices, on_device(): lax.all_to_all(reply, ('panel', 'col'), 0, 0, tiled=True)  19 us
    all_to_all x1, waiting for transfers between devices, on_device(): lax.all_to_all(reply, ('panel', 'col'), 0, 0, tiled=True)  18.6 us
    all_to_all x1, starting transfers between devices, on_device(): lax.all_to_all(bucket.reshape(owners, rows_out * TILE), ('panel', 'col'),...  15.2 us
    ppermute x4, starting transfers between devices, passed_along(): lax.ppermute(value, axis, [(source, source + steps) for source in range(i...  10.3 us
    ppermute x4, waiting for transfers between devices, passed_along(): lax.ppermute(value, axis, [(source, source + steps) for source in range(i...  7.57 us
    dot_general x1, matrix products, on_device(): jnp.einsum('rj,bji->bri', values, conservative_overlay_factors, precision...  5.65 us
    unnamed x82, local copies, waits for them, and re-layouts  4.69 us
    dot_general x1, matrix products, on_device(): jnp.einsum('bji,ri->brj', conservative_overlay_factors, flux_rows, precis...  4.68 us
  transfers between devices with their start and end apart: 8, of which 4 were waited for; matrix products, arithmetic and copies ran while one was open for 36% of the time, Pallas kernels for 0%

profile of v6, /device:TPU:1, one launch (start us, length us, event | category | flops | bytes accessed | tf_op | source)
XLA Modules:
  0.0 171.3 jit_solution(1655973421669710946)
XLA Ops:
  0.7 2.0 %copy.129 = f32[2,4,64,256]{3,2,1,0:T(8,128)} copy(f32[2,4,64,256]{3,2,1,0:T(8,128)} %bitcast.176) | data formatting | bytes 1048576
  3.7 1.5 bitcast_dynamic-update-slice_fusion
  5.2 1.7 fusion.65
  6.9 1.3 broadcast_select_fusion.1
  8.2 1.2 fusion.33
  9.5 3.2 %collective-permute-start.1 = (f32[20,64,128]{2,1,0:T(8,128)}, f32[20,64,128]{2,1,0:T(8,128)}, u32[]{:S(2)}, u32[]{:S(2)}) collective-permute-start(f32[20,64,128]{2,1,0:T(8,128)} %get-tuple-element.73), channel_id=1, source_target_pairs={{0,96},{32,0},{64,32},{96,64},{1,97},{33,1},{65,33},{97,65},{2,98}... | collective-permute-start | bytes 1966088 | tf_op jit(solution)/shard_map/ppermute | solution.py:19
  16.0 3.6 %collective-permute-start.4 = (f32[128,2,128]{2,1,0:T(2,128)}, f32[128,2,128]{2,1,0:T(2,128)}, u32[]{:S(2)}, u32[]{:S(2)}) collective-permute-start(f32[128,2,128]{2,1,0:T(2,128)} %bitcast.23), channel_id=1, source_target_pairs={{0,128},{1,129},{2,130},{3,131},{4,132},{5,133},{6,134},{7,135},{8... | collective-permute-start | bytes 393224 | tf_op jit(solution)/shard_map/ppermute | solution.py:14
  34.5 1.3 multiply_add_fusion.1
  39.1 1.6 copy.105
  41.5 4.7 %fusion.101 = f32[256,32,128]{2,0,1:T(8,128)} fusion(f32[256,128,1]{1,0,2:T(8,128)} %bitcast.25, f32[32,128,128]{2,1,0:T(8,128)S(1)} %copy-done), kind=kOutput, calls=%fused_computation.252 | convolution fusion | flops 805306368 | bytes 6422528 | tf_op jit(solution)/shard_map/bji,ri->brj/dot_general | solution.py:167
  46.2 3.8 %gather_fusion = f32[512,128]{1,0:T(8,128)} fusion(f32[8192,128]{1,0:T(8,128)} %bitcast.175, s32[1024]{0:T(1024)S(1)} %pad_clamp_fusion.1), kind=kCustom, calls=%fused_computation | custom fusion | bytes 526336 | tf_op jit(solution)/shard_map/gather | solution.py:173
  50.2 3.9 %convolution_bitcast_fusion = f32[128,8,128]{2,1,0:T(8,128)} fusion(f32[512,128]{1,0:T(8,128)} %gather_fusion, s32[512]{0:T(512)S(1)} %copy-done.22, s32[512]{0:T(512)S(1)} %copy-done.23, s32[1024]{0:T(1024)S(1)} %copy-done.17, s32[1024]{0:T(1024)S(1)} %copy-done.18, s32[1024]{0:T(1024)S(1)} %copy-done.16, s32[1024]{0:T(1024)S(1)} %copy-done.19, ...), kind=kOutput, calls=%fused_computation.8 | convolution fusion | flops 808452096 | bytes 811520 | tf_op jit(solution)/shard_map/dot_general | solution.py:174
  54.0 2.0 %copy.104 = f32[128,8,128]{0,2,1:T(8,128)} copy(f32[128,8,128]{2,1,0:T(8,128)} %convolution_bitcast_fusion) | data formatting | bytes 1048576 | tf_op jit(solution)/shard_map/reshape | solution.py:174
  56.1 1.9 %pad_maximum_fusion.2 = f32[128,9,128]{0,2,1:T(8,128)} fusion(f32[128,1,128]{0,2,1:T(8,128)S(1)} %copy-done.11, f32[128,8,128]{0,2,1:T(8,128)} %copy.104), kind=kLoop, calls=%fused_computation.66 | loop fusion | flops 147456 | bytes 1179648 | tf_op jit(solution)/shard_map/concatenate | solution.py:179
  58.0 2.1 %copy.106 = f32[128,1,1152]{2,1,0:T(1,128)} copy(f32[128,1,1152]{0,2,1:T(8,128)} %bitcast.179) | data formatting | bytes 1179648 | tf_op jit(solution)/shard_map/all_to_all | solution.py:181
  60.1 15.2 %all-to-all-start = ((f32[128,1,1152]{2,1,0:T(1,128)}), f32[128,1,1152]{2,1,0:T(1,128)}, u32[]{:S(2)}, u32[]{:S(2)}) async-start(f32[128,1,1152]{2,1,0:T(1,128)} %copy.106), calls=%async_computation | async-start | bytes 1179648 | tf_op jit(solution)/shard_map/all_to_all | solution.py:181
  75.3 1.3 slice.512
  77.8 1.3 collective-permute-start.3
  79.1 4.2 %collective-permute-start.2 = (f32[20,4,264]{2,1,0:T(4,128)S(1)}, f32[20,4,264]{2,1,0:T(4,128)S(1)}, u32[]{:S(2)}, u32[]{:S(2)}) collective-permute-start(f32[20,4,264]{2,1,0:T(4,128)S(1)} %get-tuple-element.58), channel_id=1, source_target_pairs={{0,1},{1,2},{2,3},{3,4},{4,5},{5,6},{6,7},{7,8},{8,9},{9,10},{10,1... | collective-permute-start | bytes 253448 | tf_op jit(solution)/shard_map/ppermute | solution.py:14
  83.5 2.2 %collective-permute-done.3 = f32[20,4,264]{2,1,0:T(4,128)S(1)} collective-permute-done((f32[20,4,264]{2,1,0:T(4,128)S(1)}, f32[20,4,264]{2,1,0:T(4,128)S(1)}, u32[]{:S(2)}, u32[]{:S(2)}) %collective-permute-start.3) | collective-permute-done | bytes 84512 | tf_op jit(solution)/shard_map/ppermute | solution.py:14
  86.0 2.0 %pad_maximum_fusion = f32[20,72,264]{2,1,0:T(8,128)S(1)} fusion(f32[20,4,264]{2,1,0:T(4,128)S(1)} %collective-permute-done.3, f32[20,64,4]{2,1,0:T(8,128)} %bitcast.153, f32[12,64,256]{2,1,0:T(8,128)S(1)} %bitcast.163, f32[8,64,256]{2,1,0:T(8,128)S(1)} %bitcast.170, f32[20,64,4]{2,1,0:T(8,128)S(1)} %slice.512, f32[20,4,264]{2,1,0:T(4,128)S(1)} %collective-permute-done.2), kind=kLoop, calls=%fused_computation.2 | loop fusion | flops 1900800 | bytes 3041280 | tf_op jit(solution)/shard_map/concatenate | solution.py:28
  102.7 1.7 copy.107
  105.3 2.0 %copy.109 = f32[128,8,128]{2,1,0:T(8,128)} copy(f32[128,8,128]{0,2,1:T(8,128)} %slice.570) | data formatting | bytes 1048576 | tf_op jit(solution)/shard_map/slice | solution.py:184
  107.9 1.8 %convolution_bitcast_fusion.2 = f32[2,64,2,128]{3,1,0,2:T(8,128)S(1)} fusion(f32[128,8,128]{2,1,0:T(8,128)} %copy.109, s32[64,2,2]{0,2,1:T(2,128)S(1)} %copy-done.24, s32[64,2,2]{0,2,1:T(2,128)S(1)} %copy-done.25, s32[1024]{0:T(1024)S(1)} %copy-done.17, s32[1024]{0:T(1024)S(1)} %copy-done.18, s32[64,2,2]{0,2,1:T(2,128)S(1)} %copy-done.27, ...), kind=kOutput, calls=%fused_computation.10 | convolution fusion | flops 404226048 | bytes 673280 | tf_op jit(solution)/shard_map/dot_general | solution.py:193
  112.0 1.6 fusion.4
  113.5 19.0 %all-to-all-start.1 = ((f32[128,8,128]{2,1,0:T(8,128)}), f32[128,8,128]{2,1,0:T(8,128)S(1)}, u32[]{:S(2)}, u32[]{:S(2)}) async-start(f32[128,8,128]{2,1,0:T(8,128)} %fusion.4), calls=%async_computation.1 | async-start | bytes 1048576 | tf_op jit(solution)/shard_map/all_to_all | solution.py:211
  134.0 18.6 %all-to-all-done.1 = f32[128,8,128]{2,1,0:T(8,128)S(1)} async-done(((f32[128,8,128]{2,1,0:T(8,128)}), f32[128,8,128]{2,1,0:T(8,128)S(1)}, u32[]{:S(2)}, u32[]{:S(2)}) %all-to-all-start.1) | async-done | bytes 524320 | tf_op jit(solution)/shard_map/all_to_all | solution.py:211
  152.6 1.2 convolution_bitcast_fusion.1
  153.8 5.6 %fusion.102 = f32[512,32,128]{2,0,1:T(8,128)} fusion(f32[512,128,1]{1,0,2:T(8,128)S(1)} %convolution_bitcast_fusion.1, f32[32,128,128]{2,1,0:T(8,128)S(1)} %copy-done), kind=kOutput, calls=%fused_computation.253 | convolution fusion | flops 1610612736 | bytes 10747904 | tf_op jit(solution)/shard_map/rj,bji->bri/dot_general | solution.py:214
  159.4 4.4 %gather_fusion.1 = f32[512,128]{1,0:T(8,128)S(1)} fusion(f32[16384,128]{1,0:T(8,128)} %bitcast.174, s32[1024]{0:T(1024)S(1)} %pad_clamp_fusion), kind=kCustom, calls=%fused_computation.1 | custom fusion | bytes 526336 | tf_op jit(solution)/shard_map/gather | solution.py:219
  164.3 1.3 collective-permute-start.5
  165.6 5.0 %collective-permute-done.5 = f32[2,64,256]{2,1,0:T(8,128)S(1)} collective-permute-done((f32[2,64,256]{2,1,0:T(8,128)S(1)}, f32[2,64,256]{2,1,0:T(8,128)S(1)}, u32[]{:S(2)}, u32[]{:S(2)}) %collective-permute-start.5) | collective-permute-done | bytes 131104 | tf_op jit(solution)/shard_map/ppermute | solution.py:14
  (201 shorter events, 45.5 us)
Async XLA Ops:
  0.6 40.9 %copy-start = (f32[32,128,128]{2,1,0:T(8,128)S(1)}, f32[32,128,128]{2,1,0:T(8,128)}, u32[]{:S(2)}) copy-start(f32[32,128,128]{2,1,0:T(8,128)} %param.27) | copy-start | bytes 6291460
  0.6 7.6 %copy-start.1 = (f32[1,3,4,64,256]{4,3,2,1,0:T(8,128)S(1)}, f32[1,3,4,64,256]{4,3,2,1,0:T(8,128)}, u32[]{:S(2)}) copy-start(f32[1,3,4,64,256]{4,3,2,1,0:T(8,128)} %param.19) | copy-start | bytes 2359300
  8.2 12.8 %copy-start.28 = (s32[128,2]{0,1:T(2,128)S(1)}, s32[128,2]{0,1:T(2,128)}, u32[]{:S(2)}) copy-start(s32[128,2]{0,1:T(2,128)} %param.24) | copy-start | bytes 3076
  8.2 20.5 %copy-start.29 = (s32[128,2]{0,1:T(2,128)S(1)}, s32[128,2]{0,1:T(2,128)}, u32[]{:S(2)}) copy-start(s32[128,2]{0,1:T(2,128)} %param.25) | copy-start | bytes 3076
  9.5 67.1 %collective-permute-start.1 = (f32[20,64,128]{2,1,0:T(8,128)}, f32[20,64,128]{2,1,0:T(8,128)}, u32[]{:S(2)}, u32[]{:S(2)}) collective-permute-start(f32[20,64,128]{2,1,0:T(8,128)} %get-tuple-element.73), channel_id=1, source_target_pairs={{0,96},{32,0},{64,32},{96,64},{1,97},{33,1},{65,33},{97,65},{2,98}... | collective-permute-start | bytes 1966088 | tf_op jit(solution)/shard_map/ppermute | solution.py:19
  12.7 62.6 %collective-permute-start = (f32[20,64,128]{2,1,0:T(8,128)}, f32[20,64,128]{2,1,0:T(8,128)}, u32[]{:S(2)}, u32[]{:S(2)}) collective-permute-start(f32[20,64,128]{2,1,0:T(8,128)} %get-tuple-element.72), channel_id=1, source_target_pairs={{0,32},{32,64},{64,96},{96,0},{1,33},{33,65},{65,97},{97,1},{2,34}... | collective-permute-start | bytes 1966088 | tf_op jit(solution)/shard_map/ppermute | solution.py:19
  16.0 25.5 %collective-permute-start.4 = (f32[128,2,128]{2,1,0:T(2,128)}, f32[128,2,128]{2,1,0:T(2,128)}, u32[]{:S(2)}, u32[]{:S(2)}) collective-permute-start(f32[128,2,128]{2,1,0:T(2,128)} %bitcast.23), channel_id=1, source_target_pairs={{0,128},{1,129},{2,130},{3,131},{4,132},{5,133},{6,134},{7,135},{8... | collective-permute-start | bytes 393224 | tf_op jit(solution)/shard_map/ppermute | solution.py:14
  46.2 3.9 %copy-start.16 = (s32[1024]{0:T(1024)S(1)}, s32[1024]{0:T(1024)}, u32[]{:S(2)}) copy-start(s32[1024]{0:T(1024)} %get-tuple-element.115) | copy-start | bytes 12292
  46.2 3.9 %copy-start.17 = (s32[1024]{0:T(1024)S(1)}, s32[1024]{0:T(1024)}, u32[]{:S(2)}) copy-start(s32[1024]{0:T(1024)} %get-tuple-element.116) | copy-start | bytes 12292
  46.2 3.9 %copy-start.18 = (s32[1024]{0:T(1024)S(1)}, s32[1024]{0:T(1024)}, u32[]{:S(2)}) copy-start(s32[1024]{0:T(1024)} %get-tuple-element.117) | copy-start | bytes 12292
  46.2 3.9 %copy-start.19 = (s32[1024]{0:T(1024)S(1)}, s32[1024]{0:T(1024)}, u32[]{:S(2)}) copy-start(s32[1024]{0:T(1024)} %get-tuple-element.118) | copy-start | bytes 12292
  46.2 3.9 %copy-start.21 = (s32[512]{0:T(512)S(1)}, s32[512]{0:T(512)}, u32[]{:S(2)}) copy-start(s32[512]{0:T(512)} %eq.139) | copy-start | bytes 6148
  46.2 3.9 %copy-start.22 = (s32[512]{0:T(512)S(1)}, s32[512]{0:T(512)}, u32[]{:S(2)}) copy-start(s32[512]{0:T(512)} %get-tuple-element.121) | copy-start | bytes 6148
  46.2 3.9 %copy-start.23 = (s32[512]{0:T(512)S(1)}, s32[512]{0:T(512)}, u32[]{:S(2)}) copy-start(s32[512]{0:T(512)} %get-tuple-element.122) | copy-start | bytes 6148
  46.2 3.9 %copy-start.31 = (pred[1024]{0:T(1024)(128)(4,1)S(1)}, pred[1024]{0:T(1024)(128)(4,1)}, u32[]{:S(2)}) copy-start(pred[1024]{0:T(1024)(128)(4,1)} %get-tuple-element.119) | copy-start | bytes 3076
  46.2 3.9 %copy-start.32 = (pred[1024]{0:T(1024)(128)(4,1)S(1)}, pred[1024]{0:T(1024)(128)(4,1)}, u32[]{:S(2)}) copy-start(pred[1024]{0:T(1024)(128)(4,1)} %get-tuple-element.120) | copy-start | bytes 3076
  46.2 3.9 %copy-start.37 = (pred[512]{0:T(512)(128)(4,1)S(1)}, pred[512]{0:T(512)(128)(4,1)}, u32[]{:S(2)}) copy-start(pred[512]{0:T(512)(128)(4,1)} %fusion.93) | copy-start | bytes 1540
  50.2 5.9 %copy-start.11 = (f32[128,1,128]{0,2,1:T(8,128)S(1)}, f32[128,1,128]{0,2,1:T(8,128)}, u32[]{:S(2)}) copy-start(f32[128,1,128]{0,2,1:T(8,128)} %copy.105) | copy-start | bytes 196612
  60.1 42.6 %all-to-all-start = ((f32[128,1,1152]{2,1,0:T(1,128)}), f32[128,1,1152]{2,1,0:T(1,128)}, u32[]{:S(2)}, u32[]{:S(2)}) async-start(f32[128,1,1152]{2,1,0:T(1,128)} %copy.106), calls=%async_computation | async-start | bytes 1179648 | tf_op jit(solution)/shard_map/all_to_all | solution.py:181
  77.8 7.9 %collective-permute-start.3 = (f32[20,4,264]{2,1,0:T(4,128)S(1)}, f32[20,4,264]{2,1,0:T(4,128)S(1)}, u32[]{:S(2)}, u32[]{:S(2)}) collective-permute-start(f32[20,4,264]{2,1,0:T(4,128)S(1)} %get-tuple-element.59), channel_id=1, source_target_pairs={{1,0},{2,1},{3,2},{4,3},{5,4},{6,5},{7,6},{8,7},{9,8},{10,9},{11,1... | collective-permute-start | bytes 253448 | tf_op jit(solution)/shard_map/ppermute | solution.py:14
  79.1 6.9 %collective-permute-start.2 = (f32[20,4,264]{2,1,0:T(4,128)S(1)}, f32[20,4,264]{2,1,0:T(4,128)S(1)}, u32[]{:S(2)}, u32[]{:S(2)}) collective-permute-start(f32[20,4,264]{2,1,0:T(4,128)S(1)} %get-tuple-element.58), channel_id=1, source_target_pairs={{0,1},{1,2},{2,3},{3,4},{4,5},{5,6},{6,7},{7,8},{8,9},{9,10},{10,1... | collective-permute-start | bytes 253448 | tf_op jit(solution)/shard_map/ppermute | solution.py:14
  102.6 4.7 %copy-start.2 = (f32[2,4,64,256]{3,2,1,0:T(8,128)}, f32[2,4,64,256]{3,2,1,0:T(8,128)S(1)}, u32[]{:S(2)}) copy-start(f32[2,4,64,256]{3,2,1,0:T(8,128)S(1)} %pad_subtract_fusion.3) | copy-start | bytes 1572868
  102.6 5.2 %copy-start.24 = (s32[64,2,2]{0,2,1:T(2,128)S(1)}, s32[64,2,2]{0,2,1:T(2,128)}, u32[]{:S(2)}) copy-start(s32[64,2,2]{0,2,1:T(2,128)} %get-tuple-element.127) | copy-start | bytes 3076
  102.6 5.2 %copy-start.25 = (s32[64,2,2]{0,2,1:T(2,128)S(1)}, s32[64,2,2]{0,2,1:T(2,128)}, u32[]{:S(2)}) copy-start(s32[64,2,2]{0,2,1:T(2,128)} %get-tuple-element.128) | copy-start | bytes 3076
  102.6 5.2 %copy-start.26 = (s32[64,2,2]{0,2,1:T(2,128)S(1)}, s32[64,2,2]{0,2,1:T(2,128)}, u32[]{:S(2)}) copy-start(s32[64,2,2]{0,2,1:T(2,128)} %get-tuple-element.125) | copy-start | bytes 3076
  102.7 5.2 %copy-start.27 = (s32[64,2,2]{0,2,1:T(2,128)S(1)}, s32[64,2,2]{0,2,1:T(2,128)}, u32[]{:S(2)}) copy-start(s32[64,2,2]{0,2,1:T(2,128)} %get-tuple-element.126) | copy-start | bytes 3076
  102.7 5.2 %copy-start.33 = (pred[64,2,2]{0,2,1:T(4,128)(4,1)S(1)}, pred[64,2,2]{0,2,1:T(4,128)(4,1)}, u32[]{:S(2)}) copy-start(pred[64,2,2]{0,2,1:T(4,128)(4,1)} %get-tuple-element.123) | copy-start | bytes 772
  110.0 22.5 %copy-start.15 = (s32[128,2]{0,1:T(2,128)S(1)}, s32[128,2]{0,1:T(2,128)}, u32[]{:S(2)}) copy-start(s32[128,2]{0,1:T(2,128)} %get-tuple-element.98) | copy-start | bytes 3076
  111.9 21.2 %copy-start.20 = (s32[128,2]{0,1:T(2,128)S(1)}, s32[128,2]{0,1:T(2,128)}, u32[]{:S(2)}) copy-start(s32[128,2]{0,1:T(2,128)} %param.26) | copy-start | bytes 3076
  113.5 39.1 %copy-start.38 = (pred[512]{0:T(512)(128)(4,1)S(1)}, pred[512]{0:T(512)(128)(4,1)}, u32[]{:S(2)}) copy-start(pred[512]{0:T(512)(128)(4,1)} %fusion.93) | copy-start | bytes 1540
  113.5 39.0 %all-to-all-start.1 = ((f32[128,8,128]{2,1,0:T(8,128)}), f32[128,8,128]{2,1,0:T(8,128)S(1)}, u32[]{:S(2)}, u32[]{:S(2)}) async-start(f32[128,8,128]{2,1,0:T(8,128)} %fusion.4), calls=%async_computation.1 | async-start | bytes 1048576 | tf_op jit(solution)/shard_map/all_to_all | solution.py:211
  164.3 6.3 %collective-permute-start.5 = (f32[2,64,256]{2,1,0:T(8,128)S(1)}, f32[2,64,256]{2,1,0:T(8,128)S(1)}, u32[]{:S(2)}, u32[]{:S(2)}) collective-permute-start(f32[2,64,256]{2,1,0:T(8,128)S(1)} %reshape.627), channel_id=1, source_target_pairs={{128,0},{129,1},{130,2},{131,3},{132,4},{133,5},{134,6},{135,7},{1... | collective-permute-start | bytes 393224 | tf_op jit(solution)/shard_map/ppermute | solution.py:14
  (15 other events, 23.1 us)

commit v7 on v5

--- a/solution.py
+++ b/solution.py
@@ -20,12 +20,12 @@
 
 
 def wide_halo(array, width):
+    south = passed_along(array[..., -8:, :], "col", 1)[..., -width:, :]
+    north = passed_along(array[..., :8, :], "col", -1)[..., :width, :]
+    array = jnp.concatenate([south, array, north], axis=-2)
     west = from_behind(array[..., -TILE:], "panel", 1)[..., -width:]
     east = from_behind(array[..., :TILE], "panel", -1)[..., :width]
-    array = jnp.concatenate([west, array, east], axis=-1)
-    south = passed_along(array[..., -width:, :], "col", 1)
-    north = passed_along(array[..., :width, :], "col", -1)
-    return jnp.concatenate([south, array, north], axis=-2)
+    return jnp.concatenate([west, array, east], axis=-1)
 
 
 def vertical_mix(tracer, mixing):

time: 167 us -> 167 us (level)
  starting transfers between devices: 48.5 us -> 42.7 us
  local copies, waits for them, and re-layouts: 34.3 us -> 39.6 us
    all_to_all x1, starting transfers between devices: 18.8 us -> 11.3 us  [on_device(): lax.all_to_all(reply, ('panel', 'col'), 0, 0, tiled=True)]
    all_to_all x1, waiting for transfers between devices: 0.01 us -> 2.71 us  [on_device(): lax.all_to_all(bucket.reshape(owners, rows_out * TILE), ('panel', 'col'),...]
    ppermute x4, waiting for transfers between devices: 7.57 us -> 5.02 us  [passed_along(): lax.ppermute(value, axis, [(source, source + steps) for source in range(i...]
    slice x0 -> x2, local copies, waits for them, and re-layouts: none -> 1.86 us  [the longest x1 0.94 us: wide_halo(): south = passed_along(array[..., -8:, :], 'col', 1)[..., -width:, :]]
    unnamed x67 -> x83, local copies, waits for them, and re-layouts: 5.01 us -> 5.03 us
  transfers between devices with their start and end apart: 8 -> 8, of which waited for: 4 -> 3; matrix products, arithmetic and copies ran while one was open for 34% -> 38% of each run, Pallas kernels for 0% -> 0%
where the time goes in v7:
time: 167 us; the launch traced here: 165 us
  starting transfers between devices  42.7 us (26%)
  local copies, waits for them, and re-layouts  39.6 us (24%)
  other arithmetic  39.5 us (24%)
  waiting for transfers between devices  26.3 us (16%)
  matrix products  15.3 us (9%)
  between operations  1.75 us (1%)
    all_to_all x1, waiting for transfers between devices, on_device(): lax.all_to_all(reply, ('panel', 'col'), 0, 0, tiled=True)  18.6 us
    all_to_all x1, starting transfers between devices, on_device(): lax.all_to_all(bucket.reshape(owners, rows_out * TILE), ('panel', 'col'),...  15.9 us
    ppermute x4, starting transfers between devices, passed_along(): lax.ppermute(value, axis, [(source, source + steps) for source in range(i...  11.7 us
    all_to_all x1, starting transfers between devices, on_device(): lax.all_to_all(reply, ('panel', 'col'), 0, 0, tiled=True)  11.3 us
    gather x1, local copies, waits for them, and re-layouts, on_device(): picked = by_bank[slot_rows.reshape(-1)].reshape(slots, 2, TILE)  6.54 us
    dot_general x1, matrix products, on_device(): jnp.einsum('rj,bji->bri', values, conservative_overlay_factors, precision...  5.68 us
    unnamed x83, local copies, waits for them, and re-layouts  5.03 us
    ppermute x4, waiting for transfers between devices, passed_along(): lax.ppermute(value, axis, [(source, source + steps) for source in range(i...  5.02 us
  transfers between devices with their start and end apart: 8, of which 3 were waited for; matrix products, arithmetic and copies ran while one was open for 38% of the time, Pallas kernels for 0%

profile of v7, /device:TPU:1, one launch (start us, length us, event | category | flops | bytes accessed | tf_op | source)
XLA Modules:
  0.0 165.1 jit_solution(9795101656161251492)
XLA Ops:
  0.7 2.0 %copy.132 = f32[2,4,64,256]{3,2,1,0:T(8,128)} copy(f32[2,4,64,256]{3,2,1,0:T(8,128)} %bitcast.178) | data formatting | bytes 1048576
  2.7 1.0 fusion.83
  3.7 1.5 bitcast_dynamic-update-slice_fusion
  5.2 1.7 %fusion.80 = (f32[2,4,64,256]{3,2,1,0:T(8,128)}, f32[64,256]{1,0:T(8,128)S(1)}) fusion(f32[2,4,64,256]{3,2,1,0:T(8,128)} %bitcast_dynamic-update-slice_fusion, f32[64,256]{1,0:T(8,128)} %param.23, s32[1,64,256]{2,1,0:T(8,128)} %param.20, f32[2,4,64,256]{3,2,1,0:T(8,128)} %bitcast.180, f32[64,256]{1,0:T(8,128)} %param.22, f32[3,4,64,256]{3,2,1,0:T(8,128)} %bitcast.157), kind=kLoop, calls=%fused_computation.180 | loop fusion | flops 212992 | bytes 589824 | tf_op jit(solution)/shard_map/scatter-add | solution.py:152
  6.9 1.3 broadcast_select_fusion.2
  9.0 1.3 collective-permute-start.1
  10.3 5.3 %collective-permute-start = (f32[20,8,256]{2,1,0:T(8,128)}, f32[20,8,256]{2,1,0:T(8,128)}, u32[]{:S(2)}, u32[]{:S(2)}) collective-permute-start(f32[20,8,256]{2,1,0:T(8,128)} %get-tuple-element.75), channel_id=1, source_target_pairs={{0,1},{1,2},{2,3},{3,4},{4,5},{5,6},{6,7},{7,8},{8,9},{9,10},{10,1... | collective-permute-start | bytes 491528 | tf_op jit(solution)/shard_map/ppermute | solution.py:14
  18.0 3.8 %collective-permute-start.4 = (f32[128,2,128]{2,1,0:T(2,128)}, f32[128,2,128]{2,1,0:T(2,128)}, u32[]{:S(2)}, u32[]{:S(2)}) collective-permute-start(f32[128,2,128]{2,1,0:T(2,128)} %bitcast.23), channel_id=1, source_target_pairs={{0,128},{1,129},{2,130},{3,131},{4,132},{5,133},{6,134},{7,135},{8... | collective-permute-start | bytes 393224 | tf_op jit(solution)/shard_map/ppermute | solution.py:14
  35.3 1.1 add.347
  45.1 1.2 fusion.117
  46.3 1.5 collective-permute-start.3
  47.8 2.3 %collective-permute-start.2 = (f32[20,72,128]{2,1,0:T(8,128)}, f32[20,72,128]{2,1,0:T(8,128)}, u32[]{:S(2)}, u32[]{:S(2)}) collective-permute-start(f32[20,72,128]{2,1,0:T(8,128)} %get-tuple-element.73), channel_id=1, source_target_pairs={{0,32},{32,64},{64,96},{96,0},{1,33},{33,65},{65,97},{97,1},{2,34}... | collective-permute-start | bytes 2211848 | tf_op jit(solution)/shard_map/ppermute | solution.py:19
  50.2 4.7 %fusion.119 = f32[256,32,128]{2,0,1:T(8,128)} fusion(f32[256,128,1]{1,0,2:T(8,128)} %bitcast.25, f32[32,128,128]{2,1,0:T(8,128)S(1)} %copy-done), kind=kOutput, calls=%fused_computation.272 | convolution fusion | flops 805306368 | bytes 6422528 | tf_op jit(solution)/shard_map/bji,ri->brj/dot_general | solution.py:165
  54.9 6.5 %gather_fusion = f32[1024,128]{1,0:T(8,128)} fusion(f32[8192,128]{1,0:T(8,128)} %bitcast.176, s32[1024]{0:T(1024)} %broadcast_clamp_fusion), kind=kCustom, calls=%fused_computation | custom fusion | bytes 1052672 | tf_op jit(solution)/shard_map/gather | solution.py:170
  61.4 2.0 %copy.106 = f32[128,8,128]{0,2,1:T(8,128)} copy(f32[128,8,128]{2,1,0:T(8,128)} %bitcast.184) | data formatting | bytes 1048576 | tf_op jit(solution)/shard_map/reshape | solution.py:170
  63.4 1.1 broadcast_select_fusion
  65.4 2.0 %copy.109 = f32[128,1,1152]{2,1,0:T(1,128)} copy(f32[128,1,1152]{0,2,1:T(8,128)} %bitcast.181) | data formatting | bytes 1179648 | tf_op jit(solution)/shard_map/all_to_all | solution.py:178
  67.4 15.9 %all-to-all-start = ((f32[128,1,1152]{2,1,0:T(1,128)}), f32[128,1,1152]{2,1,0:T(1,128)}, u32[]{:S(2)}, u32[]{:S(2)}) async-start(f32[128,1,1152]{2,1,0:T(1,128)} %copy.109), calls=%async_computation | async-start | bytes 1179648 | tf_op jit(solution)/shard_map/all_to_all | solution.py:178
  83.3 1.4 slice.521
  84.7 2.2 %pad_maximum_fusion = f32[20,72,264]{2,1,0:T(8,128)S(1)} fusion(f32[20,72,4]{2,1,0:T(8,128)} %bitcast.153, f32[20,4,256]{2,1,0:T(4,128)S(1)} %slice.519, f32[12,64,256]{2,1,0:T(8,128)S(1)} %bitcast.162, f32[8,64,256]{2,1,0:T(8,128)S(1)} %bitcast.170, f32[20,4,256]{2,1,0:T(4,128)} %copy-done.2, f32[20,72,4]{2,1,0:T(8,128)S(1)} %slice.521), kind=kLoop, calls=%fused_computation.2 | loop fusion | flops 1900800 | bytes 3041280 | tf_op jit(solution)/shard_map/concatenate | solution.py:28
  101.6 2.7 %all-to-all-done = f32[128,1,1152]{2,1,0:T(1,128)} async-done(((f32[128,1,1152]{2,1,0:T(1,128)}), f32[128,1,1152]{2,1,0:T(1,128)}, u32[]{:S(2)}, u32[]{:S(2)}) %all-to-all-start) | async-done | bytes 589856 | tf_op jit(solution)/shard_map/all_to_all | solution.py:178
  104.3 1.5 copy.110
  106.7 2.0 %copy.112 = f32[128,8,128]{2,1,0:T(8,128)} copy(f32[128,8,128]{0,2,1:T(8,128)} %slice.579) | data formatting | bytes 1048576 | tf_op jit(solution)/shard_map/slice | solution.py:181
  109.3 1.8 %convolution_bitcast_fusion = f32[2,64,2,128]{3,1,0,2:T(8,128)S(1)} fusion(f32[128,8,128]{2,1,0:T(8,128)} %copy.112, s32[64,2,2]{0,2,1:T(2,128)S(1)} %copy-done.27, s32[64,2,2]{0,2,1:T(2,128)S(1)} %copy-done.28, s32[1024]{0:T(1024)S(1)} %copy-done.25, s32[1024]{0:T(1024)S(1)} %copy-done.26, s32[64,2,2]{0,2,1:T(2,128)S(1)} %copy-done.30, ...), kind=kOutput, calls=%fused_computation.9 | convolution fusion | flops 404226048 | bytes 673280 | tf_op jit(solution)/shard_map/dot_general | solution.py:190
  113.5 1.5 fusion.17
  115.0 11.3 %all-to-all-start.1 = ((f32[128,8,128]{2,1,0:T(8,128)}), f32[128,8,128]{2,1,0:T(8,128)S(1)}, u32[]{:S(2)}, u32[]{:S(2)}) async-start(f32[128,8,128]{2,1,0:T(8,128)} %fusion.17), calls=%async_computation.1 | async-start | bytes 1048576 | tf_op jit(solution)/shard_map/all_to_all | solution.py:208
  127.8 18.6 %all-to-all-done.1 = f32[128,8,128]{2,1,0:T(8,128)S(1)} async-done(((f32[128,8,128]{2,1,0:T(8,128)}), f32[128,8,128]{2,1,0:T(8,128)S(1)}, u32[]{:S(2)}, u32[]{:S(2)}) %all-to-all-start.1) | async-done | bytes 524320 | tf_op jit(solution)/shard_map/all_to_all | solution.py:208
  146.4 1.2 fusion.3
  147.6 5.7 %fusion.120 = f32[512,32,128]{2,0,1:T(8,128)} fusion(f32[512,128,1]{1,0,2:T(8,128)S(1)} %fusion.3, f32[32,128,128]{2,1,0:T(8,128)S(1)} %copy-done), kind=kOutput, calls=%fused_computation.273 | convolution fusion | flops 1610612736 | bytes 10747904 | tf_op jit(solution)/shard_map/rj,bji->bri/dot_general | solution.py:217
  153.3 4.4 %gather_fusion.1 = f32[512,128]{1,0:T(8,128)S(1)} fusion(f32[16384,128]{1,0:T(8,128)} %bitcast.177, s32[1024]{0:T(1024)S(1)} %pad_clamp_fusion), kind=kCustom, calls=%fused_computation.1 | custom fusion | bytes 526336 | tf_op jit(solution)/shard_map/gather | solution.py:223
  158.2 1.3 collective-permute-start.5
  159.5 5.0 %collective-permute-done.5 = f32[2,64,256]{2,1,0:T(8,128)S(1)} collective-permute-done((f32[2,64,256]{2,1,0:T(8,128)S(1)}, f32[2,64,256]{2,1,0:T(8,128)S(1)}, u32[]{:S(2)}, u32[]{:S(2)}) %collective-permute-start.5) | collective-permute-done | bytes 131104 | tf_op jit(solution)/shard_map/ppermute | solution.py:14
  (213 shorter events, 46.4 us)
Async XLA Ops:
  0.6 49.5 %copy-start = (f32[32,128,128]{2,1,0:T(8,128)S(1)}, f32[32,128,128]{2,1,0:T(8,128)}, u32[]{:S(2)}) copy-start(f32[32,128,128]{2,1,0:T(8,128)} %param.27) | copy-start | bytes 6291460
  0.6 7.6 %copy-start.1 = (f32[1,3,4,64,256]{4,3,2,1,0:T(8,128)S(1)}, f32[1,3,4,64,256]{4,3,2,1,0:T(8,128)}, u32[]{:S(2)}) copy-start(f32[1,3,4,64,256]{4,3,2,1,0:T(8,128)} %param.19) | copy-start | bytes 2359300
  6.9 16.3 %copy-start.31 = (s32[128,2]{0,1:T(2,128)S(1)}, s32[128,2]{0,1:T(2,128)}, u32[]{:S(2)}) copy-start(s32[128,2]{0,1:T(2,128)} %param.24) | copy-start | bytes 3076
  8.2 24.1 %copy-start.19 = (s32[128,2]{0,1:T(2,128)S(1)}, s32[128,2]{0,1:T(2,128)}, u32[]{:S(2)}) copy-start(s32[128,2]{0,1:T(2,128)} %param.26) | copy-start | bytes 3076
  9.0 34.0 %collective-permute-start.1 = (f32[20,8,256]{2,1,0:T(8,128)}, f32[20,8,256]{2,1,0:T(8,128)}, u32[]{:S(2)}, u32[]{:S(2)}) collective-permute-start(f32[20,8,256]{2,1,0:T(8,128)} %get-tuple-element.76), channel_id=1, source_target_pairs={{1,0},{2,1},{3,2},{4,3},{5,4},{6,5},{7,6},{8,7},{9,8},{10,9},{11,1... | collective-permute-start | bytes 491528 | tf_op jit(solution)/shard_map/ppermute | solution.py:14
  10.3 33.7 %collective-permute-start = (f32[20,8,256]{2,1,0:T(8,128)}, f32[20,8,256]{2,1,0:T(8,128)}, u32[]{:S(2)}, u32[]{:S(2)}) collective-permute-start(f32[20,8,256]{2,1,0:T(8,128)} %get-tuple-element.75), channel_id=1, source_target_pairs={{0,1},{1,2},{2,3},{3,4},{4,5},{5,6},{6,7},{7,8},{8,9},{9,10},{10,1... | collective-permute-start | bytes 491528 | tf_op jit(solution)/shard_map/ppermute | solution.py:14
  18.0 32.2 %collective-permute-start.4 = (f32[128,2,128]{2,1,0:T(2,128)}, f32[128,2,128]{2,1,0:T(2,128)}, u32[]{:S(2)}, u32[]{:S(2)}) collective-permute-start(f32[128,2,128]{2,1,0:T(2,128)} %bitcast.23), channel_id=1, source_target_pairs={{0,128},{1,129},{2,130},{3,131},{4,132},{5,133},{6,134},{7,135},{8... | collective-permute-start | bytes 393224 | tf_op jit(solution)/shard_map/ppermute | solution.py:14
  31.4 11.6 %copy-start.17 = (s32[256]{0:T(256)}, s32[256]{0:T(256)S(1)}, u32[]{:S(2)}) copy-start(s32[256]{0:T(256)S(1)} %multiply_add_fusion.2) | copy-start | bytes 3076
  46.3 38.4 %collective-permute-start.3 = (f32[20,72,128]{2,1,0:T(8,128)}, f32[20,72,128]{2,1,0:T(8,128)}, u32[]{:S(2)}, u32[]{:S(2)}) collective-permute-start(f32[20,72,128]{2,1,0:T(8,128)} %get-tuple-element.74), channel_id=1, source_target_pairs={{0,96},{32,0},{64,32},{96,64},{1,97},{33,1},{65,33},{97,65},{2,98}... | collective-permute-start | bytes 2211848 | tf_op jit(solution)/shard_map/ppermute | solution.py:19
  47.8 35.5 %collective-permute-start.2 = (f32[20,72,128]{2,1,0:T(8,128)}, f32[20,72,128]{2,1,0:T(8,128)}, u32[]{:S(2)}, u32[]{:S(2)}) collective-permute-start(f32[20,72,128]{2,1,0:T(8,128)} %get-tuple-element.73), channel_id=1, source_target_pairs={{0,32},{32,64},{64,96},{96,0},{1,33},{33,65},{65,97},{97,1},{2,34}... | collective-permute-start | bytes 2211848 | tf_op jit(solution)/shard_map/ppermute | solution.py:19
  67.4 36.9 %all-to-all-start = ((f32[128,1,1152]{2,1,0:T(1,128)}), f32[128,1,1152]{2,1,0:T(1,128)}, u32[]{:S(2)}, u32[]{:S(2)}) async-start(f32[128,1,1152]{2,1,0:T(1,128)} %copy.109), calls=%async_computation | async-start | bytes 1179648 | tf_op jit(solution)/shard_map/all_to_all | solution.py:178
  84.7 2.2 %copy-start.3 = (f32[20,4,256]{2,1,0:T(4,128)S(1)}, f32[20,4,256]{2,1,0:T(4,128)}, u32[]{:S(2)}) copy-start(f32[20,4,256]{2,1,0:T(4,128)} %copy-done.2) | copy-start | bytes 245764
  101.5 7.2 %copy-start.4 = (f32[2,4,64,256]{3,2,1,0:T(8,128)}, f32[2,4,64,256]{3,2,1,0:T(8,128)S(1)}, u32[]{:S(2)}) copy-start(f32[2,4,64,256]{3,2,1,0:T(8,128)S(1)} %pad_subtract_fusion.3) | copy-start | bytes 1572868
  101.5 7.7 %copy-start.25 = (s32[1024]{0:T(1024)S(1)}, s32[1024]{0:T(1024)}, u32[]{:S(2)}) copy-start(s32[1024]{0:T(1024)} %get-tuple-element.114) | copy-start | bytes 12292
  101.5 7.7 %copy-start.26 = (s32[1024]{0:T(1024)S(1)}, s32[1024]{0:T(1024)}, u32[]{:S(2)}) copy-start(s32[1024]{0:T(1024)} %get-tuple-element.115) | copy-start | bytes 12292
  101.5 7.7 %copy-start.27 = (s32[64,2,2]{0,2,1:T(2,128)S(1)}, s32[64,2,2]{0,2,1:T(2,128)}, u32[]{:S(2)}) copy-start(s32[64,2,2]{0,2,1:T(2,128)} %get-tuple-element.120) | copy-start | bytes 3076
  101.6 7.7 %copy-start.28 = (s32[64,2,2]{0,2,1:T(2,128)S(1)}, s32[64,2,2]{0,2,1:T(2,128)}, u32[]{:S(2)}) copy-start(s32[64,2,2]{0,2,1:T(2,128)} %get-tuple-element.121) | copy-start | bytes 3076
  101.6 7.7 %copy-start.29 = (s32[64,2,2]{0,2,1:T(2,128)S(1)}, s32[64,2,2]{0,2,1:T(2,128)}, u32[]{:S(2)}) copy-start(s32[64,2,2]{0,2,1:T(2,128)} %get-tuple-element.118) | copy-start | bytes 3076
  101.6 7.7 %copy-start.30 = (s32[64,2,2]{0,2,1:T(2,128)S(1)}, s32[64,2,2]{0,2,1:T(2,128)}, u32[]{:S(2)}) copy-start(s32[64,2,2]{0,2,1:T(2,128)} %get-tuple-element.119) | copy-start | bytes 3076
  101.6 7.7 %copy-start.33 = (pred[64,2,2]{0,2,1:T(4,128)(4,1)S(1)}, pred[64,2,2]{0,2,1:T(4,128)(4,1)}, u32[]{:S(2)}) copy-start(pred[64,2,2]{0,2,1:T(4,128)(4,1)} %get-tuple-element.116) | copy-start | bytes 772
  101.6 7.7 %copy-start.34 = (pred[64,2,2]{0,2,1:T(4,128)(4,1)S(1)}, pred[64,2,2]{0,2,1:T(4,128)(4,1)}, u32[]{:S(2)}) copy-start(pred[64,2,2]{0,2,1:T(4,128)(4,1)} %get-tuple-element.117) | copy-start | bytes 772
  101.6 7.7 %copy-start.38 = (pred[1024]{0:T(1024)(128)(4,1)S(1)}, pred[1024]{0:T(1024)(128)(4,1)}, u32[]{:S(2)}) copy-start(pred[1024]{0:T(1024)(128)(4,1)} %fusion.103) | copy-start | bytes 3076
  108.7 2.7 %copy-start.9 = (s32[1,64,256]{2,1,0:T(8,128)S(1)}, s32[1,64,256]{2,1,0:T(8,128)}, u32[]{:S(2)}) copy-start(s32[1,64,256]{2,1,0:T(8,128)} %param.20) | copy-start | bytes 196612
  108.7 2.7 %copy-start.6 = (f32[2,4,64,256]{3,2,1,0:T(8,128)S(1)}, f32[2,4,64,256]{3,2,1,0:T(8,128)}, u32[]{:S(2)}) copy-start(f32[2,4,64,256]{3,2,1,0:T(8,128)} %copy-done.4) | copy-start | bytes 1572868
  108.9 2.6 %copy-start.5 = (f32[2,4,64,256]{3,2,1,0:T(8,128)S(1)}, f32[2,4,64,256]{3,2,1,0:T(8,128)}, u32[]{:S(2)}) copy-start(f32[2,4,64,256]{3,2,1,0:T(8,128)} %copy-done.4) | copy-start | bytes 1572868
  109.3 3.1 %copy-start.14 = (s32[64,256]{1,0:T(8,128)S(1)}, s32[64,256]{1,0:T(8,128)}, u32[]{:S(2)}) copy-start(s32[64,256]{1,0:T(8,128)} %param.21) | copy-start | bytes 196612
  111.2 1.5 copy-start.15
  111.5 14.8 %copy-start.20 = (s32[128,2]{0,1:T(2,128)S(1)}, s32[128,2]{0,1:T(2,128)}, u32[]{:S(2)}) copy-start(s32[128,2]{0,1:T(2,128)} %param.26) | copy-start | bytes 3076
  111.5 14.9 %copy-start.18 = (s32[256]{0:T(256)S(1)}, s32[256]{0:T(256)}, u32[]{:S(2)}) copy-start(s32[256]{0:T(256)} %copy-done.17) | copy-start | bytes 3076
  111.6 15.0 %copy-start.12 = (s32[128,2,2]{2,1,0:T(2,128)S(1)}, s32[128,2,2]{2,1,0:T(2,128)}, u32[]{:S(2)}) copy-start(s32[128,2,2]{2,1,0:T(2,128)} %iota_add_fusion.1) | copy-start | bytes 6148
  115.0 31.4 %all-to-all-start.1 = ((f32[128,8,128]{2,1,0:T(8,128)}), f32[128,8,128]{2,1,0:T(8,128)S(1)}, u32[]{:S(2)}, u32[]{:S(2)}) async-start(f32[128,8,128]{2,1,0:T(8,128)} %fusion.17), calls=%async_computation.1 | async-start | bytes 1048576 | tf_op jit(solution)/shard_map/all_to_all | solution.py:208
  158.2 6.3 %collective-permute-start.5 = (f32[2,64,256]{2,1,0:T(8,128)S(1)}, f32[2,64,256]{2,1,0:T(8,128)S(1)}, u32[]{:S(2)}, u32[]{:S(2)}) collective-permute-start(f32[2,64,256]{2,1,0:T(8,128)S(1)} %reshape.651), channel_id=1, source_target_pairs={{128,0},{129,1},{130,2},{131,3},{132,4},{133,5},{134,6},{135,7},{1... | collective-permute-start | bytes 393224 | tf_op jit(solution)/shard_map/ppermute | solution.py:14
  (15 other events, 18.9 us)

commit v8 on v7

--- a/solution.py
+++ b/solution.py
@@ -149,8 +149,14 @@
         * (jnp.exp(0.1 * prior_oceanic_warmth) - device_tracer_share[1, 0])
         * unfrozen_share
     )
-    heated = device_tracer_share.at[0, 0].add(thermal_exchange_rate).at[1, 0].add(evaporation_rate)
-    start = jnp.where(on_atmos, heated, device_tracer_share)
+    start = jnp.concatenate(
+        [
+            (device_tracer_share[0, 0] + jnp.where(on_atmos, thermal_exchange_rate, 0.0))[None],
+            device_tracer_share[0, 1:],
+            (device_tracer_share[1, 0] + jnp.where(on_atmos, evaporation_rate, 0.0))[None],
+            device_tracer_share[1, 1:],
+        ]
+    ).reshape(device_tracer_share.shape)
     surface_flux = jnp.stack([thermal_exchange_rate, evaporation_rate])
     flux_rows = passed_along(to_tiles(surface_flux), "comp", 1).reshape(tile_count * 2, TILE)
     pairs = tile_count * 2

time: 167 us -> 167 us (level)
  local copies, waits for them, and re-layouts: 39.6 us -> 42.6 us
  other arithmetic: 39.5 us -> 36.6 us
    scatter-add x2 -> x0, other arithmetic: 3.19 us -> none  [on_device(): device_tracer_share.at[0, 0].add(thermal_exchange_rate).at[1, 0]]
    unnamed x0 -> x2, other arithmetic: none -> 2.28 us
    unnamed x83 -> x84, local copies, waits for them, and re-layouts: 5.03 us -> 4.91 us
  transfers between devices with their start and end apart: 8 -> 8, of which waited for: 3 -> 3; matrix products, arithmetic and copies ran while one was open for 38% -> 40% of each run, Pallas kernels for 0% -> 0%
where the time goes in v8:
time: 167 us; the launch traced here: 166 us
  starting transfers between devices  42.9 us (26%)
  local copies, waits for them, and re-layouts  42.6 us (26%)
  other arithmetic  36.6 us (22%)
  waiting for transfers between devices  26.5 us (16%)
  matrix products  15.3 us (9%)
  between operations  1.76 us (1%)
    all_to_all x1, waiting for transfers between devices, on_device(): lax.all_to_all(reply, ('panel', 'col'), 0, 0, tiled=True)  18.8 us
    all_to_all x1, starting transfers between devices, on_device(): lax.all_to_all(bucket.reshape(owners, rows_out * TILE), ('panel', 'col'),...  15.9 us
    ppermute x4, starting transfers between devices, passed_along(): lax.ppermute(value, axis, [(source, source + steps) for source in range(i...  11.8 us
    all_to_all x1, starting transfers between devices, on_device(): lax.all_to_all(reply, ('panel', 'col'), 0, 0, tiled=True)  11.3 us
    gather x1, local copies, waits for them, and re-layouts, on_device(): picked = by_bank[slot_rows.reshape(-1)].reshape(slots, 2, TILE)  6.54 us
    dot_general x1, matrix products, on_device(): jnp.einsum('rj,bji->bri', values, conservative_overlay_factors, precision...  5.66 us
    ppermute x4, waiting for transfers between devices, passed_along(): lax.ppermute(value, axis, [(source, source + steps) for source in range(i...  5.02 us
    unnamed x84, local copies, waits for them, and re-layouts  4.91 us
  transfers between devices with their start and end apart: 8, of which 3 were waited for; matrix products, arithmetic and copies ran while one was open for 40% of the time, Pallas kernels for 0%

profile of v8, /device:TPU:1, one launch (start us, length us, event | category | flops | bytes accessed | tf_op | source)
XLA Modules:
  0.0 165.6 jit_solution(17850413835605335690)
XLA Ops:
  0.7 1.2 bitcast_dynamic-update-slice_fusion.1
  2.8 1.1 bitcast_dynamic-update-slice_fusion
  5.7 1.3 collective-permute-start.1
  7.0 5.3 %collective-permute-start = (f32[20,8,256]{2,1,0:T(8,128)}, f32[20,8,256]{2,1,0:T(8,128)}, u32[]{:S(2)}, u32[]{:S(2)}) collective-permute-start(f32[20,8,256]{2,1,0:T(8,128)} %get-tuple-element.53), channel_id=1, source_target_pairs={{0,1},{1,2},{2,3},{3,4},{4,5},{5,6},{6,7},{7,8},{8,9},{9,10},{10,1... | collective-permute-start | bytes 491528 | tf_op jit(solution)/shard_map/ppermute | solution.py:14
  14.7 3.9 %collective-permute-start.4 = (f32[128,2,128]{2,1,0:T(2,128)}, f32[128,2,128]{2,1,0:T(2,128)}, u32[]{:S(2)}, u32[]{:S(2)}) collective-permute-start(f32[128,2,128]{2,1,0:T(2,128)} %bitcast.23), channel_id=1, source_target_pairs={{0,128},{1,129},{2,130},{3,131},{4,132},{5,133},{6,134},{7,135},{8... | collective-permute-start | bytes 393224 | tf_op jit(solution)/shard_map/ppermute | solution.py:14
  18.6 1.8 %maximum_bitcast_fusion = (f32[4,64,256]{2,1,0:T(8,128)}, f32[4,64,256]{2,1,0:T(8,128)}) fusion(f32[1,3,4,64,256]{4,3,2,1,0:T(8,128)} %param.15), kind=kLoop, calls=%fused_computation.136 | loop fusion | flops 131072 | bytes 786432 | tf_op jit(solution)/shard_map/max | solution.py:49
  20.4 1.5 slice_bitcast_fusion.2
  36.6 1.1 add.335
  38.9 1.6 slice.524
  45.6 1.2 fusion.111
  46.8 1.5 collective-permute-start.3
  48.3 2.3 %collective-permute-start.2 = (f32[20,72,128]{2,1,0:T(8,128)}, f32[20,72,128]{2,1,0:T(8,128)}, u32[]{:S(2)}, u32[]{:S(2)}) collective-permute-start(f32[20,72,128]{2,1,0:T(8,128)} %get-tuple-element.51), channel_id=1, source_target_pairs={{0,32},{32,64},{64,96},{96,0},{1,33},{33,65},{65,97},{97,1},{2,34}... | collective-permute-start | bytes 2211848 | tf_op jit(solution)/shard_map/ppermute | solution.py:19
  50.6 4.7 %fusion.114 = f32[256,32,128]{2,0,1:T(8,128)} fusion(f32[256,128,1]{1,0,2:T(8,128)} %bitcast.25, f32[32,128,128]{2,1,0:T(8,128)S(1)} %copy-done), kind=kOutput, calls=%fused_computation.268 | convolution fusion | flops 805306368 | bytes 6422528 | tf_op jit(solution)/shard_map/bji,ri->brj/dot_general | solution.py:171
  55.3 6.5 %gather_fusion = f32[1024,128]{1,0:T(8,128)} fusion(f32[8192,128]{1,0:T(8,128)} %bitcast.157, s32[1024]{0:T(1024)} %get-tuple-element.91), kind=kCustom, calls=%fused_computation | custom fusion | bytes 1052672 | tf_op jit(solution)/shard_map/gather | solution.py:176
  61.9 2.0 %copy.105 = f32[128,8,128]{0,2,1:T(8,128)} copy(f32[128,8,128]{2,1,0:T(8,128)} %bitcast.167) | data formatting | bytes 1048576 | tf_op jit(solution)/shard_map/reshape | solution.py:176
  63.9 1.1 broadcast_select_fusion
  65.9 2.0 %copy.108 = f32[128,1,1152]{2,1,0:T(1,128)} copy(f32[128,1,1152]{0,2,1:T(8,128)} %bitcast.164) | data formatting | bytes 1179648 | tf_op jit(solution)/shard_map/all_to_all | solution.py:184
  67.9 15.9 %all-to-all-start = ((f32[128,1,1152]{2,1,0:T(1,128)}), f32[128,1,1152]{2,1,0:T(1,128)}, u32[]{:S(2)}, u32[]{:S(2)}) async-start(f32[128,1,1152]{2,1,0:T(1,128)} %copy.108), calls=%async_computation | async-start | bytes 1179648 | tf_op jit(solution)/shard_map/all_to_all | solution.py:184
  83.8 1.4 slice.474
  85.2 2.2 %pad_maximum_fusion = f32[20,72,264]{2,1,0:T(8,128)S(1)} fusion(f32[20,72,4]{2,1,0:T(8,128)} %bitcast.154, f32[20,4,256]{2,1,0:T(4,128)S(1)} %slice.472, f32[20,64,256]{2,1,0:T(8,128)S(1)} %constant_dynamic-update-slice_fusion, f32[20,4,256]{2,1,0:T(4,128)} %copy-done.1, f32[20,72,4]{2,1,0:T(8,128)S(1)} %slice.474), kind=kLoop, calls=%fused_computation.2 | loop fusion | flops 1520640 | bytes 3041280 | tf_op jit(solution)/shard_map/concatenate | solution.py:28
  102.1 2.7 %all-to-all-done = f32[128,1,1152]{2,1,0:T(1,128)} async-done(((f32[128,1,1152]{2,1,0:T(1,128)}), f32[128,1,1152]{2,1,0:T(1,128)}, u32[]{:S(2)}, u32[]{:S(2)}) %all-to-all-start) | async-done | bytes 589856 | tf_op jit(solution)/shard_map/all_to_all | solution.py:184
  104.8 1.5 copy.109
  107.1 2.0 %copy.111 = f32[128,8,128]{2,1,0:T(8,128)} copy(f32[128,8,128]{0,2,1:T(8,128)} %slice.532) | data formatting | bytes 1048576 | tf_op jit(solution)/shard_map/slice | solution.py:187
  109.8 1.8 %convolution_bitcast_fusion = f32[2,64,2,128]{3,1,0,2:T(8,128)S(1)} fusion(f32[128,8,128]{2,1,0:T(8,128)} %copy.111, s32[64,2,2]{0,2,1:T(2,128)S(1)} %copy-done.27, s32[64,2,2]{0,2,1:T(2,128)S(1)} %copy-done.28, s32[1024]{0:T(1024)S(1)} %copy-done.25, s32[1024]{0:T(1024)S(1)} %copy-done.26, s32[64,2,2]{0,2,1:T(2,128)S(1)} %copy-done.30, ...), kind=kOutput, calls=%fused_computation.9 | convolution fusion | flops 404226048 | bytes 673280 | tf_op jit(solution)/shard_map/dot_general | solution.py:196
  113.9 1.5 fusion.17
  115.5 11.3 %all-to-all-start.1 = ((f32[128,8,128]{2,1,0:T(8,128)}), f32[128,8,128]{2,1,0:T(8,128)S(1)}, u32[]{:S(2)}, u32[]{:S(2)}) async-start(f32[128,8,128]{2,1,0:T(8,128)} %fusion.17), calls=%async_computation.1 | async-start | bytes 1048576 | tf_op jit(solution)/shard_map/all_to_all | solution.py:214
  128.1 18.8 %all-to-all-done.1 = f32[128,8,128]{2,1,0:T(8,128)S(1)} async-done(((f32[128,8,128]{2,1,0:T(8,128)}), f32[128,8,128]{2,1,0:T(8,128)S(1)}, u32[]{:S(2)}, u32[]{:S(2)}) %all-to-all-start.1) | async-done | bytes 524320 | tf_op jit(solution)/shard_map/all_to_all | solution.py:214
  146.9 1.2 fusion.3
  148.1 5.7 %fusion.115 = f32[512,32,128]{2,0,1:T(8,128)} fusion(f32[512,128,1]{1,0,2:T(8,128)S(1)} %fusion.3, f32[32,128,128]{2,1,0:T(8,128)S(1)} %copy-done), kind=kOutput, calls=%fused_computation.269 | convolution fusion | flops 1610612736 | bytes 10747904 | tf_op jit(solution)/shard_map/rj,bji->bri/dot_general | solution.py:223
  153.8 4.4 %gather_fusion.1 = f32[512,128]{1,0:T(8,128)S(1)} fusion(f32[16384,128]{1,0:T(8,128)} %bitcast.158, s32[1024]{0:T(1024)S(1)} %copy-done.20), kind=kCustom, calls=%fused_computation.1 | custom fusion | bytes 526336 | tf_op jit(solution)/shard_map/gather | solution.py:229
  158.6 1.3 collective-permute-start.5
  159.9 5.0 %collective-permute-done.5 = f32[2,64,256]{2,1,0:T(8,128)S(1)} collective-permute-done((f32[2,64,256]{2,1,0:T(8,128)S(1)}, f32[2,64,256]{2,1,0:T(8,128)S(1)}, u32[]{:S(2)}, u32[]{:S(2)}) %collective-permute-start.5) | collective-permute-done | bytes 131104 | tf_op jit(solution)/shard_map/ppermute | solution.py:14
  (212 shorter events, 46.8 us)
Async XLA Ops:
  0.6 50.0 %copy-start = (f32[32,128,128]{2,1,0:T(8,128)S(1)}, f32[32,128,128]{2,1,0:T(8,128)}, u32[]{:S(2)}) copy-start(f32[32,128,128]{2,1,0:T(8,128)} %param.23) | copy-start | bytes 6291460
  0.7 4.2 %copy-start.6 = (f32[1,3,4,64,256]{4,3,2,1,0:T(8,128)S(1)}, f32[1,3,4,64,256]{4,3,2,1,0:T(8,128)}, u32[]{:S(2)}) copy-start(f32[1,3,4,64,256]{4,3,2,1,0:T(8,128)} %param.15) | copy-start | bytes 2359300
  3.9 18.0 %copy-start.31 = (s32[128,2]{0,1:T(2,128)S(1)}, s32[128,2]{0,1:T(2,128)}, u32[]{:S(2)}) copy-start(s32[128,2]{0,1:T(2,128)} %param.20) | copy-start | bytes 3076
  4.9 26.1 %copy-start.18 = (s32[128,2]{0,1:T(2,128)S(1)}, s32[128,2]{0,1:T(2,128)}, u32[]{:S(2)}) copy-start(s32[128,2]{0,1:T(2,128)} %param.22) | copy-start | bytes 3076
  5.7 37.8 %collective-permute-start.1 = (f32[20,8,256]{2,1,0:T(8,128)}, f32[20,8,256]{2,1,0:T(8,128)}, u32[]{:S(2)}, u32[]{:S(2)}) collective-permute-start(f32[20,8,256]{2,1,0:T(8,128)} %get-tuple-element.54), channel_id=1, source_target_pairs={{1,0},{2,1},{3,2},{4,3},{5,4},{6,5},{7,6},{8,7},{9,8},{10,9},{11,1... | collective-permute-start | bytes 491528 | tf_op jit(solution)/shard_map/ppermute | solution.py:14
  7.0 37.4 %collective-permute-start = (f32[20,8,256]{2,1,0:T(8,128)}, f32[20,8,256]{2,1,0:T(8,128)}, u32[]{:S(2)}, u32[]{:S(2)}) collective-permute-start(f32[20,8,256]{2,1,0:T(8,128)} %get-tuple-element.53), channel_id=1, source_target_pairs={{0,1},{1,2},{2,3},{3,4},{4,5},{5,6},{6,7},{7,8},{8,9},{9,10},{10,1... | collective-permute-start | bytes 491528 | tf_op jit(solution)/shard_map/ppermute | solution.py:14
  14.7 36.0 %collective-permute-start.4 = (f32[128,2,128]{2,1,0:T(2,128)}, f32[128,2,128]{2,1,0:T(2,128)}, u32[]{:S(2)}, u32[]{:S(2)}) collective-permute-start(f32[128,2,128]{2,1,0:T(2,128)} %bitcast.23), channel_id=1, source_target_pairs={{0,128},{1,129},{2,130},{3,131},{4,132},{5,133},{6,134},{7,135},{8... | collective-permute-start | bytes 393224 | tf_op jit(solution)/shard_map/ppermute | solution.py:14
  30.1 3.7 %copy-start.16 = (s32[256]{0:T(256)}, s32[256]{0:T(256)S(1)}, u32[]{:S(2)}) copy-start(s32[256]{0:T(256)S(1)} %multiply_add_fusion.2) | copy-start | bytes 3076
  46.8 38.4 %collective-permute-start.3 = (f32[20,72,128]{2,1,0:T(8,128)}, f32[20,72,128]{2,1,0:T(8,128)}, u32[]{:S(2)}, u32[]{:S(2)}) collective-permute-start(f32[20,72,128]{2,1,0:T(8,128)} %get-tuple-element.52), channel_id=1, source_target_pairs={{0,96},{32,0},{64,32},{96,64},{1,97},{33,1},{65,33},{97,65},{2,98}... | collective-permute-start | bytes 2211848 | tf_op jit(solution)/shard_map/ppermute | solution.py:19
  48.3 35.5 %collective-permute-start.2 = (f32[20,72,128]{2,1,0:T(8,128)}, f32[20,72,128]{2,1,0:T(8,128)}, u32[]{:S(2)}, u32[]{:S(2)}) collective-permute-start(f32[20,72,128]{2,1,0:T(8,128)} %get-tuple-element.51), channel_id=1, source_target_pairs={{0,32},{32,64},{64,96},{96,0},{1,33},{33,65},{65,97},{97,1},{2,34}... | collective-permute-start | bytes 2211848 | tf_op jit(solution)/shard_map/ppermute | solution.py:19
  67.9 36.9 %all-to-all-start = ((f32[128,1,1152]{2,1,0:T(1,128)}), f32[128,1,1152]{2,1,0:T(1,128)}, u32[]{:S(2)}, u32[]{:S(2)}) async-start(f32[128,1,1152]{2,1,0:T(1,128)} %copy.108), calls=%async_computation | async-start | bytes 1179648 | tf_op jit(solution)/shard_map/all_to_all | solution.py:184
  85.2 2.2 %copy-start.2 = (f32[20,4,256]{2,1,0:T(4,128)S(1)}, f32[20,4,256]{2,1,0:T(4,128)}, u32[]{:S(2)}) copy-start(f32[20,4,256]{2,1,0:T(4,128)} %copy-done.1) | copy-start | bytes 245764
  102.0 7.2 %copy-start.3 = (f32[2,4,64,256]{3,2,1,0:T(8,128)}, f32[2,4,64,256]{3,2,1,0:T(8,128)S(1)}, u32[]{:S(2)}) copy-start(f32[2,4,64,256]{3,2,1,0:T(8,128)S(1)} %pad_subtract_fusion.3) | copy-start | bytes 1572868
  102.0 7.7 %copy-start.25 = (s32[1024]{0:T(1024)S(1)}, s32[1024]{0:T(1024)}, u32[]{:S(2)}) copy-start(s32[1024]{0:T(1024)} %get-tuple-element.92) | copy-start | bytes 12292
  102.0 7.7 %copy-start.26 = (s32[1024]{0:T(1024)S(1)}, s32[1024]{0:T(1024)}, u32[]{:S(2)}) copy-start(s32[1024]{0:T(1024)} %get-tuple-element.93) | copy-start | bytes 12292
  102.0 7.7 %copy-start.27 = (s32[64,2,2]{0,2,1:T(2,128)S(1)}, s32[64,2,2]{0,2,1:T(2,128)}, u32[]{:S(2)}) copy-start(s32[64,2,2]{0,2,1:T(2,128)} %get-tuple-element.98) | copy-start | bytes 3076
  102.0 7.7 %copy-start.28 = (s32[64,2,2]{0,2,1:T(2,128)S(1)}, s32[64,2,2]{0,2,1:T(2,128)}, u32[]{:S(2)}) copy-start(s32[64,2,2]{0,2,1:T(2,128)} %get-tuple-element.99) | copy-start | bytes 3076
  102.0 7.7 %copy-start.29 = (s32[64,2,2]{0,2,1:T(2,128)S(1)}, s32[64,2,2]{0,2,1:T(2,128)}, u32[]{:S(2)}) copy-start(s32[64,2,2]{0,2,1:T(2,128)} %get-tuple-element.96) | copy-start | bytes 3076
  102.0 7.7 %copy-start.30 = (s32[64,2,2]{0,2,1:T(2,128)S(1)}, s32[64,2,2]{0,2,1:T(2,128)}, u32[]{:S(2)}) copy-start(s32[64,2,2]{0,2,1:T(2,128)} %get-tuple-element.97) | copy-start | bytes 3076
  102.1 7.7 %copy-start.33 = (pred[64,2,2]{0,2,1:T(4,128)(4,1)S(1)}, pred[64,2,2]{0,2,1:T(4,128)(4,1)}, u32[]{:S(2)}) copy-start(pred[64,2,2]{0,2,1:T(4,128)(4,1)} %get-tuple-element.94) | copy-start | bytes 772
  102.1 7.7 %copy-start.34 = (pred[64,2,2]{0,2,1:T(4,128)(4,1)S(1)}, pred[64,2,2]{0,2,1:T(4,128)(4,1)}, u32[]{:S(2)}) copy-start(pred[64,2,2]{0,2,1:T(4,128)(4,1)} %get-tuple-element.95) | copy-start | bytes 772
  102.1 7.7 %copy-start.38 = (pred[1024]{0:T(1024)(128)(4,1)S(1)}, pred[1024]{0:T(1024)(128)(4,1)}, u32[]{:S(2)}) copy-start(pred[1024]{0:T(1024)(128)(4,1)} %fusion.98) | copy-start | bytes 3076
  109.2 2.7 %copy-start.9 = (s32[1,64,256]{2,1,0:T(8,128)S(1)}, s32[1,64,256]{2,1,0:T(8,128)}, u32[]{:S(2)}) copy-start(s32[1,64,256]{2,1,0:T(8,128)} %param.16) | copy-start | bytes 196612
  109.2 2.7 %copy-start.5 = (f32[2,4,64,256]{3,2,1,0:T(8,128)S(1)}, f32[2,4,64,256]{3,2,1,0:T(8,128)}, u32[]{:S(2)}) copy-start(f32[2,4,64,256]{3,2,1,0:T(8,128)} %copy-done.3) | copy-start | bytes 1572868
  109.4 2.6 %copy-start.4 = (f32[2,4,64,256]{3,2,1,0:T(8,128)S(1)}, f32[2,4,64,256]{3,2,1,0:T(8,128)}, u32[]{:S(2)}) copy-start(f32[2,4,64,256]{3,2,1,0:T(8,128)} %copy-done.3) | copy-start | bytes 1572868
  109.8 3.1 %copy-start.13 = (s32[64,256]{1,0:T(8,128)S(1)}, s32[64,256]{1,0:T(8,128)}, u32[]{:S(2)}) copy-start(s32[64,256]{1,0:T(8,128)} %param.17) | copy-start | bytes 196612
  111.6 1.5 copy-start.14
  112.0 14.8 %copy-start.17 = (s32[256]{0:T(256)S(1)}, s32[256]{0:T(256)}, u32[]{:S(2)}) copy-start(s32[256]{0:T(256)} %copy-done.16) | copy-start | bytes 3076
  113.9 13.3 %copy-start.19 = (s32[128,2]{0,1:T(2,128)S(1)}, s32[128,2]{0,1:T(2,128)}, u32[]{:S(2)}) copy-start(s32[128,2]{0,1:T(2,128)} %param.22) | copy-start | bytes 3076
  115.5 31.4 %all-to-all-start.1 = ((f32[128,8,128]{2,1,0:T(8,128)}), f32[128,8,128]{2,1,0:T(8,128)S(1)}, u32[]{:S(2)}, u32[]{:S(2)}) async-start(f32[128,8,128]{2,1,0:T(8,128)} %fusion.17), calls=%async_computation.1 | async-start | bytes 1048576 | tf_op jit(solution)/shard_map/all_to_all | solution.py:214
  148.1 5.7 %copy-start.20 = (s32[1024]{0:T(1024)S(1)}, s32[1024]{0:T(1024)}, u32[]{:S(2)}) copy-start(s32[1024]{0:T(1024)} %get-tuple-element.90) | copy-start | bytes 12292
  158.6 6.3 %collective-permute-start.5 = (f32[2,64,256]{2,1,0:T(8,128)S(1)}, f32[2,64,256]{2,1,0:T(8,128)S(1)}, u32[]{:S(2)}, u32[]{:S(2)}) collective-permute-start(f32[2,64,256]{2,1,0:T(8,128)S(1)} %reshape.572), channel_id=1, source_target_pairs={{128,0},{129,1},{130,2},{131,3},{132,4},{133,5},{134,6},{135,7},{1... | collective-permute-start | bytes 393224 | tf_op jit(solution)/shard_map/ppermute | solution.py:14
  (15 other events, 18.8 us)

commit v9 on v7

--- a/solution.py
+++ b/solution.py
@@ -206,7 +206,8 @@
     ocean_tiles = to_tiles(ocean_surface).reshape(pairs, TILE)
     reply = jnp.dot(slot_hit2.T, ocean_tiles, precision=HIGHEST).reshape(owners, capacity * 2, TILE)
     returned = lax.all_to_all(reply, ("panel", "col"), 0, 0, tiled=True).reshape(slots * 2, TILE)
-    place_rep = jnp.broadcast_to(bucket_place[:, None], (pairs, 2)).reshape(-1)
+    reply, late_place = lax.optimization_barrier((reply, bucket_place))
+    place_rep = jnp.broadcast_to(late_place[:, None], (pairs, 2)).reshape(-1)
     p_rows = lax.broadcasted_iota(jnp.int32, (pairs * 2, slots * 2), 0)
     p_cols = lax.broadcasted_iota(jnp.int32, (pairs * 2, slots * 2), 1)
     place_hit2 = ((place_rep[:, None] == p_cols // 2) & (p_cols % 2 == p_rows % 2)).astype(

time: 167 us -> 166 us (level)
  no operation moved by 1% of the time
where the time goes in v9:
time: 166 us; the launch traced here: 165 us
  starting transfers between devices  42.9 us (26%)
  local copies, waits for them, and re-layouts  40.7 us (25%)
  other arithmetic  38.8 us (23%)
  waiting for transfers between devices  26.3 us (16%)
  matrix products  14.7 us (9%)
  between operations  1.74 us (1%)
    all_to_all x1, waiting for transfers between devices, on_device(): lax.all_to_all(reply, ('panel', 'col'), 0, 0, tiled=True)  18.6 us
    all_to_all x1, starting transfers between devices, on_device(): lax.all_to_all(bucket.reshape(owners, rows_out * TILE), ('panel', 'col'),...  15.9 us
    ppermute x4, starting transfers between devices, passed_along(): lax.ppermute(value, axis, [(source, source + steps) for source in range(i...  11.7 us
    all_to_all x1, starting transfers between devices, on_device(): lax.all_to_all(reply, ('panel', 'col'), 0, 0, tiled=True)  11.5 us
    gather x1, local copies, waits for them, and re-layouts, on_device(): picked = by_bank[slot_rows.reshape(-1)].reshape(slots, 2, TILE)  6.54 us
    dot_general x1, matrix products, on_device(): jnp.einsum('rj,bji->bri', values, conservative_overlay_factors, precision...  5.67 us
    unnamed x83, local copies, waits for them, and re-layouts  5.04 us
    ppermute x4, waiting for transfers between devices, passed_along(): lax.ppermute(value, axis, [(source, source + steps) for source in range(i...  5.02 us
  transfers between devices with their start and end apart: 8, of which 3 were waited for; matrix products, arithmetic and copies ran while one was open for 38% of the time, Pallas kernels for 0%

profile of v9, /device:TPU:1, one launch (start us, length us, event | category | flops | bytes accessed | tf_op | source)
XLA Modules:
  0.0 165.1 jit_solution(17905632291011911560)
XLA Ops:
  0.7 2.0 %copy.128 = f32[2,4,64,256]{3,2,1,0:T(8,128)} copy(f32[2,4,64,256]{3,2,1,0:T(8,128)} %bitcast.178) | data formatting | bytes 1048576
  2.7 1.0 fusion.93
  3.7 1.5 bitcast_dynamic-update-slice_fusion
  5.2 1.7 %fusion.90 = (f32[2,4,64,256]{3,2,1,0:T(8,128)}, f32[64,256]{1,0:T(8,128)S(1)}) fusion(f32[2,4,64,256]{3,2,1,0:T(8,128)} %bitcast_dynamic-update-slice_fusion, f32[64,256]{1,0:T(8,128)} %param.23, s32[1,64,256]{2,1,0:T(8,128)} %param.20, f32[2,4,64,256]{3,2,1,0:T(8,128)} %bitcast.180, f32[64,256]{1,0:T(8,128)} %param.22, f32[3,4,64,256]{3,2,1,0:T(8,128)} %bitcast.157), kind=kLoop, calls=%fused_computation.189 | loop fusion | flops 212992 | bytes 589824 | tf_op jit(solution)/shard_map/scatter-add | solution.py:152
  6.9 1.3 broadcast_select_fusion.2
  9.0 1.3 collective-permute-start.1
  10.3 5.3 %collective-permute-start = (f32[20,8,256]{2,1,0:T(8,128)}, f32[20,8,256]{2,1,0:T(8,128)}, u32[]{:S(2)}, u32[]{:S(2)}) collective-permute-start(f32[20,8,256]{2,1,0:T(8,128)} %get-tuple-element.77), channel_id=1, source_target_pairs={{0,1},{1,2},{2,3},{3,4},{4,5},{5,6},{6,7},{7,8},{8,9},{9,10},{10,1... | collective-permute-start | bytes 491528 | tf_op jit(solution)/shard_map/ppermute | solution.py:14
  18.0 3.8 %collective-permute-start.4 = (f32[128,2,128]{2,1,0:T(2,128)}, f32[128,2,128]{2,1,0:T(2,128)}, u32[]{:S(2)}, u32[]{:S(2)}) collective-permute-start(f32[128,2,128]{2,1,0:T(2,128)} %bitcast.23), channel_id=1, source_target_pairs={{0,128},{1,129},{2,130},{3,131},{4,132},{5,133},{6,134},{7,135},{8... | collective-permute-start | bytes 393224 | tf_op jit(solution)/shard_map/ppermute | solution.py:14
  35.3 1.1 add.343
  45.1 1.2 fusion.127
  46.3 1.5 collective-permute-start.3
  47.8 2.3 %collective-permute-start.2 = (f32[20,72,128]{2,1,0:T(8,128)}, f32[20,72,128]{2,1,0:T(8,128)}, u32[]{:S(2)}, u32[]{:S(2)}) collective-permute-start(f32[20,72,128]{2,1,0:T(8,128)} %get-tuple-element.75), channel_id=1, source_target_pairs={{0,32},{32,64},{64,96},{96,0},{1,33},{33,65},{65,97},{97,1},{2,34}... | collective-permute-start | bytes 2211848 | tf_op jit(solution)/shard_map/ppermute | solution.py:19
  50.2 4.7 %fusion.129 = f32[256,32,128]{2,0,1:T(8,128)} fusion(f32[256,128,1]{1,0,2:T(8,128)} %bitcast.25, f32[32,128,128]{2,1,0:T(8,128)S(1)} %copy-done), kind=kOutput, calls=%fused_computation.281 | convolution fusion | flops 805306368 | bytes 6422528 | tf_op jit(solution)/shard_map/bji,ri->brj/dot_general | solution.py:165
  54.9 6.5 %gather_fusion = f32[1024,128]{1,0:T(8,128)} fusion(f32[8192,128]{1,0:T(8,128)} %bitcast.176, s32[1024]{0:T(1024)} %broadcast_clamp_fusion), kind=kCustom, calls=%fused_computation | custom fusion | bytes 1052672 | tf_op jit(solution)/shard_map/gather | solution.py:170
  61.4 2.0 %copy.106 = f32[128,8,128]{0,2,1:T(8,128)} copy(f32[128,8,128]{2,1,0:T(8,128)} %bitcast.184) | data formatting | bytes 1048576 | tf_op jit(solution)/shard_map/reshape | solution.py:170
  63.4 1.1 broadcast_select_fusion
  65.4 2.0 %copy.109 = f32[128,1,1152]{2,1,0:T(1,128)} copy(f32[128,1,1152]{0,2,1:T(8,128)} %bitcast.181) | data formatting | bytes 1179648 | tf_op jit(solution)/shard_map/all_to_all | solution.py:178
  67.4 15.9 %all-to-all-start = ((f32[128,1,1152]{2,1,0:T(1,128)}), f32[128,1,1152]{2,1,0:T(1,128)}, u32[]{:S(2)}, u32[]{:S(2)}) async-start(f32[128,1,1152]{2,1,0:T(1,128)} %copy.109), calls=%async_computation | async-start | bytes 1179648 | tf_op jit(solution)/shard_map/all_to_all | solution.py:178
  83.3 1.4 slice.521
  84.7 2.2 %pad_maximum_fusion = f32[20,72,264]{2,1,0:T(8,128)S(1)} fusion(f32[20,72,4]{2,1,0:T(8,128)} %bitcast.153, f32[20,4,256]{2,1,0:T(4,128)S(1)} %slice.519, f32[12,64,256]{2,1,0:T(8,128)S(1)} %bitcast.162, f32[8,64,256]{2,1,0:T(8,128)S(1)} %bitcast.170, f32[20,4,256]{2,1,0:T(4,128)} %copy-done.2, f32[20,72,4]{2,1,0:T(8,128)S(1)} %slice.521), kind=kLoop, calls=%fused_computation.2 | loop fusion | flops 1900800 | bytes 3041280 | tf_op jit(solution)/shard_map/concatenate | solution.py:28
  101.6 2.7 %all-to-all-done = f32[128,1,1152]{2,1,0:T(1,128)} async-done(((f32[128,1,1152]{2,1,0:T(1,128)}), f32[128,1,1152]{2,1,0:T(1,128)}, u32[]{:S(2)}, u32[]{:S(2)}) %all-to-all-start) | async-done | bytes 589856 | tf_op jit(solution)/shard_map/all_to_all | solution.py:178
  104.3 1.5 copy.110
  106.7 2.0 %copy.112 = f32[128,8,128]{2,1,0:T(8,128)} copy(f32[128,8,128]{0,2,1:T(8,128)} %slice.579) | data formatting | bytes 1048576 | tf_op jit(solution)/shard_map/slice | solution.py:181
  109.3 1.8 %convolution_bitcast_fusion = f32[2,64,2,128]{3,1,0,2:T(8,128)S(1)} fusion(f32[128,8,128]{2,1,0:T(8,128)} %copy.112, s32[64,2,2]{0,2,1:T(2,128)S(1)} %copy-done.23, s32[64,2,2]{0,2,1:T(2,128)S(1)} %copy-done.24, s32[1024]{0:T(1024)S(1)} %copy-done.19, s32[1024]{0:T(1024)S(1)} %copy-done.20, s32[64,2,2]{0,2,1:T(2,128)S(1)} %copy-done.26, ...), kind=kOutput, calls=%fused_computation.9 | convolution fusion | flops 404226048 | bytes 673280 | tf_op jit(solution)/shard_map/dot_general | solution.py:190
  113.7 1.1 copy.119
  114.8 11.5 %all-to-all-start.1 = ((f32[128,8,128]{2,1,0:T(8,128)}), f32[128,8,128]{2,1,0:T(8,128)S(1)}, u32[]{:S(2)}, u32[]{:S(2)}) async-start(f32[128,8,128]{2,1,0:T(8,128)} %copy.119), calls=%async_computation.1 | async-start | bytes 1048576 | tf_op jit(solution)/shard_map/all_to_all | solution.py:208
  127.8 18.6 %all-to-all-done.1 = f32[128,8,128]{2,1,0:T(8,128)S(1)} async-done(((f32[128,8,128]{2,1,0:T(8,128)}), f32[128,8,128]{2,1,0:T(8,128)S(1)}, u32[]{:S(2)}, u32[]{:S(2)}) %all-to-all-start.1) | async-done | bytes 524320 | tf_op jit(solution)/shard_map/all_to_all | solution.py:208
  146.4 1.2 fusion.3
  147.6 5.7 %fusion.130 = f32[512,32,128]{2,0,1:T(8,128)} fusion(f32[512,128,1]{1,0,2:T(8,128)S(1)} %fusion.3, f32[32,128,128]{2,1,0:T(8,128)S(1)} %copy-done), kind=kOutput, calls=%fused_computation.282 | convolution fusion | flops 1610612736 | bytes 10747904 | tf_op jit(solution)/shard_map/rj,bji->bri/dot_general | solution.py:218
  153.3 4.4 %gather_fusion.1 = f32[512,128]{1,0:T(8,128)S(1)} fusion(f32[16384,128]{1,0:T(8,128)} %bitcast.177, s32[1024]{0:T(1024)S(1)} %pad_clamp_fusion), kind=kCustom, calls=%fused_computation.1 | custom fusion | bytes 526336 | tf_op jit(solution)/shard_map/gather | solution.py:224
  158.1 1.3 collective-permute-start.5
  159.4 5.0 %collective-permute-done.5 = f32[2,64,256]{2,1,0:T(8,128)S(1)} collective-permute-done((f32[2,64,256]{2,1,0:T(8,128)S(1)}, f32[2,64,256]{2,1,0:T(8,128)S(1)}, u32[]{:S(2)}, u32[]{:S(2)}) %collective-permute-start.5) | collective-permute-done | bytes 131104 | tf_op jit(solution)/shard_map/ppermute | solution.py:14
  (213 shorter events, 46.7 us)
Async XLA Ops:
  0.6 49.5 %copy-start = (f32[32,128,128]{2,1,0:T(8,128)S(1)}, f32[32,128,128]{2,1,0:T(8,128)}, u32[]{:S(2)}) copy-start(f32[32,128,128]{2,1,0:T(8,128)} %param.27) | copy-start | bytes 6291460
  0.6 7.6 %copy-start.1 = (f32[1,3,4,64,256]{4,3,2,1,0:T(8,128)S(1)}, f32[1,3,4,64,256]{4,3,2,1,0:T(8,128)}, u32[]{:S(2)}) copy-start(f32[1,3,4,64,256]{4,3,2,1,0:T(8,128)} %param.19) | copy-start | bytes 2359300
  6.9 16.3 %copy-start.27 = (s32[128,2]{0,1:T(2,128)S(1)}, s32[128,2]{0,1:T(2,128)}, u32[]{:S(2)}) copy-start(s32[128,2]{0,1:T(2,128)} %param.24) | copy-start | bytes 3076
  8.2 24.1 %copy-start.17 = (s32[128,2]{0,1:T(2,128)S(1)}, s32[128,2]{0,1:T(2,128)}, u32[]{:S(2)}) copy-start(s32[128,2]{0,1:T(2,128)} %param.26) | copy-start | bytes 3076
  9.0 34.0 %collective-permute-start.1 = (f32[20,8,256]{2,1,0:T(8,128)}, f32[20,8,256]{2,1,0:T(8,128)}, u32[]{:S(2)}, u32[]{:S(2)}) collective-permute-start(f32[20,8,256]{2,1,0:T(8,128)} %get-tuple-element.78), channel_id=1, source_target_pairs={{1,0},{2,1},{3,2},{4,3},{5,4},{6,5},{7,6},{8,7},{9,8},{10,9},{11,1... | collective-permute-start | bytes 491528 | tf_op jit(solution)/shard_map/ppermute | solution.py:14
  10.3 33.7 %collective-permute-start = (f32[20,8,256]{2,1,0:T(8,128)}, f32[20,8,256]{2,1,0:T(8,128)}, u32[]{:S(2)}, u32[]{:S(2)}) collective-permute-start(f32[20,8,256]{2,1,0:T(8,128)} %get-tuple-element.77), channel_id=1, source_target_pairs={{0,1},{1,2},{2,3},{3,4},{4,5},{5,6},{6,7},{7,8},{8,9},{9,10},{10,1... | collective-permute-start | bytes 491528 | tf_op jit(solution)/shard_map/ppermute | solution.py:14
  18.0 32.2 %collective-permute-start.4 = (f32[128,2,128]{2,1,0:T(2,128)}, f32[128,2,128]{2,1,0:T(2,128)}, u32[]{:S(2)}, u32[]{:S(2)}) collective-permute-start(f32[128,2,128]{2,1,0:T(2,128)} %bitcast.23), channel_id=1, source_target_pairs={{0,128},{1,129},{2,130},{3,131},{4,132},{5,133},{6,134},{7,135},{8... | collective-permute-start | bytes 393224 | tf_op jit(solution)/shard_map/ppermute | solution.py:14
  31.4 11.6 %copy-start.15 = (s32[256]{0:T(256)}, s32[256]{0:T(256)S(1)}, u32[]{:S(2)}) copy-start(s32[256]{0:T(256)S(1)} %multiply_add_fusion.2) | copy-start | bytes 3076
  46.3 38.4 %collective-permute-start.3 = (f32[20,72,128]{2,1,0:T(8,128)}, f32[20,72,128]{2,1,0:T(8,128)}, u32[]{:S(2)}, u32[]{:S(2)}) collective-permute-start(f32[20,72,128]{2,1,0:T(8,128)} %get-tuple-element.76), channel_id=1, source_target_pairs={{0,96},{32,0},{64,32},{96,64},{1,97},{33,1},{65,33},{97,65},{2,98}... | collective-permute-start | bytes 2211848 | tf_op jit(solution)/shard_map/ppermute | solution.py:19
  47.8 35.5 %collective-permute-start.2 = (f32[20,72,128]{2,1,0:T(8,128)}, f32[20,72,128]{2,1,0:T(8,128)}, u32[]{:S(2)}, u32[]{:S(2)}) collective-permute-start(f32[20,72,128]{2,1,0:T(8,128)} %get-tuple-element.75), channel_id=1, source_target_pairs={{0,32},{32,64},{64,96},{96,0},{1,33},{33,65},{65,97},{97,1},{2,34}... | collective-permute-start | bytes 2211848 | tf_op jit(solution)/shard_map/ppermute | solution.py:19
  67.4 36.9 %all-to-all-start = ((f32[128,1,1152]{2,1,0:T(1,128)}), f32[128,1,1152]{2,1,0:T(1,128)}, u32[]{:S(2)}, u32[]{:S(2)}) async-start(f32[128,1,1152]{2,1,0:T(1,128)} %copy.109), calls=%async_computation | async-start | bytes 1179648 | tf_op jit(solution)/shard_map/all_to_all | solution.py:178
  84.7 2.2 %copy-start.3 = (f32[20,4,256]{2,1,0:T(4,128)S(1)}, f32[20,4,256]{2,1,0:T(4,128)}, u32[]{:S(2)}) copy-start(f32[20,4,256]{2,1,0:T(4,128)} %copy-done.2) | copy-start | bytes 245764
  101.5 7.2 %copy-start.4 = (f32[2,4,64,256]{3,2,1,0:T(8,128)}, f32[2,4,64,256]{3,2,1,0:T(8,128)S(1)}, u32[]{:S(2)}) copy-start(f32[2,4,64,256]{3,2,1,0:T(8,128)S(1)} %pad_subtract_fusion.3) | copy-start | bytes 1572868
  101.5 7.7 %copy-start.19 = (s32[1024]{0:T(1024)S(1)}, s32[1024]{0:T(1024)}, u32[]{:S(2)}) copy-start(s32[1024]{0:T(1024)} %get-tuple-element.116) | copy-start | bytes 12292
  101.5 7.7 %copy-start.20 = (s32[1024]{0:T(1024)S(1)}, s32[1024]{0:T(1024)}, u32[]{:S(2)}) copy-start(s32[1024]{0:T(1024)} %get-tuple-element.117) | copy-start | bytes 12292
  101.5 7.7 %copy-start.23 = (s32[64,2,2]{0,2,1:T(2,128)S(1)}, s32[64,2,2]{0,2,1:T(2,128)}, u32[]{:S(2)}) copy-start(s32[64,2,2]{0,2,1:T(2,128)} %get-tuple-element.122) | copy-start | bytes 3076
  101.6 7.7 %copy-start.24 = (s32[64,2,2]{0,2,1:T(2,128)S(1)}, s32[64,2,2]{0,2,1:T(2,128)}, u32[]{:S(2)}) copy-start(s32[64,2,2]{0,2,1:T(2,128)} %get-tuple-element.123) | copy-start | bytes 3076
  101.6 7.7 %copy-start.25 = (s32[64,2,2]{0,2,1:T(2,128)S(1)}, s32[64,2,2]{0,2,1:T(2,128)}, u32[]{:S(2)}) copy-start(s32[64,2,2]{0,2,1:T(2,128)} %get-tuple-element.120) | copy-start | bytes 3076
  101.6 7.7 %copy-start.26 = (s32[64,2,2]{0,2,1:T(2,128)S(1)}, s32[64,2,2]{0,2,1:T(2,128)}, u32[]{:S(2)}) copy-start(s32[64,2,2]{0,2,1:T(2,128)} %get-tuple-element.121) | copy-start | bytes 3076
  101.6 7.7 %copy-start.32 = (pred[64,2,2]{0,2,1:T(4,128)(4,1)S(1)}, pred[64,2,2]{0,2,1:T(4,128)(4,1)}, u32[]{:S(2)}) copy-start(pred[64,2,2]{0,2,1:T(4,128)(4,1)} %get-tuple-element.118) | copy-start | bytes 772
  101.6 7.7 %copy-start.33 = (pred[64,2,2]{0,2,1:T(4,128)(4,1)S(1)}, pred[64,2,2]{0,2,1:T(4,128)(4,1)}, u32[]{:S(2)}) copy-start(pred[64,2,2]{0,2,1:T(4,128)(4,1)} %get-tuple-element.119) | copy-start | bytes 772
  101.6 7.7 %copy-start.35 = (pred[1024]{0:T(1024)(128)(4,1)S(1)}, pred[1024]{0:T(1024)(128)(4,1)}, u32[]{:S(2)}) copy-start(pred[1024]{0:T(1024)(128)(4,1)} %fusion.113) | copy-start | bytes 3076
  108.7 2.7 %copy-start.9 = (s32[1,64,256]{2,1,0:T(8,128)S(1)}, s32[1,64,256]{2,1,0:T(8,128)}, u32[]{:S(2)}) copy-start(s32[1,64,256]{2,1,0:T(8,128)} %param.20) | copy-start | bytes 196612
  108.7 2.7 %copy-start.6 = (f32[2,4,64,256]{3,2,1,0:T(8,128)S(1)}, f32[2,4,64,256]{3,2,1,0:T(8,128)}, u32[]{:S(2)}) copy-start(f32[2,4,64,256]{3,2,1,0:T(8,128)} %copy-done.4) | copy-start | bytes 1572868
  108.9 2.6 %copy-start.5 = (f32[2,4,64,256]{3,2,1,0:T(8,128)S(1)}, f32[2,4,64,256]{3,2,1,0:T(8,128)}, u32[]{:S(2)}) copy-start(f32[2,4,64,256]{3,2,1,0:T(8,128)} %copy-done.4) | copy-start | bytes 1572868
  109.3 3.0 %copy-start.14 = (s32[64,256]{1,0:T(8,128)S(1)}, s32[64,256]{1,0:T(8,128)}, u32[]{:S(2)}) copy-start(s32[64,256]{1,0:T(8,128)} %param.21) | copy-start | bytes 196612
  111.2 1.5 copy-start.21
  112.7 13.6 %copy-start.18 = (s32[128,2]{0,1:T(2,128)S(1)}, s32[128,2]{0,1:T(2,128)}, u32[]{:S(2)}) copy-start(s32[128,2]{0,1:T(2,128)} %param.26) | copy-start | bytes 3076
  112.7 13.6 %copy-start.12 = (s32[128,2,2]{2,1,0:T(2,128)S(1)}, s32[128,2,2]{2,1,0:T(2,128)}, u32[]{:S(2)}) copy-start(s32[128,2,2]{2,1,0:T(2,128)} %iota_add_fusion.1) | copy-start | bytes 6148
  114.8 12.7 %copy-start.16 = (s32[256]{0:T(256)S(1)}, s32[256]{0:T(256)}, u32[]{:S(2)}) copy-start(s32[256]{0:T(256)} %copy-done.15) | copy-start | bytes 3076
  114.8 31.5 %all-to-all-start.1 = ((f32[128,8,128]{2,1,0:T(8,128)}), f32[128,8,128]{2,1,0:T(8,128)S(1)}, u32[]{:S(2)}, u32[]{:S(2)}) async-start(f32[128,8,128]{2,1,0:T(8,128)} %copy.119), calls=%async_computation.1 | async-start | bytes 1048576 | tf_op jit(solution)/shard_map/all_to_all | solution.py:208
  158.1 6.3 %collective-permute-start.5 = (f32[2,64,256]{2,1,0:T(8,128)S(1)}, f32[2,64,256]{2,1,0:T(8,128)S(1)}, u32[]{:S(2)}, u32[]{:S(2)}) collective-permute-start(f32[2,64,256]{2,1,0:T(8,128)S(1)} %reshape.644), channel_id=1, source_target_pairs={{128,0},{129,1},{130,2},{131,3},{132,4},{133,5},{134,6},{135,7},{1... | collective-permute-start | bytes 393224 | tf_op jit(solution)/shard_map/ppermute | solution.py:14
  (15 other events, 18.7 us)

commit v10 on v7

--- a/solution.py
+++ b/solution.py
@@ -187,7 +187,7 @@
     slot_hit2 = (
         (recv_rep[None, :] == row_ids // 2) & (col_ids % 2 == row_ids % 2)
     ).astype(jnp.float32)
-    summed = jnp.dot(slot_hit2, received, precision=HIGHEST)
+    summed = jnp.dot(slot_hit2, received, precision=lax.Precision.HIGH)
     forcing = from_tiles(summed.reshape(tile_count, 2, TILE), grid_rows, grid_cols)
 
     tracer = advect(start, coeffs, grid_rows)
@@ -204,7 +204,7 @@
     )
     ocean_surface = jnp.stack([sea_temp, ice_cover])
     ocean_tiles = to_tiles(ocean_surface).reshape(pairs, TILE)
-    reply = jnp.dot(slot_hit2.T, ocean_tiles, precision=HIGHEST).reshape(owners, capacity * 2, TILE)
+    reply = jnp.dot(slot_hit2.T, ocean_tiles, precision=lax.Precision.HIGH).reshape(owners, capacity * 2, TILE)
     returned = lax.all_to_all(reply, ("panel", "col"), 0, 0, tiled=True).reshape(slots * 2, TILE)
     place_rep = jnp.broadcast_to(bucket_place[:, None], (pairs, 2)).reshape(-1)
     p_rows = lax.broadcasted_iota(jnp.int32, (pairs * 2, slots * 2), 0)
@@ -212,7 +212,7 @@
     place_hit2 = ((place_rep[:, None] == p_cols // 2) & (p_cols % 2 == p_rows % 2)).astype(
         jnp.float32
     )
-    values = jnp.dot(place_hit2, returned, precision=HIGHEST)
+    values = jnp.dot(place_hit2, returned, precision=lax.Precision.HIGH)
 
     by_bank_back = jnp.einsum(
         "rj,bji->bri", values, conservative_overlay_factors, precision=lax.Precision.HIGH
@@ -226,7 +226,7 @@
     bank_count = (bank_tile_entry[:, :1] == bank_ids).astype(jnp.float32) + (
         bank_tile_entry[:, 1:] == bank_ids
     ).astype(jnp.float32)
-    denominator = jnp.dot(bank_count, column_sums, precision=HIGHEST)
+    denominator = jnp.dot(bank_count, column_sums, precision=lax.Precision.HIGH)
     remap_back = numerator / denominator[:, None, :]
     remapped = passed_along(from_tiles(remap_back, grid_rows, grid_cols), "comp", -1)
     surface_here = jnp.where(on_atmos, remapped, ocean_surface)

time: 167 us -> 166 us (level)
  no operation moved by 1% of the time
where the time goes in v10:
time: 166 us; the launch traced here: 164 us
  starting transfers between devices  42.7 us (26%)
  local copies, waits for them, and re-layouts  39.6 us (24%)
  other arithmetic  39.5 us (24%)
  waiting for transfers between devices  26.4 us (16%)
  matrix products  14.4 us (9%)
  between operations  1.75 us (1%)
    all_to_all x1, waiting for transfers between devices, on_device(): lax.all_to_all(reply, ('panel', 'col'), 0, 0, tiled=True)  18.6 us
    all_to_all x1, starting transfers between devices, on_device(): lax.all_to_all(bucket.reshape(owners, rows_out * TILE), ('panel', 'col'),...  15.9 us
    ppermute x4, starting transfers between devices, passed_along(): lax.ppermute(value, axis, [(source, source + steps) for source in range(i...  11.7 us
    all_to_all x1, starting transfers between devices, on_device(): lax.all_to_all(reply, ('panel', 'col'), 0, 0, tiled=True)  11.3 us
    gather x1, local copies, waits for them, and re-layouts, on_device(): picked = by_bank[slot_rows.reshape(-1)].reshape(slots, 2, TILE)  6.54 us
    dot_general x1, matrix products, on_device(): jnp.einsum('rj,bji->bri', values, conservative_overlay_factors, precision...  5.67 us
    unnamed x83, local copies, waits for them, and re-layouts  5.03 us
    ppermute x4, waiting for transfers between devices, passed_along(): lax.ppermute(value, axis, [(source, source + steps) for source in range(i...  5.02 us
  transfers between devices with their start and end apart: 8, of which 3 were waited for; matrix products, arithmetic and copies ran while one was open for 38% of the time, Pallas kernels for 0%

profile of v10, /device:TPU:1, one launch (start us, length us, event | category | flops | bytes accessed | tf_op | source)
XLA Modules:
  0.0 164.3 jit_solution(15734140149525830902)
XLA Ops:
  0.7 2.0 %copy.132 = f32[2,4,64,256]{3,2,1,0:T(8,128)} copy(f32[2,4,64,256]{3,2,1,0:T(8,128)} %bitcast.178) | data formatting | bytes 1048576
  2.7 1.0 fusion.83
  3.7 1.5 bitcast_dynamic-update-slice_fusion
  5.2 1.7 %fusion.80 = (f32[2,4,64,256]{3,2,1,0:T(8,128)}, f32[64,256]{1,0:T(8,128)S(1)}) fusion(f32[2,4,64,256]{3,2,1,0:T(8,128)} %bitcast_dynamic-update-slice_fusion, f32[64,256]{1,0:T(8,128)} %param.23, s32[1,64,256]{2,1,0:T(8,128)} %param.20, f32[2,4,64,256]{3,2,1,0:T(8,128)} %bitcast.180, f32[64,256]{1,0:T(8,128)} %param.22, f32[3,4,64,256]{3,2,1,0:T(8,128)} %bitcast.157), kind=kLoop, calls=%fused_computation.180 | loop fusion | flops 212992 | bytes 589824 | tf_op jit(solution)/shard_map/scatter-add | solution.py:152
  6.9 1.3 broadcast_select_fusion.2
  9.0 1.3 collective-permute-start.1
  10.3 5.3 %collective-permute-start = (f32[20,8,256]{2,1,0:T(8,128)}, f32[20,8,256]{2,1,0:T(8,128)}, u32[]{:S(2)}, u32[]{:S(2)}) collective-permute-start(f32[20,8,256]{2,1,0:T(8,128)} %get-tuple-element.75), channel_id=1, source_target_pairs={{0,1},{1,2},{2,3},{3,4},{4,5},{5,6},{6,7},{7,8},{8,9},{9,10},{10,1... | collective-permute-start | bytes 491528 | tf_op jit(solution)/shard_map/ppermute | solution.py:14
  18.0 3.8 %collective-permute-start.4 = (f32[128,2,128]{2,1,0:T(2,128)}, f32[128,2,128]{2,1,0:T(2,128)}, u32[]{:S(2)}, u32[]{:S(2)}) collective-permute-start(f32[128,2,128]{2,1,0:T(2,128)} %bitcast.23), channel_id=1, source_target_pairs={{0,128},{1,129},{2,130},{3,131},{4,132},{5,133},{6,134},{7,135},{8... | collective-permute-start | bytes 393224 | tf_op jit(solution)/shard_map/ppermute | solution.py:14
  30.1 1.0 fusion.70
  35.3 1.1 add.347
  45.1 1.2 fusion.117
  46.3 1.5 collective-permute-start.3
  47.8 2.3 %collective-permute-start.2 = (f32[20,72,128]{2,1,0:T(8,128)}, f32[20,72,128]{2,1,0:T(8,128)}, u32[]{:S(2)}, u32[]{:S(2)}) collective-permute-start(f32[20,72,128]{2,1,0:T(8,128)} %get-tuple-element.73), channel_id=1, source_target_pairs={{0,32},{32,64},{64,96},{96,0},{1,33},{33,65},{65,97},{97,1},{2,34}... | collective-permute-start | bytes 2211848 | tf_op jit(solution)/shard_map/ppermute | solution.py:19
  50.2 4.7 %fusion.119 = f32[256,32,128]{2,0,1:T(8,128)} fusion(f32[256,128,1]{1,0,2:T(8,128)} %bitcast.25, f32[32,128,128]{2,1,0:T(8,128)S(1)} %copy-done), kind=kOutput, calls=%fused_computation.272 | convolution fusion | flops 805306368 | bytes 6422528 | tf_op jit(solution)/shard_map/bji,ri->brj/dot_general | solution.py:165
  54.9 6.5 %gather_fusion = f32[1024,128]{1,0:T(8,128)} fusion(f32[8192,128]{1,0:T(8,128)} %bitcast.176, s32[1024]{0:T(1024)} %broadcast_clamp_fusion), kind=kCustom, calls=%fused_computation | custom fusion | bytes 1052672 | tf_op jit(solution)/shard_map/gather | solution.py:170
  61.4 2.0 %copy.106 = f32[128,8,128]{0,2,1:T(8,128)} copy(f32[128,8,128]{2,1,0:T(8,128)} %bitcast.184) | data formatting | bytes 1048576 | tf_op jit(solution)/shard_map/reshape | solution.py:170
  63.4 1.1 broadcast_select_fusion
  65.4 2.0 %copy.109 = f32[128,1,1152]{2,1,0:T(1,128)} copy(f32[128,1,1152]{0,2,1:T(8,128)} %bitcast.181) | data formatting | bytes 1179648 | tf_op jit(solution)/shard_map/all_to_all | solution.py:178
  67.4 15.9 %all-to-all-start = ((f32[128,1,1152]{2,1,0:T(1,128)}), f32[128,1,1152]{2,1,0:T(1,128)}, u32[]{:S(2)}, u32[]{:S(2)}) async-start(f32[128,1,1152]{2,1,0:T(1,128)} %copy.109), calls=%async_computation | async-start | bytes 1179648 | tf_op jit(solution)/shard_map/all_to_all | solution.py:178
  83.3 1.4 slice.521
  84.7 2.2 %pad_maximum_fusion = f32[20,72,264]{2,1,0:T(8,128)S(1)} fusion(f32[20,72,4]{2,1,0:T(8,128)} %bitcast.153, f32[20,4,256]{2,1,0:T(4,128)S(1)} %slice.519, f32[12,64,256]{2,1,0:T(8,128)S(1)} %bitcast.162, f32[8,64,256]{2,1,0:T(8,128)S(1)} %bitcast.170, f32[20,4,256]{2,1,0:T(4,128)} %copy-done.2, f32[20,72,4]{2,1,0:T(8,128)S(1)} %slice.521), kind=kLoop, calls=%fused_computation.2 | loop fusion | flops 1900800 | bytes 3041280 | tf_op jit(solution)/shard_map/concatenate | solution.py:28
  101.6 2.7 %all-to-all-done = f32[128,1,1152]{2,1,0:T(1,128)} async-done(((f32[128,1,1152]{2,1,0:T(1,128)}), f32[128,1,1152]{2,1,0:T(1,128)}, u32[]{:S(2)}, u32[]{:S(2)}) %all-to-all-start) | async-done | bytes 589856 | tf_op jit(solution)/shard_map/all_to_all | solution.py:178
  104.3 1.5 copy.110
  106.7 2.0 %copy.112 = f32[128,8,128]{2,1,0:T(8,128)} copy(f32[128,8,128]{0,2,1:T(8,128)} %slice.579) | data formatting | bytes 1048576 | tf_op jit(solution)/shard_map/slice | solution.py:181
  109.3 1.7 %convolution_bitcast_fusion = f32[2,64,2,128]{3,1,0,2:T(8,128)S(1)} fusion(f32[128,8,128]{2,1,0:T(8,128)} %copy.112, s32[64,2,2]{0,2,1:T(2,128)S(1)} %copy-done.27, s32[64,2,2]{0,2,1:T(2,128)S(1)} %copy-done.28, s32[1024]{0:T(1024)S(1)} %copy-done.25, s32[1024]{0:T(1024)S(1)} %copy-done.26, s32[64,2,2]{0,2,1:T(2,128)S(1)} %copy-done.30, ...), kind=kOutput, calls=%fused_computation.9 | convolution fusion | flops 202899456 | bytes 673280 | tf_op jit(solution)/shard_map/dot_general | solution.py:190
  113.3 1.2 fusion.17
  114.6 11.3 %all-to-all-start.1 = ((f32[128,8,128]{2,1,0:T(8,128)}), f32[128,8,128]{2,1,0:T(8,128)S(1)}, u32[]{:S(2)}, u32[]{:S(2)}) async-start(f32[128,8,128]{2,1,0:T(8,128)} %fusion.17), calls=%async_computation.1 | async-start | bytes 1048576 | tf_op jit(solution)/shard_map/all_to_all | solution.py:208
  127.3 18.6 %all-to-all-done.1 = f32[128,8,128]{2,1,0:T(8,128)S(1)} async-done(((f32[128,8,128]{2,1,0:T(8,128)}), f32[128,8,128]{2,1,0:T(8,128)S(1)}, u32[]{:S(2)}, u32[]{:S(2)}) %all-to-all-start.1) | async-done | bytes 524320 | tf_op jit(solution)/shard_map/all_to_all | solution.py:208
  146.8 5.7 %fusion.120 = f32[512,32,128]{2,0,1:T(8,128)} fusion(f32[512,128,1]{1,0,2:T(8,128)S(1)} %fusion.3, f32[32,128,128]{2,1,0:T(8,128)S(1)} %copy-done), kind=kOutput, calls=%fused_computation.273 | convolution fusion | flops 1610612736 | bytes 10747904 | tf_op jit(solution)/shard_map/rj,bji->bri/dot_general | solution.py:217
  152.5 4.4 %gather_fusion.1 = f32[512,128]{1,0:T(8,128)S(1)} fusion(f32[16384,128]{1,0:T(8,128)} %bitcast.177, s32[1024]{0:T(1024)S(1)} %pad_clamp_fusion), kind=kCustom, calls=%fused_computation.1 | custom fusion | bytes 526336 | tf_op jit(solution)/shard_map/gather | solution.py:223
  157.4 1.3 collective-permute-start.5
  158.7 5.0 %collective-permute-done.5 = f32[2,64,256]{2,1,0:T(8,128)S(1)} collective-permute-done((f32[2,64,256]{2,1,0:T(8,128)S(1)}, f32[2,64,256]{2,1,0:T(8,128)S(1)}, u32[]{:S(2)}, u32[]{:S(2)}) %collective-permute-start.5) | collective-permute-done | bytes 131104 | tf_op jit(solution)/shard_map/ppermute | solution.py:14
  (213 shorter events, 46.2 us)
Async XLA Ops:
  0.6 49.5 %copy-start = (f32[32,128,128]{2,1,0:T(8,128)S(1)}, f32[32,128,128]{2,1,0:T(8,128)}, u32[]{:S(2)}) copy-start(f32[32,128,128]{2,1,0:T(8,128)} %param.27) | copy-start | bytes 6291460
  0.6 7.6 %copy-start.1 = (f32[1,3,4,64,256]{4,3,2,1,0:T(8,128)S(1)}, f32[1,3,4,64,256]{4,3,2,1,0:T(8,128)}, u32[]{:S(2)}) copy-start(f32[1,3,4,64,256]{4,3,2,1,0:T(8,128)} %param.19) | copy-start | bytes 2359300
  6.9 16.3 %copy-start.31 = (s32[128,2]{0,1:T(2,128)S(1)}, s32[128,2]{0,1:T(2,128)}, u32[]{:S(2)}) copy-start(s32[128,2]{0,1:T(2,128)} %param.24) | copy-start | bytes 3076
  8.2 24.1 %copy-start.19 = (s32[128,2]{0,1:T(2,128)S(1)}, s32[128,2]{0,1:T(2,128)}, u32[]{:S(2)}) copy-start(s32[128,2]{0,1:T(2,128)} %param.26) | copy-start | bytes 3076
  9.0 34.0 %collective-permute-start.1 = (f32[20,8,256]{2,1,0:T(8,128)}, f32[20,8,256]{2,1,0:T(8,128)}, u32[]{:S(2)}, u32[]{:S(2)}) collective-permute-start(f32[20,8,256]{2,1,0:T(8,128)} %get-tuple-element.76), channel_id=1, source_target_pairs={{1,0},{2,1},{3,2},{4,3},{5,4},{6,5},{7,6},{8,7},{9,8},{10,9},{11,1... | collective-permute-start | bytes 491528 | tf_op jit(solution)/shard_map/ppermute | solution.py:14
  10.3 33.7 %collective-permute-start = (f32[20,8,256]{2,1,0:T(8,128)}, f32[20,8,256]{2,1,0:T(8,128)}, u32[]{:S(2)}, u32[]{:S(2)}) collective-permute-start(f32[20,8,256]{2,1,0:T(8,128)} %get-tuple-element.75), channel_id=1, source_target_pairs={{0,1},{1,2},{2,3},{3,4},{4,5},{5,6},{6,7},{7,8},{8,9},{9,10},{10,1... | collective-permute-start | bytes 491528 | tf_op jit(solution)/shard_map/ppermute | solution.py:14
  18.0 32.2 %collective-permute-start.4 = (f32[128,2,128]{2,1,0:T(2,128)}, f32[128,2,128]{2,1,0:T(2,128)}, u32[]{:S(2)}, u32[]{:S(2)}) collective-permute-start(f32[128,2,128]{2,1,0:T(2,128)} %bitcast.23), channel_id=1, source_target_pairs={{0,128},{1,129},{2,130},{3,131},{4,132},{5,133},{6,134},{7,135},{8... | collective-permute-start | bytes 393224 | tf_op jit(solution)/shard_map/ppermute | solution.py:14
  31.4 11.6 %copy-start.17 = (s32[256]{0:T(256)}, s32[256]{0:T(256)S(1)}, u32[]{:S(2)}) copy-start(s32[256]{0:T(256)S(1)} %multiply_add_fusion.2) | copy-start | bytes 3076
  46.3 38.4 %collective-permute-start.3 = (f32[20,72,128]{2,1,0:T(8,128)}, f32[20,72,128]{2,1,0:T(8,128)}, u32[]{:S(2)}, u32[]{:S(2)}) collective-permute-start(f32[20,72,128]{2,1,0:T(8,128)} %get-tuple-element.74), channel_id=1, source_target_pairs={{0,96},{32,0},{64,32},{96,64},{1,97},{33,1},{65,33},{97,65},{2,98}... | collective-permute-start | bytes 2211848 | tf_op jit(solution)/shard_map/ppermute | solution.py:19
  47.8 35.5 %collective-permute-start.2 = (f32[20,72,128]{2,1,0:T(8,128)}, f32[20,72,128]{2,1,0:T(8,128)}, u32[]{:S(2)}, u32[]{:S(2)}) collective-permute-start(f32[20,72,128]{2,1,0:T(8,128)} %get-tuple-element.73), channel_id=1, source_target_pairs={{0,32},{32,64},{64,96},{96,0},{1,33},{33,65},{65,97},{97,1},{2,34}... | collective-permute-start | bytes 2211848 | tf_op jit(solution)/shard_map/ppermute | solution.py:19
  67.4 36.9 %all-to-all-start = ((f32[128,1,1152]{2,1,0:T(1,128)}), f32[128,1,1152]{2,1,0:T(1,128)}, u32[]{:S(2)}, u32[]{:S(2)}) async-start(f32[128,1,1152]{2,1,0:T(1,128)} %copy.109), calls=%async_computation | async-start | bytes 1179648 | tf_op jit(solution)/shard_map/all_to_all | solution.py:178
  84.7 2.2 %copy-start.3 = (f32[20,4,256]{2,1,0:T(4,128)S(1)}, f32[20,4,256]{2,1,0:T(4,128)}, u32[]{:S(2)}) copy-start(f32[20,4,256]{2,1,0:T(4,128)} %copy-done.2) | copy-start | bytes 245764
  101.5 7.2 %copy-start.4 = (f32[2,4,64,256]{3,2,1,0:T(8,128)}, f32[2,4,64,256]{3,2,1,0:T(8,128)S(1)}, u32[]{:S(2)}) copy-start(f32[2,4,64,256]{3,2,1,0:T(8,128)S(1)} %pad_subtract_fusion.3) | copy-start | bytes 1572868
  101.5 7.7 %copy-start.25 = (s32[1024]{0:T(1024)S(1)}, s32[1024]{0:T(1024)}, u32[]{:S(2)}) copy-start(s32[1024]{0:T(1024)} %get-tuple-element.114) | copy-start | bytes 12292
  101.5 7.7 %copy-start.26 = (s32[1024]{0:T(1024)S(1)}, s32[1024]{0:T(1024)}, u32[]{:S(2)}) copy-start(s32[1024]{0:T(1024)} %get-tuple-element.115) | copy-start | bytes 12292
  101.5 7.7 %copy-start.27 = (s32[64,2,2]{0,2,1:T(2,128)S(1)}, s32[64,2,2]{0,2,1:T(2,128)}, u32[]{:S(2)}) copy-start(s32[64,2,2]{0,2,1:T(2,128)} %get-tuple-element.120) | copy-start | bytes 3076
  101.6 7.7 %copy-start.28 = (s32[64,2,2]{0,2,1:T(2,128)S(1)}, s32[64,2,2]{0,2,1:T(2,128)}, u32[]{:S(2)}) copy-start(s32[64,2,2]{0,2,1:T(2,128)} %get-tuple-element.121) | copy-start | bytes 3076
  101.6 7.7 %copy-start.29 = (s32[64,2,2]{0,2,1:T(2,128)S(1)}, s32[64,2,2]{0,2,1:T(2,128)}, u32[]{:S(2)}) copy-start(s32[64,2,2]{0,2,1:T(2,128)} %get-tuple-element.118) | copy-start | bytes 3076
  101.6 7.7 %copy-start.30 = (s32[64,2,2]{0,2,1:T(2,128)S(1)}, s32[64,2,2]{0,2,1:T(2,128)}, u32[]{:S(2)}) copy-start(s32[64,2,2]{0,2,1:T(2,128)} %get-tuple-element.119) | copy-start | bytes 3076
  101.6 7.7 %copy-start.33 = (pred[64,2,2]{0,2,1:T(4,128)(4,1)S(1)}, pred[64,2,2]{0,2,1:T(4,128)(4,1)}, u32[]{:S(2)}) copy-start(pred[64,2,2]{0,2,1:T(4,128)(4,1)} %get-tuple-element.116) | copy-start | bytes 772
  101.6 7.7 %copy-start.34 = (pred[64,2,2]{0,2,1:T(4,128)(4,1)S(1)}, pred[64,2,2]{0,2,1:T(4,128)(4,1)}, u32[]{:S(2)}) copy-start(pred[64,2,2]{0,2,1:T(4,128)(4,1)} %get-tuple-element.117) | copy-start | bytes 772
  101.6 7.7 %copy-start.38 = (pred[1024]{0:T(1024)(128)(4,1)S(1)}, pred[1024]{0:T(1024)(128)(4,1)}, u32[]{:S(2)}) copy-start(pred[1024]{0:T(1024)(128)(4,1)} %fusion.103) | copy-start | bytes 3076
  108.7 2.6 %copy-start.9 = (s32[1,64,256]{2,1,0:T(8,128)S(1)}, s32[1,64,256]{2,1,0:T(8,128)}, u32[]{:S(2)}) copy-start(s32[1,64,256]{2,1,0:T(8,128)} %param.20) | copy-start | bytes 196612
  108.7 2.6 %copy-start.6 = (f32[2,4,64,256]{3,2,1,0:T(8,128)S(1)}, f32[2,4,64,256]{3,2,1,0:T(8,128)}, u32[]{:S(2)}) copy-start(f32[2,4,64,256]{3,2,1,0:T(8,128)} %copy-done.4) | copy-start | bytes 1572868
  108.9 2.4 %copy-start.5 = (f32[2,4,64,256]{3,2,1,0:T(8,128)S(1)}, f32[2,4,64,256]{3,2,1,0:T(8,128)}, u32[]{:S(2)}) copy-start(f32[2,4,64,256]{3,2,1,0:T(8,128)} %copy-done.4) | copy-start | bytes 1572868
  109.3 2.9 %copy-start.14 = (s32[64,256]{1,0:T(8,128)S(1)}, s32[64,256]{1,0:T(8,128)}, u32[]{:S(2)}) copy-start(s32[64,256]{1,0:T(8,128)} %param.21) | copy-start | bytes 196612
  111.0 1.5 copy-start.15
  111.3 14.5 %copy-start.20 = (s32[128,2]{0,1:T(2,128)S(1)}, s32[128,2]{0,1:T(2,128)}, u32[]{:S(2)}) copy-start(s32[128,2]{0,1:T(2,128)} %param.26) | copy-start | bytes 3076
  111.4 14.6 %copy-start.18 = (s32[256]{0:T(256)S(1)}, s32[256]{0:T(256)}, u32[]{:S(2)}) copy-start(s32[256]{0:T(256)} %copy-done.17) | copy-start | bytes 3076
  111.5 14.7 %copy-start.12 = (s32[128,2,2]{2,1,0:T(2,128)S(1)}, s32[128,2,2]{2,1,0:T(2,128)}, u32[]{:S(2)}) copy-start(s32[128,2,2]{2,1,0:T(2,128)} %iota_add_fusion.1) | copy-start | bytes 6148
  114.6 31.4 %all-to-all-start.1 = ((f32[128,8,128]{2,1,0:T(8,128)}), f32[128,8,128]{2,1,0:T(8,128)S(1)}, u32[]{:S(2)}, u32[]{:S(2)}) async-start(f32[128,8,128]{2,1,0:T(8,128)} %fusion.17), calls=%async_computation.1 | async-start | bytes 1048576 | tf_op jit(solution)/shard_map/all_to_all | solution.py:208
  157.4 6.3 %collective-permute-start.5 = (f32[2,64,256]{2,1,0:T(8,128)S(1)}, f32[2,64,256]{2,1,0:T(8,128)S(1)}, u32[]{:S(2)}, u32[]{:S(2)}) collective-permute-start(f32[2,64,256]{2,1,0:T(8,128)S(1)} %reshape.651), channel_id=1, source_target_pairs={{128,0},{129,1},{130,2},{131,3},{132,4},{133,5},{134,6},{135,7},{1... | collective-permute-start | bytes 393224 | tf_op jit(solution)/shard_map/ppermute | solution.py:14
  (15 other events, 18.9 us)

commit v11 on v10

--- a/solution.py
+++ b/solution.py
@@ -206,7 +206,8 @@
     ocean_tiles = to_tiles(ocean_surface).reshape(pairs, TILE)
     reply = jnp.dot(slot_hit2.T, ocean_tiles, precision=lax.Precision.HIGH).reshape(owners, capacity * 2, TILE)
     returned = lax.all_to_all(reply, ("panel", "col"), 0, 0, tiled=True).reshape(slots * 2, TILE)
-    place_rep = jnp.broadcast_to(bucket_place[:, None], (pairs, 2)).reshape(-1)
+    reply, late_place = lax.optimization_barrier((reply, bucket_place))
+    place_rep = jnp.broadcast_to(late_place[:, None], (pairs, 2)).reshape(-1)
     p_rows = lax.broadcasted_iota(jnp.int32, (pairs * 2, slots * 2), 0)
     p_cols = lax.broadcasted_iota(jnp.int32, (pairs * 2, slots * 2), 1)
     place_hit2 = ((place_rep[:, None] == p_cols // 2) & (p_cols % 2 == p_rows % 2)).astype(

time: 166 us -> 166 us (level)
  no operation moved by 1% of the time
where the time goes in v11:
time: 166 us; the launch traced here: 164 us
  starting transfers between devices  42.9 us (26%)
  local copies, waits for them, and re-layouts  40.7 us (25%)
  other arithmetic  38.8 us (23%)
  waiting for transfers between devices  26.4 us (16%)
  matrix products  13.9 us (8%)
  between operations  1.74 us (1%)
    all_to_all x1, waiting for transfers between devices, on_device(): lax.all_to_all(reply, ('panel', 'col'), 0, 0, tiled=True)  18.6 us
    all_to_all x1, starting transfers between devices, on_device(): lax.all_to_all(bucket.reshape(owners, rows_out * TILE), ('panel', 'col'),...  15.9 us
    ppermute x4, starting transfers between devices, passed_along(): lax.ppermute(value, axis, [(source, source + steps) for source in range(i...  11.7 us
    all_to_all x1, starting transfers between devices, on_device(): lax.all_to_all(reply, ('panel', 'col'), 0, 0, tiled=True)  11.4 us
    gather x1, local copies, waits for them, and re-layouts, on_device(): picked = by_bank[slot_rows.reshape(-1)].reshape(slots, 2, TILE)  6.54 us
    dot_general x1, matrix products, on_device(): jnp.einsum('rj,bji->bri', values, conservative_overlay_factors, precision...  5.67 us
    unnamed x83, local copies, waits for them, and re-layouts  5.04 us
    ppermute x4, waiting for transfers between devices, passed_along(): lax.ppermute(value, axis, [(source, source + steps) for source in range(i...  5.02 us
  transfers between devices with their start and end apart: 8, of which 3 were waited for; matrix products, arithmetic and copies ran while one was open for 38% of the time, Pallas kernels for 0%

profile of v11, /device:TPU:1, one launch (start us, length us, event | category | flops | bytes accessed | tf_op | source)
XLA Modules:
  0.0 164.3 jit_solution(3943650697753587033)
XLA Ops:
  0.7 2.0 %copy.128 = f32[2,4,64,256]{3,2,1,0:T(8,128)} copy(f32[2,4,64,256]{3,2,1,0:T(8,128)} %bitcast.178) | data formatting | bytes 1048576
  2.7 1.0 fusion.93
  3.7 1.5 bitcast_dynamic-update-slice_fusion
  5.2 1.7 %fusion.90 = (f32[2,4,64,256]{3,2,1,0:T(8,128)}, f32[64,256]{1,0:T(8,128)S(1)}) fusion(f32[2,4,64,256]{3,2,1,0:T(8,128)} %bitcast_dynamic-update-slice_fusion, f32[64,256]{1,0:T(8,128)} %param.23, s32[1,64,256]{2,1,0:T(8,128)} %param.20, f32[2,4,64,256]{3,2,1,0:T(8,128)} %bitcast.180, f32[64,256]{1,0:T(8,128)} %param.22, f32[3,4,64,256]{3,2,1,0:T(8,128)} %bitcast.157), kind=kLoop, calls=%fused_computation.189 | loop fusion | flops 212992 | bytes 589824 | tf_op jit(solution)/shard_map/scatter-add | solution.py:152
  6.9 1.3 broadcast_select_fusion.2
  9.0 1.3 collective-permute-start.1
  10.3 5.3 %collective-permute-start = (f32[20,8,256]{2,1,0:T(8,128)}, f32[20,8,256]{2,1,0:T(8,128)}, u32[]{:S(2)}, u32[]{:S(2)}) collective-permute-start(f32[20,8,256]{2,1,0:T(8,128)} %get-tuple-element.77), channel_id=1, source_target_pairs={{0,1},{1,2},{2,3},{3,4},{4,5},{5,6},{6,7},{7,8},{8,9},{9,10},{10,1... | collective-permute-start | bytes 491528 | tf_op jit(solution)/shard_map/ppermute | solution.py:14
  18.0 3.8 %collective-permute-start.4 = (f32[128,2,128]{2,1,0:T(2,128)}, f32[128,2,128]{2,1,0:T(2,128)}, u32[]{:S(2)}, u32[]{:S(2)}) collective-permute-start(f32[128,2,128]{2,1,0:T(2,128)} %bitcast.23), channel_id=1, source_target_pairs={{0,128},{1,129},{2,130},{3,131},{4,132},{5,133},{6,134},{7,135},{8... | collective-permute-start | bytes 393224 | tf_op jit(solution)/shard_map/ppermute | solution.py:14
  30.1 1.0 fusion.80
  35.3 1.1 add.343
  45.1 1.2 fusion.127
  46.3 1.5 collective-permute-start.3
  47.8 2.3 %collective-permute-start.2 = (f32[20,72,128]{2,1,0:T(8,128)}, f32[20,72,128]{2,1,0:T(8,128)}, u32[]{:S(2)}, u32[]{:S(2)}) collective-permute-start(f32[20,72,128]{2,1,0:T(8,128)} %get-tuple-element.75), channel_id=1, source_target_pairs={{0,32},{32,64},{64,96},{96,0},{1,33},{33,65},{65,97},{97,1},{2,34}... | collective-permute-start | bytes 2211848 | tf_op jit(solution)/shard_map/ppermute | solution.py:19
  50.2 4.7 %fusion.129 = f32[256,32,128]{2,0,1:T(8,128)} fusion(f32[256,128,1]{1,0,2:T(8,128)} %bitcast.25, f32[32,128,128]{2,1,0:T(8,128)S(1)} %copy-done), kind=kOutput, calls=%fused_computation.281 | convolution fusion | flops 805306368 | bytes 6422528 | tf_op jit(solution)/shard_map/bji,ri->brj/dot_general | solution.py:165
  54.9 6.5 %gather_fusion = f32[1024,128]{1,0:T(8,128)} fusion(f32[8192,128]{1,0:T(8,128)} %bitcast.176, s32[1024]{0:T(1024)} %broadcast_clamp_fusion), kind=kCustom, calls=%fused_computation | custom fusion | bytes 1052672 | tf_op jit(solution)/shard_map/gather | solution.py:170
  61.4 2.0 %copy.106 = f32[128,8,128]{0,2,1:T(8,128)} copy(f32[128,8,128]{2,1,0:T(8,128)} %bitcast.184) | data formatting | bytes 1048576 | tf_op jit(solution)/shard_map/reshape | solution.py:170
  63.4 1.1 broadcast_select_fusion
  65.4 2.0 %copy.109 = f32[128,1,1152]{2,1,0:T(1,128)} copy(f32[128,1,1152]{0,2,1:T(8,128)} %bitcast.181) | data formatting | bytes 1179648 | tf_op jit(solution)/shard_map/all_to_all | solution.py:178
  67.4 15.9 %all-to-all-start = ((f32[128,1,1152]{2,1,0:T(1,128)}), f32[128,1,1152]{2,1,0:T(1,128)}, u32[]{:S(2)}, u32[]{:S(2)}) async-start(f32[128,1,1152]{2,1,0:T(1,128)} %copy.109), calls=%async_computation | async-start | bytes 1179648 | tf_op jit(solution)/shard_map/all_to_all | solution.py:178
  83.3 1.4 slice.521
  84.7 2.2 %pad_maximum_fusion = f32[20,72,264]{2,1,0:T(8,128)S(1)} fusion(f32[20,72,4]{2,1,0:T(8,128)} %bitcast.153, f32[20,4,256]{2,1,0:T(4,128)S(1)} %slice.519, f32[12,64,256]{2,1,0:T(8,128)S(1)} %bitcast.162, f32[8,64,256]{2,1,0:T(8,128)S(1)} %bitcast.170, f32[20,4,256]{2,1,0:T(4,128)} %copy-done.2, f32[20,72,4]{2,1,0:T(8,128)S(1)} %slice.521), kind=kLoop, calls=%fused_computation.2 | loop fusion | flops 1900800 | bytes 3041280 | tf_op jit(solution)/shard_map/concatenate | solution.py:28
  101.6 2.7 %all-to-all-done = f32[128,1,1152]{2,1,0:T(1,128)} async-done(((f32[128,1,1152]{2,1,0:T(1,128)}), f32[128,1,1152]{2,1,0:T(1,128)}, u32[]{:S(2)}, u32[]{:S(2)}) %all-to-all-start) | async-done | bytes 589856 | tf_op jit(solution)/shard_map/all_to_all | solution.py:178
  104.3 1.5 copy.110
  106.7 2.0 %copy.112 = f32[128,8,128]{2,1,0:T(8,128)} copy(f32[128,8,128]{0,2,1:T(8,128)} %slice.579) | data formatting | bytes 1048576 | tf_op jit(solution)/shard_map/slice | solution.py:181
  109.3 1.7 %convolution_bitcast_fusion = f32[2,64,2,128]{3,1,0,2:T(8,128)S(1)} fusion(f32[128,8,128]{2,1,0:T(8,128)} %copy.112, s32[64,2,2]{0,2,1:T(2,128)S(1)} %copy-done.23, s32[64,2,2]{0,2,1:T(2,128)S(1)} %copy-done.24, s32[1024]{0:T(1024)S(1)} %copy-done.19, s32[1024]{0:T(1024)S(1)} %copy-done.20, s32[64,2,2]{0,2,1:T(2,128)S(1)} %copy-done.26, ...), kind=kOutput, calls=%fused_computation.9 | convolution fusion | flops 202899456 | bytes 673280 | tf_op jit(solution)/shard_map/dot_general | solution.py:190
  113.3 1.1 copy.119
  114.4 11.4 %all-to-all-start.1 = ((f32[128,8,128]{2,1,0:T(8,128)}), f32[128,8,128]{2,1,0:T(8,128)S(1)}, u32[]{:S(2)}, u32[]{:S(2)}) async-start(f32[128,8,128]{2,1,0:T(8,128)} %copy.119), calls=%async_computation.1 | async-start | bytes 1048576 | tf_op jit(solution)/shard_map/all_to_all | solution.py:208
  127.3 18.6 %all-to-all-done.1 = f32[128,8,128]{2,1,0:T(8,128)S(1)} async-done(((f32[128,8,128]{2,1,0:T(8,128)}), f32[128,8,128]{2,1,0:T(8,128)S(1)}, u32[]{:S(2)}, u32[]{:S(2)}) %all-to-all-start.1) | async-done | bytes 524320 | tf_op jit(solution)/shard_map/all_to_all | solution.py:208
  146.8 5.7 %fusion.130 = f32[512,32,128]{2,0,1:T(8,128)} fusion(f32[512,128,1]{1,0,2:T(8,128)S(1)} %fusion.3, f32[32,128,128]{2,1,0:T(8,128)S(1)} %copy-done), kind=kOutput, calls=%fused_computation.282 | convolution fusion | flops 1610612736 | bytes 10747904 | tf_op jit(solution)/shard_map/rj,bji->bri/dot_general | solution.py:218
  152.5 4.4 %gather_fusion.1 = f32[512,128]{1,0:T(8,128)S(1)} fusion(f32[16384,128]{1,0:T(8,128)} %bitcast.177, s32[1024]{0:T(1024)S(1)} %pad_clamp_fusion), kind=kCustom, calls=%fused_computation.1 | custom fusion | bytes 526336 | tf_op jit(solution)/shard_map/gather | solution.py:224
  157.3 1.3 collective-permute-start.5
  158.6 5.0 %collective-permute-done.5 = f32[2,64,256]{2,1,0:T(8,128)S(1)} collective-permute-done((f32[2,64,256]{2,1,0:T(8,128)S(1)}, f32[2,64,256]{2,1,0:T(8,128)S(1)}, u32[]{:S(2)}, u32[]{:S(2)}) %collective-permute-start.5) | collective-permute-done | bytes 131104 | tf_op jit(solution)/shard_map/ppermute | solution.py:14
  (213 shorter events, 46.2 us)
Async XLA Ops:
  0.6 49.5 %copy-start = (f32[32,128,128]{2,1,0:T(8,128)S(1)}, f32[32,128,128]{2,1,0:T(8,128)}, u32[]{:S(2)}) copy-start(f32[32,128,128]{2,1,0:T(8,128)} %param.27) | copy-start | bytes 6291460
  0.6 7.6 %copy-start.1 = (f32[1,3,4,64,256]{4,3,2,1,0:T(8,128)S(1)}, f32[1,3,4,64,256]{4,3,2,1,0:T(8,128)}, u32[]{:S(2)}) copy-start(f32[1,3,4,64,256]{4,3,2,1,0:T(8,128)} %param.19) | copy-start | bytes 2359300
  6.9 16.3 %copy-start.27 = (s32[128,2]{0,1:T(2,128)S(1)}, s32[128,2]{0,1:T(2,128)}, u32[]{:S(2)}) copy-start(s32[128,2]{0,1:T(2,128)} %param.24) | copy-start | bytes 3076
  8.2 24.1 %copy-start.17 = (s32[128,2]{0,1:T(2,128)S(1)}, s32[128,2]{0,1:T(2,128)}, u32[]{:S(2)}) copy-start(s32[128,2]{0,1:T(2,128)} %param.26) | copy-start | bytes 3076
  9.0 34.0 %collective-permute-start.1 = (f32[20,8,256]{2,1,0:T(8,128)}, f32[20,8,256]{2,1,0:T(8,128)}, u32[]{:S(2)}, u32[]{:S(2)}) collective-permute-start(f32[20,8,256]{2,1,0:T(8,128)} %get-tuple-element.78), channel_id=1, source_target_pairs={{1,0},{2,1},{3,2},{4,3},{5,4},{6,5},{7,6},{8,7},{9,8},{10,9},{11,1... | collective-permute-start | bytes 491528 | tf_op jit(solution)/shard_map/ppermute | solution.py:14
  10.3 33.7 %collective-permute-start = (f32[20,8,256]{2,1,0:T(8,128)}, f32[20,8,256]{2,1,0:T(8,128)}, u32[]{:S(2)}, u32[]{:S(2)}) collective-permute-start(f32[20,8,256]{2,1,0:T(8,128)} %get-tuple-element.77), channel_id=1, source_target_pairs={{0,1},{1,2},{2,3},{3,4},{4,5},{5,6},{6,7},{7,8},{8,9},{9,10},{10,1... | collective-permute-start | bytes 491528 | tf_op jit(solution)/shard_map/ppermute | solution.py:14
  18.0 32.2 %collective-permute-start.4 = (f32[128,2,128]{2,1,0:T(2,128)}, f32[128,2,128]{2,1,0:T(2,128)}, u32[]{:S(2)}, u32[]{:S(2)}) collective-permute-start(f32[128,2,128]{2,1,0:T(2,128)} %bitcast.23), channel_id=1, source_target_pairs={{0,128},{1,129},{2,130},{3,131},{4,132},{5,133},{6,134},{7,135},{8... | collective-permute-start | bytes 393224 | tf_op jit(solution)/shard_map/ppermute | solution.py:14
  31.4 11.6 %copy-start.15 = (s32[256]{0:T(256)}, s32[256]{0:T(256)S(1)}, u32[]{:S(2)}) copy-start(s32[256]{0:T(256)S(1)} %multiply_add_fusion.2) | copy-start | bytes 3076
  46.3 38.4 %collective-permute-start.3 = (f32[20,72,128]{2,1,0:T(8,128)}, f32[20,72,128]{2,1,0:T(8,128)}, u32[]{:S(2)}, u32[]{:S(2)}) collective-permute-start(f32[20,72,128]{2,1,0:T(8,128)} %get-tuple-element.76), channel_id=1, source_target_pairs={{0,96},{32,0},{64,32},{96,64},{1,97},{33,1},{65,33},{97,65},{2,98}... | collective-permute-start | bytes 2211848 | tf_op jit(solution)/shard_map/ppermute | solution.py:19
  47.8 35.5 %collective-permute-start.2 = (f32[20,72,128]{2,1,0:T(8,128)}, f32[20,72,128]{2,1,0:T(8,128)}, u32[]{:S(2)}, u32[]{:S(2)}) collective-permute-start(f32[20,72,128]{2,1,0:T(8,128)} %get-tuple-element.75), channel_id=1, source_target_pairs={{0,32},{32,64},{64,96},{96,0},{1,33},{33,65},{65,97},{97,1},{2,34}... | collective-permute-start | bytes 2211848 | tf_op jit(solution)/shard_map/ppermute | solution.py:19
  67.4 36.9 %all-to-all-start = ((f32[128,1,1152]{2,1,0:T(1,128)}), f32[128,1,1152]{2,1,0:T(1,128)}, u32[]{:S(2)}, u32[]{:S(2)}) async-start(f32[128,1,1152]{2,1,0:T(1,128)} %copy.109), calls=%async_computation | async-start | bytes 1179648 | tf_op jit(solution)/shard_map/all_to_all | solution.py:178
  84.7 2.2 %copy-start.3 = (f32[20,4,256]{2,1,0:T(4,128)S(1)}, f32[20,4,256]{2,1,0:T(4,128)}, u32[]{:S(2)}) copy-start(f32[20,4,256]{2,1,0:T(4,128)} %copy-done.2) | copy-start | bytes 245764
  101.5 7.2 %copy-start.4 = (f32[2,4,64,256]{3,2,1,0:T(8,128)}, f32[2,4,64,256]{3,2,1,0:T(8,128)S(1)}, u32[]{:S(2)}) copy-start(f32[2,4,64,256]{3,2,1,0:T(8,128)S(1)} %pad_subtract_fusion.3) | copy-start | bytes 1572868
  101.5 7.7 %copy-start.19 = (s32[1024]{0:T(1024)S(1)}, s32[1024]{0:T(1024)}, u32[]{:S(2)}) copy-start(s32[1024]{0:T(1024)} %get-tuple-element.116) | copy-start | bytes 12292
  101.5 7.7 %copy-start.20 = (s32[1024]{0:T(1024)S(1)}, s32[1024]{0:T(1024)}, u32[]{:S(2)}) copy-start(s32[1024]{0:T(1024)} %get-tuple-element.117) | copy-start | bytes 12292
  101.5 7.7 %copy-start.23 = (s32[64,2,2]{0,2,1:T(2,128)S(1)}, s32[64,2,2]{0,2,1:T(2,128)}, u32[]{:S(2)}) copy-start(s32[64,2,2]{0,2,1:T(2,128)} %get-tuple-element.122) | copy-start | bytes 3076
  101.6 7.7 %copy-start.24 = (s32[64,2,2]{0,2,1:T(2,128)S(1)}, s32[64,2,2]{0,2,1:T(2,128)}, u32[]{:S(2)}) copy-start(s32[64,2,2]{0,2,1:T(2,128)} %get-tuple-element.123) | copy-start | bytes 3076
  101.6 7.7 %copy-start.25 = (s32[64,2,2]{0,2,1:T(2,128)S(1)}, s32[64,2,2]{0,2,1:T(2,128)}, u32[]{:S(2)}) copy-start(s32[64,2,2]{0,2,1:T(2,128)} %get-tuple-element.120) | copy-start | bytes 3076
  101.6 7.7 %copy-start.26 = (s32[64,2,2]{0,2,1:T(2,128)S(1)}, s32[64,2,2]{0,2,1:T(2,128)}, u32[]{:S(2)}) copy-start(s32[64,2,2]{0,2,1:T(2,128)} %get-tuple-element.121) | copy-start | bytes 3076
  101.6 7.7 %copy-start.32 = (pred[64,2,2]{0,2,1:T(4,128)(4,1)S(1)}, pred[64,2,2]{0,2,1:T(4,128)(4,1)}, u32[]{:S(2)}) copy-start(pred[64,2,2]{0,2,1:T(4,128)(4,1)} %get-tuple-element.118) | copy-start | bytes 772
  101.6 7.7 %copy-start.33 = (pred[64,2,2]{0,2,1:T(4,128)(4,1)S(1)}, pred[64,2,2]{0,2,1:T(4,128)(4,1)}, u32[]{:S(2)}) copy-start(pred[64,2,2]{0,2,1:T(4,128)(4,1)} %get-tuple-element.119) | copy-start | bytes 772
  101.6 7.7 %copy-start.35 = (pred[1024]{0:T(1024)(128)(4,1)S(1)}, pred[1024]{0:T(1024)(128)(4,1)}, u32[]{:S(2)}) copy-start(pred[1024]{0:T(1024)(128)(4,1)} %fusion.113) | copy-start | bytes 3076
  108.7 2.6 %copy-start.9 = (s32[1,64,256]{2,1,0:T(8,128)S(1)}, s32[1,64,256]{2,1,0:T(8,128)}, u32[]{:S(2)}) copy-start(s32[1,64,256]{2,1,0:T(8,128)} %param.20) | copy-start | bytes 196612
  108.7 2.6 %copy-start.6 = (f32[2,4,64,256]{3,2,1,0:T(8,128)S(1)}, f32[2,4,64,256]{3,2,1,0:T(8,128)}, u32[]{:S(2)}) copy-start(f32[2,4,64,256]{3,2,1,0:T(8,128)} %copy-done.4) | copy-start | bytes 1572868
  108.9 2.4 %copy-start.5 = (f32[2,4,64,256]{3,2,1,0:T(8,128)S(1)}, f32[2,4,64,256]{3,2,1,0:T(8,128)}, u32[]{:S(2)}) copy-start(f32[2,4,64,256]{3,2,1,0:T(8,128)} %copy-done.4) | copy-start | bytes 1572868
  109.3 2.9 %copy-start.14 = (s32[64,256]{1,0:T(8,128)S(1)}, s32[64,256]{1,0:T(8,128)}, u32[]{:S(2)}) copy-start(s32[64,256]{1,0:T(8,128)} %param.21) | copy-start | bytes 196612
  111.0 1.5 copy-start.21
  112.6 13.3 %copy-start.18 = (s32[128,2]{0,1:T(2,128)S(1)}, s32[128,2]{0,1:T(2,128)}, u32[]{:S(2)}) copy-start(s32[128,2]{0,1:T(2,128)} %param.26) | copy-start | bytes 3076
  112.6 13.3 %copy-start.12 = (s32[128,2,2]{2,1,0:T(2,128)S(1)}, s32[128,2,2]{2,1,0:T(2,128)}, u32[]{:S(2)}) copy-start(s32[128,2,2]{2,1,0:T(2,128)} %iota_add_fusion.1) | copy-start | bytes 6148
  114.4 12.7 %copy-start.16 = (s32[256]{0:T(256)S(1)}, s32[256]{0:T(256)}, u32[]{:S(2)}) copy-start(s32[256]{0:T(256)} %copy-done.15) | copy-start | bytes 3076
  114.4 31.5 %all-to-all-start.1 = ((f32[128,8,128]{2,1,0:T(8,128)}), f32[128,8,128]{2,1,0:T(8,128)S(1)}, u32[]{:S(2)}, u32[]{:S(2)}) async-start(f32[128,8,128]{2,1,0:T(8,128)} %copy.119), calls=%async_computation.1 | async-start | bytes 1048576 | tf_op jit(solution)/shard_map/all_to_all | solution.py:208
  157.3 6.3 %collective-permute-start.5 = (f32[2,64,256]{2,1,0:T(8,128)S(1)}, f32[2,64,256]{2,1,0:T(8,128)S(1)}, u32[]{:S(2)}, u32[]{:S(2)}) collective-permute-start(f32[2,64,256]{2,1,0:T(8,128)S(1)} %reshape.644), channel_id=1, source_target_pairs={{128,0},{129,1},{130,2},{131,3},{132,4},{133,5},{134,6},{135,7},{1... | collective-permute-start | bytes 393224 | tf_op jit(solution)/shard_map/ppermute | solution.py:14
  (15 other events, 18.7 us)
